TPU v7x, 768 devices: a whole 4x8x12 slice. The times are simulated.
768 devices in a mesh: gx: 48 (over y_lo, z, core), gy: 16 (over x, y_hi).
Axes of the slice: x: 4, y: 8 (y_hi: 4, y_lo: 2; y = y_hi * 2 + y_lo), z: 12, core: 2. Of those that a mesh axis runs over, the one named last changes fastest.
Arguments:
- pressure: float32 [192, 512, 384], P('gx', 'gy'), may hold values from -6 to 6
- previous: float32 [192, 512, 384], P('gx', 'gy'), may hold values from -6 to 6
- material: int32 [192, 512, 384], P('gx', 'gy'), may hold values from 0 to 2
- slot_cell: int32 [49152], P(('gx', 'gy')), may hold values from -1 to 49150, as said below
- angles: float32 [2, 4096], replicated, may hold values from -3.140625 to 3.140625
- spectra_in: float32 [2, 384, 4096], P(None, 'gx', 'gy'), may hold values from -6 to 6
Outputs:
- pressure_out: float32 [192, 512, 384], P('gx', 'gy')
- previous_out: float32 [192, 512, 384], P('gx', 'gy')
- spectra: float32 [2, 384, 4096], P(None, 'gx', 'gy')
Inputs may be any that keep to these rules, and one draw needn't show every extreme that they name: `slot_cell`: slots j of block i = j // 64 belong to device i in the order of gx+gy. A live entry is the index (x * 32 + y) * 384 + z of a cell of that device's tile with z < 383; -1 marks an empty slot. A device's live slots come first; the number of live slots differs from device to device.
All inputs are finite; a program needn't handle non-finite values.
Results may differ from a plain program's by a relative error of at most 0.0003.
Values sent between devices are 32-bit elements; how exact they have to be, the bound alone decides.
No kernel may reach another device: no remote copies, remote signals or barrier semaphores. Data moves between devices by JAX's collectives and lax.ppermute only.
A program may use at most 32 MiB of HBM per device.

v0:
```python
import jax
import jax.numpy as jnp
from jax import lax
from jax.sharding import PartitionSpec as P

STEPS = 16
START = 3000


SIGMA_ABS = 0.5
LAMBDA_SQ = 0.25
KAPPA = 0.37


def with_halo(shard, sides, width):
    for axis, dim in sides:
        count, length = (lax.axis_size(axis), shard.shape[dim])
        up = [(i, (i + 1) % count) for i in range(count - 1)]
        down = [(j, i) for i, j in up]
        last = lax.slice_in_dim(shard, length - width, length, axis=dim)
        initial = lax.slice_in_dim(shard, 0, width, axis=dim)
        before = lax.ppermute(last, axis, up)
        after = lax.ppermute(initial, axis, down)
        shard = jnp.concatenate([before, shard, after], axis=dim)
    return shard


def advance(padded, open_big, before, loss):
    center = padded[1:-1, 1:-1]
    open_center = open_big[1:-1, 1:-1]
    summed = open_big[:-2, 1:-1] * (padded[:-2, 1:-1] - center)
    summed = summed + open_big[2:, 1:-1] * (padded[2:, 1:-1] - center)
    summed = summed + open_big[1:-1, :-2] * (padded[1:-1, :-2] - center)
    summed = summed + open_big[1:-1, 2:] * (padded[1:-1, 2:] - center)
    z_pad = ((0, 0), (0, 0), (1, 1))
    center_z = jnp.pad(center, z_pad)
    open_z = jnp.pad(open_center, z_pad)
    summed = summed + open_z[:, :, 2:] * (center_z[:, :, 2:] - center)
    summed = summed + open_z[:, :, :-2] * (center_z[:, :, :-2] - center)
    update = 2.0 * center - (1.0 - loss) * before + LAMBDA_SQ * (open_center * summed)
    return open_center * update / (1.0 + loss)


def project(angle_rows, coords, series_g, series_p):
    elevation = angle_rows[0]
    azimuth = angle_rows[1]
    unit_x = jnp.cos(elevation) * jnp.cos(azimuth)
    unit_y = jnp.cos(elevation) * jnp.sin(azimuth)
    unit_z = jnp.sin(elevation)
    phases = KAPPA * (
        unit_x[:, None] * coords[0][None, :]
        + unit_y[:, None] * coords[1][None, :]
        + unit_z[:, None] * coords[2][None, :]
    )
    best_prec = lax.Precision.HIGHEST
    normal_part = jnp.einsum("os,ts->ot", jnp.cos(phases), series_g, precision=best_prec)
    pressure_part = jnp.einsum(
        "os,ts->ot", unit_z[:, None] * jnp.sin(phases), series_p, precision=best_prec
    )
    return normal_part + pressure_part


def sample_cells(field, safe_cell, live_slot):
    flat_field = field.reshape(-1)
    cell_value = flat_field[safe_cell]
    above_value = flat_field[safe_cell + 1]
    return jnp.stack([live_slot * (above_value - cell_value), live_slot * cell_value])


def body(pressure, previous, material, slot_cell, angles, spectra_in):
    tile_x, tile_y, depth_z = pressure.shape
    slot_count = slot_cell.shape[0]
    step_count = STEPS
    open_cell = (material != 1).astype(jnp.float32)
    loss = jnp.where(material == 2, jnp.float32(SIGMA_ABS), jnp.float32(0.0))
    safe_cell = jnp.maximum(slot_cell, 0)
    live_slot = (slot_cell >= 0).astype(jnp.float32)
    gx_index = lax.axis_index("gx")
    gy_index = lax.axis_index("gy")
    x_global = gx_index * tile_x + safe_cell // (tile_y * depth_z)
    y_global = gy_index * tile_y + safe_cell // depth_z % tile_y
    z_global = safe_cell % depth_z
    coords = jnp.stack([x_global, y_global, z_global]).astype(jnp.float32)
    open_big = with_halo(open_cell, (("gx", 0), ("gy", 1)), 1)

    def one_step(state_pair, unused):
        current, before = state_pair
        padded = with_halo(current, (("gx", 0), ("gy", 1)), 1)
        following = advance(padded, open_big, before, loss)
        return ((following, current), sample_cells(following, safe_cell, live_slot))

    (current, before), samples = lax.scan(one_step, (pressure, previous), None, length=step_count)
    series_g = samples[:, 0]
    series_p = samples[:, 1]
    trace_block = lax.psum_scatter(
        project(angles, coords, series_g, series_p), "gy", scatter_dimension=0, tiled=True
    )
    sample_total = slot_count * lax.axis_size("gx") * lax.axis_size("gy")
    traces = lax.psum(trace_block, "gx") / jnp.sqrt(jnp.float32(sample_total))
    bin_local = spectra_in.shape[1]
    bin_total = bin_local * lax.axis_size("gx")
    bin_ids = gx_index * bin_local + jnp.arange(bin_local, dtype=jnp.int32)
    time_ids = jnp.arange(step_count, dtype=jnp.int32)
    turn_ids = (START + time_ids)[None, :] * (bin_ids + 1)[:, None] % (2 * (bin_total + 1))
    angles_kt = jnp.pi * turn_ids.astype(jnp.float32) / (bin_total + 1)
    best_prec = lax.Precision.HIGHEST
    real_part = spectra_in[0] + jnp.dot(jnp.cos(angles_kt), traces.T, precision=best_prec)
    imag_part = spectra_in[1] - jnp.dot(jnp.sin(angles_kt), traces.T, precision=best_prec)
    return (current, before, jnp.stack([real_part, imag_part]))


def solution(mesh):
    return jax.shard_map(
        body,
        mesh=mesh,
        in_specs=(
            P("gx", "gy", None),
            P("gx", "gy", None),
            P("gx", "gy", None),
            P(("gx", "gy")),
            P(),
            P(None, "gx", "gy"),
        ),
        out_specs=(P("gx", "gy", None), P("gx", "gy", None), P(None, "gx", "gy")),
        check_vma=False,
    )
```

profile of v0, /device:TPU:1, one launch (start us, length us, event | category | flops | bytes accessed | tf_op | source)
XLA Modules:
  0.0 672.3 jit_solution(5014832247647766216)
XLA Ops:
  8.2 5.4 collective-permute-start.4
  13.6 8.3 %collective-permute-start.5 = (f32[1,32,384]{2,1,0:T(8,128)S(1)}, f32[1,32,384]{2,1,0:T(8,128)S(1)}, u32[]{:S(2)}, u32[]{:S(2)}) collective-permute-start(f32[1,32,384]{2,1,0:T(8,128)S(1)} %get-tuple-element.167), channel_id=1, source_target_pairs={{16,0},{32,16},{48,32},{64,48},{80,64},{96,80},{112,96},{128,112},... | collective-permute-start | bytes 147464 | tf_op jit(solution)/shard_map/ppermute | solution.py:23
  29.9 327.9 %while.16 = (s32[]{:T(128)}, f32[4,32,384]{2,1,0:T(8,128)S(1)}, f32[4,32,384]{2,1,0:T(8,128)S(1)}, f32[16,2,64]{2,1,0:T(2,128)S(1)}, f32[4,32,384]{2,1,0:T(8,128...) while((s32[]{:T(128)}, f32[4,32,384]{2,1,0:T(8,128)S(1)}, ...), condition=%wide.region_1.2_spmd, body=%wide.region_0.1_spmd.sunk | while | flops 1526530 | bytes 4665625 | solution.py:92
  39.7 6.4 collective-permute-start.3
  58.4 6.4 collective-permute-start.3
  78.4 6.4 collective-permute-start.3
  98.9 6.4 collective-permute-start.3
  113.1 4.9 collective-permute-done.1
  119.4 6.4 collective-permute-start.3
  139.5 6.4 collective-permute-start.3
  159.7 6.4 collective-permute-start.3
  179.8 6.7 collective-permute-start.3
  200.1 7.5 %collective-permute-start.3 = (f32[6,1,384]{2,1,0:T(1,128)S(1)}, f32[6,1,384]{2,1,0:T(1,128)S(1)}, u32[]{:S(2)}, u32[]{:S(2)}) collective-permute-start(f32[6,1,384]{2,1,0:T(1,128)S(1)} %get-tuple-element.254), channel_id=1, source_target_pairs={{0,1},{1,2},{2,3},{3,4},{4,5},{5,6},{6,7},{7,8},{8,9},{9,10},{10,1... | collective-permute-start | bytes 27656 | tf_op jit(solution)/shard_map/while/body/eval_jaxpr/ppermute | solution.py:22
  221.1 7.5 %collective-permute-start.3 = (f32[6,1,384]{2,1,0:T(1,128)S(1)}, f32[6,1,384]{2,1,0:T(1,128)S(1)}, u32[]{:S(2)}, u32[]{:S(2)}) collective-permute-start(f32[6,1,384]{2,1,0:T(1,128)S(1)} %get-tuple-element.254), channel_id=1, source_target_pairs={{0,1},{1,2},{2,3},{3,4},{4,5},{5,6},{6,7},{7,8},{8,9},{9,10},{10,1... | collective-permute-start | bytes 27656 | tf_op jit(solution)/shard_map/while/body/eval_jaxpr/ppermute | solution.py:22
  242.2 7.5 %collective-permute-start.3 = (f32[6,1,384]{2,1,0:T(1,128)S(1)}, f32[6,1,384]{2,1,0:T(1,128)S(1)}, u32[]{:S(2)}, u32[]{:S(2)}) collective-permute-start(f32[6,1,384]{2,1,0:T(1,128)S(1)} %get-tuple-element.254), channel_id=1, source_target_pairs={{0,1},{1,2},{2,3},{3,4},{4,5},{5,6},{6,7},{7,8},{8,9},{9,10},{10,1... | collective-permute-start | bytes 27656 | tf_op jit(solution)/shard_map/while/body/eval_jaxpr/ppermute | solution.py:22
  263.2 7.5 %collective-permute-start.3 = (f32[6,1,384]{2,1,0:T(1,128)S(1)}, f32[6,1,384]{2,1,0:T(1,128)S(1)}, u32[]{:S(2)}, u32[]{:S(2)}) collective-permute-start(f32[6,1,384]{2,1,0:T(1,128)S(1)} %get-tuple-element.254), channel_id=1, source_target_pairs={{0,1},{1,2},{2,3},{3,4},{4,5},{5,6},{6,7},{7,8},{8,9},{9,10},{10,1... | collective-permute-start | bytes 27656 | tf_op jit(solution)/shard_map/while/body/eval_jaxpr/ppermute | solution.py:22
  284.3 7.5 %collective-permute-start.3 = (f32[6,1,384]{2,1,0:T(1,128)S(1)}, f32[6,1,384]{2,1,0:T(1,128)S(1)}, u32[]{:S(2)}, u32[]{:S(2)}) collective-permute-start(f32[6,1,384]{2,1,0:T(1,128)S(1)} %get-tuple-element.254), channel_id=1, source_target_pairs={{0,1},{1,2},{2,3},{3,4},{4,5},{5,6},{6,7},{7,8},{8,9},{9,10},{10,1... | collective-permute-start | bytes 27656 | tf_op jit(solution)/shard_map/while/body/eval_jaxpr/ppermute | solution.py:22
  305.4 7.5 %collective-permute-start.3 = (f32[6,1,384]{2,1,0:T(1,128)S(1)}, f32[6,1,384]{2,1,0:T(1,128)S(1)}, u32[]{:S(2)}, u32[]{:S(2)}) collective-permute-start(f32[6,1,384]{2,1,0:T(1,128)S(1)} %get-tuple-element.254), channel_id=1, source_target_pairs={{0,1},{1,2},{2,3},{3,4},{4,5},{5,6},{6,7},{7,8},{8,9},{9,10},{10,1... | collective-permute-start | bytes 27656 | tf_op jit(solution)/shard_map/while/body/eval_jaxpr/ppermute | solution.py:22
  326.4 7.5 %collective-permute-start.3 = (f32[6,1,384]{2,1,0:T(1,128)S(1)}, f32[6,1,384]{2,1,0:T(1,128)S(1)}, u32[]{:S(2)}, u32[]{:S(2)}) collective-permute-start(f32[6,1,384]{2,1,0:T(1,128)S(1)} %get-tuple-element.254), channel_id=1, source_target_pairs={{0,1},{1,2},{2,3},{3,4},{4,5},{5,6},{6,7},{7,8},{8,9},{9,10},{10,1... | collective-permute-start | bytes 27656 | tf_op jit(solution)/shard_map/while/body/eval_jaxpr/ppermute | solution.py:22
  347.5 7.5 %collective-permute-start.3 = (f32[6,1,384]{2,1,0:T(1,128)S(1)}, f32[6,1,384]{2,1,0:T(1,128)S(1)}, u32[]{:S(2)}, u32[]{:S(2)}) collective-permute-start(f32[6,1,384]{2,1,0:T(1,128)S(1)} %get-tuple-element.254), channel_id=1, source_target_pairs={{0,1},{1,2},{2,3},{3,4},{4,5},{5,6},{6,7},{7,8},{8,9},{9,10},{10,1... | collective-permute-start | bytes 27656 | tf_op jit(solution)/shard_map/while/body/eval_jaxpr/ppermute | solution.py:22
  357.9 9.3 %fusion.28 = f32[4096,16]{0,1:T(8,128)S(1)} fusion(f32[16,64]{1,0:T(8,128)S(1)} %bitcast.72, f32[64]{0:T(128)S(1)} %get-tuple-element.174, f32[4096]{0:T(1024)S(1)} %bitcast.69, f32[64]{0:T(128)S(1)} %get-tuple-element.175, f32[4096]{0:T(1024)S(1)} %bitcast.67, f32[64]{0:T(128)S(1)} %get-tuple-element.173, f32[4096]{0:T(1024)S(1)} %bitcast.65), kind=kOutput, calls=%fused_computation.51 | convolution fusion | flops 51904512 | bytes 316160 | tf_op jit(solution)/shard_map/os,ts->ot/dot_general | solution.py:56
  367.2 11.9 %convolution_add_fusion = f32[4096,16]{0,1:T(8,128)} fusion(f32[4096,16]{0,1:T(8,128)S(1)} %fusion.28, f32[16,64]{1,0:T(8,128)S(1)} %bitcast.71, f32[64]{0:T(128)S(1)} %get-tuple-element.174, f32[4096]{0:T(1024)S(1)} %bitcast.70, f32[64]{0:T(128)S(1)} %get-tuple-element.175, f32[4096]{0:T(1024)S(1)} %bitcast.68, f32[64]{0:T(128)S(1)} %get-tuple-element.173, ...), kind=kOutput, calls=%fused_computation.48 | convolution fusion | flops 52232192 | bytes 578304 | tf_op jit(solution)/shard_map/os,ts->ot/dot_general | solution.py:57
  379.2 128.9 %reduce-scatter.2.cloned.1.call-done = f32[256,16]{0,1:T(8,128)} async-done(((f32[4096,16]{0,1:T(8,128)}), f32[256,16]{0,1:T(8,128)}) %reduce-scatter.2.cloned.1.call-update) | async-done | bytes 16400 | tf_op jit(solution)/shard_map/reduce_scatter | solution.py:95
  508.1 156.3 %psum.7 = f32[256,16]{0,1:T(8,128)S(1)} all-reduce(f32[256,16]{0,1:T(8,128)} %reduce-scatter.2.cloned.1.call-done), channel_id=1, replica_groups=mesh['gx'=48,'gy'=16] {'gx'}, use_global_device_ids=true, to_apply=%region_3.4 | all-reduce | flops 4096 | bytes 32768 | tf_op jit(solution)/shard_map/psum | solution.py:99
  (393 shorter events, 219.1 us)
Async XLA Ops:
  7.2 500.9 %reduce-scatter.2.cloned.1.call-start = ((), (), s32[]{:S(2)}) async-start(), calls=%async_computation.1 | async-start | bytes 278528 | tf_op jit(solution)/shard_map/reduce_scatter | solution.py:95
  8.2 14.8 %collective-permute-start.4 = (f32[1,32,384]{2,1,0:T(8,128)S(1)}, f32[1,32,384]{2,1,0:T(8,128)S(1)}, u32[]{:S(2)}, u32[]{:S(2)}) collective-permute-start(f32[1,32,384]{2,1,0:T(8,128)S(1)} %get-tuple-element.166), channel_id=1, source_target_pairs={{0,16},{16,32},{32,48},{48,64},{64,80},{80,96},{96,112},{112,128},... | collective-permute-start | bytes 147464 | tf_op jit(solution)/shard_map/ppermute | solution.py:22
  13.6 9.5 %collective-permute-start.5 = (f32[1,32,384]{2,1,0:T(8,128)S(1)}, f32[1,32,384]{2,1,0:T(8,128)S(1)}, u32[]{:S(2)}, u32[]{:S(2)}) collective-permute-start(f32[1,32,384]{2,1,0:T(8,128)S(1)} %get-tuple-element.167), channel_id=1, source_target_pairs={{16,0},{32,16},{48,32},{64,48},{80,64},{96,80},{112,96},{128,112},... | collective-permute-start | bytes 147464 | tf_op jit(solution)/shard_map/ppermute | solution.py:23
  38.4 7.7 %collective-permute-start.2 = (f32[6,1,384]{2,1,0:T(1,128)S(1)}, f32[6,1,384]{2,1,0:T(1,128)S(1)}, u32[]{:S(2)}, u32[]{:S(2)}) collective-permute-start(f32[6,1,384]{2,1,0:T(1,128)S(1)} %get-tuple-element.253), channel_id=1, source_target_pairs={{1,0},{2,1},{3,2},{4,3},{5,4},{6,5},{7,6},{8,7},{9,8},{10,9},{11,1... | collective-permute-start | bytes 27656 | tf_op jit(solution)/shard_map/while/body/eval_jaxpr/ppermute | solution.py:23
  57.1 7.7 %collective-permute-start.2 = (f32[6,1,384]{2,1,0:T(1,128)S(1)}, f32[6,1,384]{2,1,0:T(1,128)S(1)}, u32[]{:S(2)}, u32[]{:S(2)}) collective-permute-start(f32[6,1,384]{2,1,0:T(1,128)S(1)} %get-tuple-element.253), channel_id=1, source_target_pairs={{1,0},{2,1},{3,2},{4,3},{5,4},{6,5},{7,6},{8,7},{9,8},{10,9},{11,1... | collective-permute-start | bytes 27656 | tf_op jit(solution)/shard_map/while/body/eval_jaxpr/ppermute | solution.py:23
  77.1 7.7 %collective-permute-start.2 = (f32[6,1,384]{2,1,0:T(1,128)S(1)}, f32[6,1,384]{2,1,0:T(1,128)S(1)}, u32[]{:S(2)}, u32[]{:S(2)}) collective-permute-start(f32[6,1,384]{2,1,0:T(1,128)S(1)} %get-tuple-element.253), channel_id=1, source_target_pairs={{1,0},{2,1},{3,2},{4,3},{5,4},{6,5},{7,6},{8,7},{9,8},{10,9},{11,1... | collective-permute-start | bytes 27656 | tf_op jit(solution)/shard_map/while/body/eval_jaxpr/ppermute | solution.py:23
  97.6 7.7 %collective-permute-start.2 = (f32[6,1,384]{2,1,0:T(1,128)S(1)}, f32[6,1,384]{2,1,0:T(1,128)S(1)}, u32[]{:S(2)}, u32[]{:S(2)}) collective-permute-start(f32[6,1,384]{2,1,0:T(1,128)S(1)} %get-tuple-element.253), channel_id=1, source_target_pairs={{1,0},{2,1},{3,2},{4,3},{5,4},{6,5},{7,6},{8,7},{9,8},{10,9},{11,1... | collective-permute-start | bytes 27656 | tf_op jit(solution)/shard_map/while/body/eval_jaxpr/ppermute | solution.py:23
  178.5 8.0 %collective-permute-start.2 = (f32[6,1,384]{2,1,0:T(1,128)S(1)}, f32[6,1,384]{2,1,0:T(1,128)S(1)}, u32[]{:S(2)}, u32[]{:S(2)}) collective-permute-start(f32[6,1,384]{2,1,0:T(1,128)S(1)} %get-tuple-element.253), channel_id=1, source_target_pairs={{1,0},{2,1},{3,2},{4,3},{5,4},{6,5},{7,6},{8,7},{9,8},{10,9},{11,1... | collective-permute-start | bytes 27656 | tf_op jit(solution)/shard_map/while/body/eval_jaxpr/ppermute | solution.py:23
  198.8 8.9 %collective-permute-start.2 = (f32[6,1,384]{2,1,0:T(1,128)S(1)}, f32[6,1,384]{2,1,0:T(1,128)S(1)}, u32[]{:S(2)}, u32[]{:S(2)}) collective-permute-start(f32[6,1,384]{2,1,0:T(1,128)S(1)} %get-tuple-element.253), channel_id=1, source_target_pairs={{1,0},{2,1},{3,2},{4,3},{5,4},{6,5},{7,6},{8,7},{9,8},{10,9},{11,1... | collective-permute-start | bytes 27656 | tf_op jit(solution)/shard_map/while/body/eval_jaxpr/ppermute | solution.py:23
  200.1 8.3 %collective-permute-start.3 = (f32[6,1,384]{2,1,0:T(1,128)S(1)}, f32[6,1,384]{2,1,0:T(1,128)S(1)}, u32[]{:S(2)}, u32[]{:S(2)}) collective-permute-start(f32[6,1,384]{2,1,0:T(1,128)S(1)} %get-tuple-element.254), channel_id=1, source_target_pairs={{0,1},{1,2},{2,3},{3,4},{4,5},{5,6},{6,7},{7,8},{8,9},{9,10},{10,1... | collective-permute-start | bytes 27656 | tf_op jit(solution)/shard_map/while/body/eval_jaxpr/ppermute | solution.py:22
  219.8 8.9 %collective-permute-start.2 = (f32[6,1,384]{2,1,0:T(1,128)S(1)}, f32[6,1,384]{2,1,0:T(1,128)S(1)}, u32[]{:S(2)}, u32[]{:S(2)}) collective-permute-start(f32[6,1,384]{2,1,0:T(1,128)S(1)} %get-tuple-element.253), channel_id=1, source_target_pairs={{1,0},{2,1},{3,2},{4,3},{5,4},{6,5},{7,6},{8,7},{9,8},{10,9},{11,1... | collective-permute-start | bytes 27656 | tf_op jit(solution)/shard_map/while/body/eval_jaxpr/ppermute | solution.py:23
  221.1 8.3 %collective-permute-start.3 = (f32[6,1,384]{2,1,0:T(1,128)S(1)}, f32[6,1,384]{2,1,0:T(1,128)S(1)}, u32[]{:S(2)}, u32[]{:S(2)}) collective-permute-start(f32[6,1,384]{2,1,0:T(1,128)S(1)} %get-tuple-element.254), channel_id=1, source_target_pairs={{0,1},{1,2},{2,3},{3,4},{4,5},{5,6},{6,7},{7,8},{8,9},{9,10},{10,1... | collective-permute-start | bytes 27656 | tf_op jit(solution)/shard_map/while/body/eval_jaxpr/ppermute | solution.py:22
  240.9 8.9 %collective-permute-start.2 = (f32[6,1,384]{2,1,0:T(1,128)S(1)}, f32[6,1,384]{2,1,0:T(1,128)S(1)}, u32[]{:S(2)}, u32[]{:S(2)}) collective-permute-start(f32[6,1,384]{2,1,0:T(1,128)S(1)} %get-tuple-element.253), channel_id=1, source_target_pairs={{1,0},{2,1},{3,2},{4,3},{5,4},{6,5},{7,6},{8,7},{9,8},{10,9},{11,1... | collective-permute-start | bytes 27656 | tf_op jit(solution)/shard_map/while/body/eval_jaxpr/ppermute | solution.py:23
  242.2 8.3 %collective-permute-start.3 = (f32[6,1,384]{2,1,0:T(1,128)S(1)}, f32[6,1,384]{2,1,0:T(1,128)S(1)}, u32[]{:S(2)}, u32[]{:S(2)}) collective-permute-start(f32[6,1,384]{2,1,0:T(1,128)S(1)} %get-tuple-element.254), channel_id=1, source_target_pairs={{0,1},{1,2},{2,3},{3,4},{4,5},{5,6},{6,7},{7,8},{8,9},{9,10},{10,1... | collective-permute-start | bytes 27656 | tf_op jit(solution)/shard_map/while/body/eval_jaxpr/ppermute | solution.py:22
  261.9 8.9 %collective-permute-start.2 = (f32[6,1,384]{2,1,0:T(1,128)S(1)}, f32[6,1,384]{2,1,0:T(1,128)S(1)}, u32[]{:S(2)}, u32[]{:S(2)}) collective-permute-start(f32[6,1,384]{2,1,0:T(1,128)S(1)} %get-tuple-element.253), channel_id=1, source_target_pairs={{1,0},{2,1},{3,2},{4,3},{5,4},{6,5},{7,6},{8,7},{9,8},{10,9},{11,1... | collective-permute-start | bytes 27656 | tf_op jit(solution)/shard_map/while/body/eval_jaxpr/ppermute | solution.py:23
  263.2 8.3 %collective-permute-start.3 = (f32[6,1,384]{2,1,0:T(1,128)S(1)}, f32[6,1,384]{2,1,0:T(1,128)S(1)}, u32[]{:S(2)}, u32[]{:S(2)}) collective-permute-start(f32[6,1,384]{2,1,0:T(1,128)S(1)} %get-tuple-element.254), channel_id=1, source_target_pairs={{0,1},{1,2},{2,3},{3,4},{4,5},{5,6},{6,7},{7,8},{8,9},{9,10},{10,1... | collective-permute-start | bytes 27656 | tf_op jit(solution)/shard_map/while/body/eval_jaxpr/ppermute | solution.py:22
  283.0 8.9 %collective-permute-start.2 = (f32[6,1,384]{2,1,0:T(1,128)S(1)}, f32[6,1,384]{2,1,0:T(1,128)S(1)}, u32[]{:S(2)}, u32[]{:S(2)}) collective-permute-start(f32[6,1,384]{2,1,0:T(1,128)S(1)} %get-tuple-element.253), channel_id=1, source_target_pairs={{1,0},{2,1},{3,2},{4,3},{5,4},{6,5},{7,6},{8,7},{9,8},{10,9},{11,1... | collective-permute-start | bytes 27656 | tf_op jit(solution)/shard_map/while/body/eval_jaxpr/ppermute | solution.py:23
  284.3 8.3 %collective-permute-start.3 = (f32[6,1,384]{2,1,0:T(1,128)S(1)}, f32[6,1,384]{2,1,0:T(1,128)S(1)}, u32[]{:S(2)}, u32[]{:S(2)}) collective-permute-start(f32[6,1,384]{2,1,0:T(1,128)S(1)} %get-tuple-element.254), channel_id=1, source_target_pairs={{0,1},{1,2},{2,3},{3,4},{4,5},{5,6},{6,7},{7,8},{8,9},{9,10},{10,1... | collective-permute-start | bytes 27656 | tf_op jit(solution)/shard_map/while/body/eval_jaxpr/ppermute | solution.py:22
  304.1 8.9 %collective-permute-start.2 = (f32[6,1,384]{2,1,0:T(1,128)S(1)}, f32[6,1,384]{2,1,0:T(1,128)S(1)}, u32[]{:S(2)}, u32[]{:S(2)}) collective-permute-start(f32[6,1,384]{2,1,0:T(1,128)S(1)} %get-tuple-element.253), channel_id=1, source_target_pairs={{1,0},{2,1},{3,2},{4,3},{5,4},{6,5},{7,6},{8,7},{9,8},{10,9},{11,1... | collective-permute-start | bytes 27656 | tf_op jit(solution)/shard_map/while/body/eval_jaxpr/ppermute | solution.py:23
  305.4 8.3 %collective-permute-start.3 = (f32[6,1,384]{2,1,0:T(1,128)S(1)}, f32[6,1,384]{2,1,0:T(1,128)S(1)}, u32[]{:S(2)}, u32[]{:S(2)}) collective-permute-start(f32[6,1,384]{2,1,0:T(1,128)S(1)} %get-tuple-element.254), channel_id=1, source_target_pairs={{0,1},{1,2},{2,3},{3,4},{4,5},{5,6},{6,7},{7,8},{8,9},{9,10},{10,1... | collective-permute-start | bytes 27656 | tf_op jit(solution)/shard_map/while/body/eval_jaxpr/ppermute | solution.py:22
  325.1 8.9 %collective-permute-start.2 = (f32[6,1,384]{2,1,0:T(1,128)S(1)}, f32[6,1,384]{2,1,0:T(1,128)S(1)}, u32[]{:S(2)}, u32[]{:S(2)}) collective-permute-start(f32[6,1,384]{2,1,0:T(1,128)S(1)} %get-tuple-element.253), channel_id=1, source_target_pairs={{1,0},{2,1},{3,2},{4,3},{5,4},{6,5},{7,6},{8,7},{9,8},{10,9},{11,1... | collective-permute-start | bytes 27656 | tf_op jit(solution)/shard_map/while/body/eval_jaxpr/ppermute | solution.py:23
  326.4 8.3 %collective-permute-start.3 = (f32[6,1,384]{2,1,0:T(1,128)S(1)}, f32[6,1,384]{2,1,0:T(1,128)S(1)}, u32[]{:S(2)}, u32[]{:S(2)}) collective-permute-start(f32[6,1,384]{2,1,0:T(1,128)S(1)} %get-tuple-element.254), channel_id=1, source_target_pairs={{0,1},{1,2},{2,3},{3,4},{4,5},{5,6},{6,7},{7,8},{8,9},{9,10},{10,1... | collective-permute-start | bytes 27656 | tf_op jit(solution)/shard_map/while/body/eval_jaxpr/ppermute | solution.py:22
  346.2 8.9 %collective-permute-start.2 = (f32[6,1,384]{2,1,0:T(1,128)S(1)}, f32[6,1,384]{2,1,0:T(1,128)S(1)}, u32[]{:S(2)}, u32[]{:S(2)}) collective-permute-start(f32[6,1,384]{2,1,0:T(1,128)S(1)} %get-tuple-element.253), channel_id=1, source_target_pairs={{1,0},{2,1},{3,2},{4,3},{5,4},{6,5},{7,6},{8,7},{9,8},{10,9},{11,1... | collective-permute-start | bytes 27656 | tf_op jit(solution)/shard_map/while/body/eval_jaxpr/ppermute | solution.py:23
  347.5 8.3 %collective-permute-start.3 = (f32[6,1,384]{2,1,0:T(1,128)S(1)}, f32[6,1,384]{2,1,0:T(1,128)S(1)}, u32[]{:S(2)}, u32[]{:S(2)}) collective-permute-start(f32[6,1,384]{2,1,0:T(1,128)S(1)} %get-tuple-element.254), channel_id=1, source_target_pairs={{0,1},{1,2},{2,3},{3,4},{4,5},{5,6},{6,7},{7,8},{8,9},{9,10},{10,1... | collective-permute-start | bytes 27656 | tf_op jit(solution)/shard_map/while/body/eval_jaxpr/ppermute | solution.py:22
  (53 other events, 628.9 us)
Sparse Core Ops, SparseCore 0:
  379.3 128.7 reduce-scatter.1
where the time goes:
time: 679 us; the launch traced here: 672 us
  starting transfers between devices  225 us (33%)
  waiting for transfers between devices  218 us (32%)
  blocking collectives  156 us (23%)
  local copies, waits for them, and re-layouts  27.2 us (4%)
  matrix products  21.7 us (3%)
  between operations  14.3 us (2%)
  other arithmetic  7.86 us (1%)
    ppermute x34, starting transfers between devices, with_halo(): before = lax.ppermute(last, axis, up)  164 us
    psum x1, blocking collectives, body(): traces = lax.psum(trace_block, 'gx') / jnp.sqrt(jnp.float32(sample_total))  156 us
    reduce_scatter x1, waiting for transfers between devices, body(): lax.psum_scatter(project(angles, coords, series_g, series_p), 'gy', scatt...  129 us
    ppermute x34, waiting for transfers between devices, with_halo(): after = lax.ppermute(initial, axis, down)  76.6 us
    ppermute x34, starting transfers between devices, with_halo(): after = lax.ppermute(initial, axis, down)  61 us
  transfers between devices with their start and end apart: 69, of which 34 were waited for; matrix products, arithmetic and copies ran while one was open for 0% of the time, Pallas kernels for 0%

commit v1 on v0

v1 whole, which is shorter than its diff:
```python
import jax
import jax.numpy as jnp
from jax import lax
from jax.experimental import pallas as pl
from jax.experimental.pallas import tpu as pltpu
from jax.sharding import PartitionSpec as P

STEPS = 16
START = 3000
KAPPA = 0.37
W = 4
F32 = jnp.float32
TURN = 6.283185307179586


def call(kernel, outs, scratch=(), name=None):
    return pl.pallas_call(
        kernel,
        out_shape=outs,
        scratch_shapes=list(scratch),
        compiler_params=pltpu.CompilerParams(vmem_limit_bytes=48 * 1024 * 1024),
        name=name,
    )


def low_half(shape):
    return lax.broadcasted_iota(jnp.int32, shape, len(shape) - 2) % 8 < 4


def edge_tiles(cur, bef):
    first, last = (cur[:, 0:8], bef[:, 0:8]), (cur[:, -8:], bef[:, -8:])
    keep = low_half(first[0].shape)
    down = jnp.where(keep, first[0], pltpu.roll(first[1], 4, 1))
    up = jnp.where(keep, pltpu.roll(last[1], 4, 1), last[0])
    return up, down


def prepare_kernel(cur_ref, bef_ref, mat_ref, state_ref, up_ref, down_ref):
    tx = cur_ref.shape[0]
    mat = mat_ref[...]
    gain = jnp.where(mat == 1, 0.0, jnp.where(mat == 2, F32(1.0) / F32(1.5), F32(1.0)))
    cur = jnp.where(mat == 1, 0.0, cur_ref[...])
    bef = jnp.where(mat == 1, 0.0, bef_ref[...])
    state_ref[0:tx] = cur
    state_ref[tx : 2 * tx] = bef
    state_ref[2 * tx :] = gain
    up, down = edge_tiles(cur, bef)
    up_ref[0:tx] = up
    up_ref[tx:] = gain[:, -8:]
    down_ref[0:tx] = down
    down_ref[tx:] = gain[:, 0:8]


def shifted(v, axis, by, edge):
    n = v.shape[axis]
    moved = pltpu.roll(v, by % n, axis)
    if not edge:
        return moved
    ids = lax.broadcasted_iota(jnp.int32, v.shape, axis)
    return jnp.where(ids == (0 if by == 1 else n - 1), 0.0, moved)


def neighbours(plane, x):
    v = plane(x)
    total = plane(x - 1) + plane(x + 1)
    total = total + (shifted(v, 0, 1, False) + shifted(v, 0, -1, False))
    return v, total + (shifted(v, 1, 1, True) + shifted(v, 1, -1, True))


def window_kernel(first, final, tx, ty, *refs):
    refs = list(refs)
    own, xlo, xhi = refs[:3]
    columns = (refs[3:6], refs[6:9])
    refs = refs[9:]
    if not first:
        gain_in, count_in = refs[:2]
        refs = refs[2:]
    cell_col, cell_row = refs[:2]
    refs = refs[2:]
    if final:
        out_cur, out_bef, sample_ref, one, two = refs
    elif first:
        state_ref, up_ref, down_ref, sample_ref, gain_out, count_out, one, two = refs
    else:
        state_ref, up_ref, down_ref, sample_ref, one, two = refs
    gain_ref, count_ref = (gain_out, count_out) if first else (gain_in, count_in)
    keep = low_half((tx, 8, own.shape[2]))
    for part, tiles in enumerate((xlo, own, xhi)):
        rows = slice(part * tx, (part + 1) * tx)
        lower, upper = columns[0][part], columns[1][part]
        one[rows, 0:ty] = tiles[0:tx]
        two[rows, 0:ty] = tiles[tx : 2 * tx]
        one[rows, ty:] = jnp.where(keep, upper[0:tx], lower[0:tx])
        two[rows, ty:] = pltpu.roll(jnp.where(keep, lower[0:tx], upper[0:tx]), 4, 1)
        if first:
            gain_ref[rows, 0:ty] = tiles[2 * tx :]
            gain_ref[rows, ty:] = jnp.where(keep, upper[tx:], lower[tx:])
    if first:
        count_ref[...] = jnp.zeros(count_ref.shape, F32)
        for x in range(1, 3 * tx - 1):
            opened = lambda i: jnp.where(gain_ref[i] > 0.0, F32(1.0), F32(0.0))
            count_ref[x] = neighbours(opened, x)[1]
    nz = own.shape[2]
    cell = cell_row[...]
    live = cell >= 0
    safe = jnp.maximum(cell, 0)
    lane = lax.broadcasted_iota(jnp.int32, (1, 128), 1)
    z_of = safe % nz + (lane >= 64).astype(jnp.int32)
    row_of = jnp.where(live, safe // nz, -1)
    zhot = (lax.broadcasted_iota(jnp.int32, (nz, 128), 0) == z_of).astype(jnp.bfloat16)
    rhot = lax.broadcasted_iota(jnp.int32, (tx * ty, 128), 0) == row_of

    for step in range(1, W + 1):
        cur, bef = (one, two) if step % 2 else (two, one)
        for x in range(step, 3 * tx - step):
            v, total = neighbours(lambda i: cur[i], x)
            b = bef[x]
            inner = 0.25 * (total - count_ref[x] * v) + 2.0 * (v - b)
            bef[x] = gain_ref[x] * inner + b
        now = bef[tx : 2 * tx, 0:ty].reshape(tx * ty, nz)
        high = now.astype(jnp.bfloat16)
        low = (now - high.astype(F32)).astype(jnp.bfloat16)
        dot = lambda a: jnp.dot(a, zhot, preferred_element_type=F32)
        picked = jnp.where(rhot, dot(high) + dot(low), 0.0)
        sample_ref[pl.ds(step - 1, 1), :] = jnp.sum(picked, axis=0, keepdims=True)
    cur, bef = (one, two) if W % 2 == 0 else (two, one)
    cur, bef = cur[tx : 2 * tx, 0:ty], bef[tx : 2 * tx, 0:ty]
    if final:
        out_cur[...] = cur
        out_bef[...] = bef
    else:
        state_ref[0:tx] = cur
        state_ref[tx:] = bef
        up, down = edge_tiles(cur, bef)
        up_ref[...] = up
        down_ref[...] = down


def sin_cos_turns(p):
    r = p - jnp.floor(p + 0.5)
    q = r * r
    s = F32(-0.00702838626472677)
    for c in (0.0820504017189708, -0.599252197803835, 2.55016331894515, -5.16771276462447, 3.14159265353629):
        s = s * q + F32(c)
    s = s * r
    c_ = F32(-0.0243963243010939)
    for c in (0.234937313786045, -1.33521200304381, 4.0587091595557, -4.93480213707881, 0.999999999779904):
        c_ = c_ * q + F32(c)
    return 2.0 * s * c_, 1.0 - 2.0 * s * s


def phase_kernel(coord_ref, angle_ref, high_ref, low_ref):
    ux, uy, uz = angle_ref[0:1], angle_ref[1:2], angle_ref[2:3]
    slots = 64
    for d in range(coord_ref.shape[0] // slots):
        rows = pl.ds(d * slots, slots)
        xyz = coord_ref[rows, :]
        turns = (KAPPA / TURN) * (ux * xyz[:, 0:1] + uy * xyz[:, 1:2] + uz * xyz[:, 2:3])
        s, c = sin_cos_turns(turns)
        for k, v in enumerate((uz * s - c, c)):
            high = v.astype(jnp.bfloat16)
            at = pl.ds((2 * d + k) * slots, slots)
            high_ref[at, :] = high
            low_ref[at, :] = (v - high.astype(F32)).astype(jnp.bfloat16)


def project_kernel(sample_ref, high_ref, low_ref, out_ref):
    total = jnp.zeros(out_ref.shape, F32)
    for d in range(sample_ref.shape[0]):
        s = sample_ref[d]
        rows = slice(d * 128, (d + 1) * 128)
        high = s.astype(jnp.bfloat16)
        low = (s - high.astype(F32)).astype(jnp.bfloat16)
        dot = lambda a, b: jnp.dot(a, b, preferred_element_type=F32)
        total = total + dot(high, high_ref[rows]) + (dot(low, high_ref[rows]) + dot(high, low_ref[rows]))
    out_ref[...] = total


def spectra_kernel(scale, trace_ref, wave_ref, spec_ref, out_ref):
    dot = lambda a, b: jnp.dot(a, b, preferred_element_type=F32, precision=lax.Precision.HIGHEST)
    traces = trace_ref[...] * F32(scale)
    out_ref[0] = spec_ref[0] + dot(wave_ref[0], traces)
    out_ref[1] = spec_ref[1] - dot(wave_ref[1], traces)


def steps_of(count, by):
    return [(i, i + by) for i in range(count) if 0 <= i + by < count]


def sum_gx(v):
    return lax.psum(v, "gx")


def body(pressure, previous, material, slot_cell, angles, spectra_in):
    tx, ty, nz = pressure.shape
    ngx, ngy = lax.axis_size("gx"), lax.axis_size("gy")
    gx, gy = lax.axis_index("gx"), lax.axis_index("gy")
    shape = lambda *s: jax.ShapeDtypeStruct(s, F32)

    def corner(v, dx, dy):
        pairs = [
            (i * ngy + j, (i + dx) * ngy + j + dy)
            for i in range(ngx)
            for j in range(ngy)
            if 0 <= i + dx < ngx and 0 <= j + dy < ngy
        ]
        return lax.ppermute(v, ("gx", "gy"), pairs)

    def exchange(state, up, down):
        xlo = lax.ppermute(state, "gx", steps_of(ngx, 1))
        xhi = lax.ppermute(state, "gx", steps_of(ngx, -1))
        lower = [corner(up, dx, 1) for dx in (1, 0, -1)]
        upper = [corner(down, dx, -1) for dx in (1, 0, -1)]
        return [state, xlo, xhi, *lower, *upper]

    cells = jnp.concatenate([slot_cell, slot_cell])[None, :]
    state, up, down = call(
        prepare_kernel, [shape(3 * tx, ty, nz), shape(2 * tx, 8, nz), shape(2 * tx, 8, nz)], name="prepare"
    )(pressure, previous, material)
    big = (3 * tx, ty + 8, nz)
    scratch = [pltpu.VMEM(big, F32), pltpu.VMEM(big, F32)]
    rounds = STEPS // W
    samples, extra = [], []
    for r in range(rounds):
        first, final = r == 0, r == rounds - 1
        outs = [shape(tx, ty, nz)] * 2 if final else [shape(2 * tx, ty, nz), shape(tx, 8, nz), shape(tx, 8, nz)]
        outs = outs + [shape(W, 128)] + ([shape(*big)] * 2 if first else [])
        kernel = lambda *refs, first=first, final=final: window_kernel(first, final, tx, ty, *refs)
        got = call(kernel, outs, scratch, name=f"window{r}")(*exchange(state, up, down), *extra, cells.T, cells)
        if final:
            current, before, sample = got
        elif first:
            state, up, down, sample, *extra = got
        else:
            state, up, down, sample = got
        samples.append(sample)

    row_cells = jnp.maximum(lax.all_gather(slot_cell, "gy"), 0)
    x_at = gx * tx + row_cells // (ty * nz)
    y_at = jnp.arange(ngy, dtype=jnp.int32)[:, None] * ty + row_cells // nz % ty
    coords = jnp.stack([x_at, y_at, row_cells % nz], axis=-1).astype(F32).reshape(-1, 3)
    own = spectra_in.shape[2]
    elevation, azimuth = lax.dynamic_slice_in_dim(angles, gy * own, own, axis=1)
    units = jnp.stack(
        [jnp.cos(elevation) * jnp.cos(azimuth), jnp.cos(elevation) * jnp.sin(azimuth), jnp.sin(elevation)]
    )
    depth = coords.shape[0] * 2
    half = jax.ShapeDtypeStruct((depth, own), jnp.bfloat16)
    high, low = call(phase_kernel, [half, half], name="phases")(coords, units)

    series = lax.all_gather(jnp.concatenate(samples), "gy")
    part = call(project_kernel, shape(STEPS, own), name="project")(series, high, low)
    traces = sum_gx(part)

    bin_local = spectra_in.shape[1]
    bin_total = bin_local * ngx
    bin_ids = gx * bin_local + jnp.arange(bin_local, dtype=jnp.int32)
    time_ids = jnp.arange(STEPS, dtype=jnp.int32)
    turn_ids = (START + time_ids)[None, :] * (bin_ids + 1)[:, None] % (2 * (bin_total + 1))
    theta = jnp.pi * turn_ids.astype(F32) / (bin_total + 1)
    waves = jnp.stack([jnp.cos(theta), jnp.sin(theta)])
    scale = float(slot_cell.shape[0] * ngx * ngy) ** -0.5
    spectra = call(
        lambda *refs: spectra_kernel(scale, *refs), shape(*spectra_in.shape), name="spectra"
    )(traces, waves, spectra_in)
    return current, before, spectra


def solution(mesh):
    return jax.shard_map(
        body,
        mesh=mesh,
        in_specs=(
            P("gx", "gy", None),
            P("gx", "gy", None),
            P("gx", "gy", None),
            P(("gx", "gy")),
            P(),
            P(None, "gx", "gy"),
        ),
        out_specs=(P("gx", "gy", None), P("gx", "gy", None), P(None, "gx", "gy")),
        check_vma=False,
    )
```

time: 679 us -> 395 us (0.58)
  the two profiles are of different devices: /device:TPU:1 before, /device:TPU:8 now
where the time goes in v1:
time: 395 us; the launch traced here: 393 us
  blocking collectives  218 us (55%)
  starting transfers between devices  127 us (32%)
  waiting for transfers between devices  20.7 us (5%)
  local copies, waits for them, and re-layouts  12.8 us (3%)
  Pallas kernels  11.9 us (3%)
    psum x1, blocking collectives, sum_gx(): return lax.psum(v, 'gx')  156 us
    ppermute x24, starting transfers between devices, corner(): return lax.ppermute(v, ('gx', 'gy'), pairs)  87 us
    all_gather x1, blocking collectives, body(): series = lax.all_gather(jnp.concatenate(samples), 'gy')  46 us
    ppermute x4, starting transfers between devices, exchange(): xhi = lax.ppermute(state, 'gx', steps_of(ngx, -1))  31.9 us
    ppermute x24, waiting for transfers between devices, corner(): return lax.ppermute(v, ('gx', 'gy'), pairs)  20.7 us
    unnamed x1, blocking collectives  15.6 us
    unnamed x41, local copies, waits for them, and re-layouts  11.1 us
    pallas_call x4, Pallas kernels, body(): call(kernel, outs, scratch, name=f'window{r}')  8.86 us
  transfers between devices with their start and end apart: 32, of which 11 were waited for; matrix products, arithmetic and copies ran while one was open for 1% of the time, Pallas kernels for 0%

profile of v1, /device:TPU:8, one launch (start us, length us, event | category | flops | bytes accessed | tf_op | source)
XLA Modules:
  0.0 393.4 jit_solution(1639853885589275248)
XLA Ops:
  5.4 13.9 %collective-permute-start.1 = (f32[12,32,384]{2,1,0:T(8,128)S(1)}, f32[12,32,384]{2,1,0:T(8,128)S(1)}, u32[]{:S(2)}, u32[]{:S(2)}) collective-permute-start(f32[12,32,384]{2,1,0:T(8,128)S(1)} %get-tuple-element.25.refs_0_), channel_id=1, source_target_pairs={{16,0},{32,16},{48,32},{64,48},{80,64},{96,80},{112,96},{128,112},... | collective-permute-start | bytes 1769480 | tf_op jit(solution)/shard_map/ppermute | solution.py:211
  20.7 5.1 %collective-permute-start.3 = (f32[8,8,384]{2,1,0:T(8,128)S(1)}, f32[8,8,384]{2,1,0:T(8,128)S(1)}, u32[]{:S(2)}, u32[]{:S(2)}) collective-permute-start(f32[8,8,384]{2,1,0:T(8,128)S(1)} %get-tuple-element.26), channel_id=1, source_target_pairs={{0,1},{1,2},{2,3},{3,4},{4,5},{5,6},{6,7},{7,8},{8,9},{9,10},{10,1... | collective-permute-start | bytes 294920 | tf_op jit(solution)/shard_map/ppermute | solution.py:207
  25.8 8.0 %collective-permute-start.4 = (f32[8,8,384]{2,1,0:T(8,128)S(1)}, f32[8,8,384]{2,1,0:T(8,128)S(1)}, u32[]{:S(2)}, u32[]{:S(2)}) collective-permute-start(f32[8,8,384]{2,1,0:T(8,128)S(1)} %get-tuple-element.26), channel_id=1, source_target_pairs={{16,1},{17,2},{18,3},{19,4},{20,5},{21,6},{22,7},{23,8},{24,9},{25... | collective-permute-start | bytes 294920 | tf_op jit(solution)/shard_map/ppermute | solution.py:207
  36.6 15.6 %all-reduce = s32[1024]{0:T(1024)S(1)} all-reduce(s32[1024]{0:T(1024)S(1)} %dynamic-update-slice), channel_id=3, replica_groups=mesh['gx'=48,'gy'=16] {'gy'}, use_global_device_ids=true, to_apply=%add | all-reduce | flops 1024 | bytes 8192
  56.3 3.9 collective-permute-done.5.refs_6_
  60.3 4.5 %collective-permute-done.6.refs_7_ = f32[8,8,384]{2,1,0:T(8,128)S(1)} collective-permute-done((f32[8,8,384]{2,1,0:T(8,128)S(1)}, f32[8,8,384]{2,1,0:T(8,128)S(1)}, u32[]{:S(2)}, u32[]{:S(2)}) %collective-permute-start.6) | collective-permute-done | bytes 98336 | tf_op jit(solution)/shard_map/ppermute | solution.py:207
  69.7 2.7 window0.1
  75.0 5.8 %collective-permute-start.9 = (f32[8,32,384]{2,1,0:T(8,128)S(1)}, f32[8,32,384]{2,1,0:T(8,128)S(1)}, u32[]{:S(2)}, u32[]{:S(2)}) collective-permute-start(f32[8,32,384]{2,1,0:T(8,128)S(1)} %get-tuple-element.28.refs_0_), channel_id=1, source_target_pairs={{16,0},{32,16},{48,32},{64,48},{80,64},{96,80},{112,96},{128,112},... | collective-permute-start | bytes 1179656 | tf_op jit(solution)/shard_map/ppermute | solution.py:211
  82.1 5.8 %collective-permute-start.11 = (f32[4,8,384]{2,1,0:T(8,128)}, f32[4,8,384]{2,1,0:T(8,128)S(1)}, u32[]{:S(2)}, u32[]{:S(2)}) collective-permute-start(f32[4,8,384]{2,1,0:T(8,128)} %get-tuple-element.29), channel_id=1, source_target_pairs={{0,1},{1,2},{2,3},{3,4},{4,5},{5,6},{6,7},{7,8},{8,9},{9,10},{10,1... | collective-permute-start | bytes 147464 | tf_op jit(solution)/shard_map/ppermute | solution.py:207
  87.9 10.4 %collective-permute-start.12 = (f32[4,8,384]{2,1,0:T(8,128)}, f32[4,8,384]{2,1,0:T(8,128)S(1)}, u32[]{:S(2)}, u32[]{:S(2)}) collective-permute-start(f32[4,8,384]{2,1,0:T(8,128)} %get-tuple-element.29), channel_id=1, source_target_pairs={{16,1},{17,2},{18,3},{19,4},{20,5},{21,6},{22,7},{23,8},{24,9},{25... | collective-permute-start | bytes 147464 | tf_op jit(solution)/shard_map/ppermute | solution.py:207
  102.7 3.5 collective-permute-done.13.refs_6_
  111.3 6.1 %collective-permute-start.17 = (f32[8,32,384]{2,1,0:T(8,128)S(1)}, f32[8,32,384]{2,1,0:T(8,128)S(1)}, u32[]{:S(2)}, u32[]{:S(2)}) collective-permute-start(f32[8,32,384]{2,1,0:T(8,128)S(1)} %get-tuple-element.33.refs_0_), channel_id=1, source_target_pairs={{16,0},{32,16},{48,32},{64,48},{80,64},{96,80},{112,96},{128,112},... | collective-permute-start | bytes 1179656 | tf_op jit(solution)/shard_map/ppermute | solution.py:211
  117.5 2.5 collective-permute-start.18
  120.0 7.8 %collective-permute-start.19 = (f32[4,8,384]{2,1,0:T(8,128)S(1)}, f32[4,8,384]{2,1,0:T(8,128)S(1)}, u32[]{:S(2)}, u32[]{:S(2)}) collective-permute-start(f32[4,8,384]{2,1,0:T(8,128)S(1)} %get-tuple-element.34), channel_id=1, source_target_pairs={{0,1},{1,2},{2,3},{3,4},{4,5},{5,6},{6,7},{7,8},{8,9},{9,10},{10,1... | collective-permute-start | bytes 147464 | tf_op jit(solution)/shard_map/ppermute | solution.py:207
  127.9 10.2 %collective-permute-start.20 = (f32[4,8,384]{2,1,0:T(8,128)S(1)}, f32[4,8,384]{2,1,0:T(8,128)S(1)}, u32[]{:S(2)}, u32[]{:S(2)}) collective-permute-start(f32[4,8,384]{2,1,0:T(8,128)S(1)} %get-tuple-element.34), channel_id=1, source_target_pairs={{16,1},{17,2},{18,3},{19,4},{20,5},{21,6},{22,7},{23,8},{24,9},{25... | collective-permute-start | bytes 147464 | tf_op jit(solution)/shard_map/ppermute | solution.py:207
  142.1 3.5 collective-permute-done.21.refs_6_
  147.0 2.2 window2.1
  151.2 6.1 %collective-permute-start.25 = (f32[8,32,384]{2,1,0:T(8,128)S(1)}, f32[8,32,384]{2,1,0:T(8,128)S(1)}, u32[]{:S(2)}, u32[]{:S(2)}) collective-permute-start(f32[8,32,384]{2,1,0:T(8,128)S(1)} %get-tuple-element.36.refs_0_), channel_id=1, source_target_pairs={{16,0},{32,16},{48,32},{64,48},{80,64},{96,80},{112,96},{128,112},... | collective-permute-start | bytes 1179656 | tf_op jit(solution)/shard_map/ppermute | solution.py:211
  158.2 2.5 collective-permute-start.26
  160.7 7.8 %collective-permute-start.27 = (f32[4,8,384]{2,1,0:T(8,128)S(1)}, f32[4,8,384]{2,1,0:T(8,128)S(1)}, u32[]{:S(2)}, u32[]{:S(2)}) collective-permute-start(f32[4,8,384]{2,1,0:T(8,128)S(1)} %get-tuple-element.37), channel_id=1, source_target_pairs={{0,1},{1,2},{2,3},{3,4},{4,5},{5,6},{6,7},{7,8},{8,9},{9,10},{10,1... | collective-permute-start | bytes 147464 | tf_op jit(solution)/shard_map/ppermute | solution.py:207
  168.6 8.5 %collective-permute-start.28 = (f32[4,8,384]{2,1,0:T(8,128)S(1)}, f32[4,8,384]{2,1,0:T(8,128)S(1)}, u32[]{:S(2)}, u32[]{:S(2)}) collective-permute-start(f32[4,8,384]{2,1,0:T(8,128)S(1)} %get-tuple-element.37), channel_id=1, source_target_pairs={{16,1},{17,2},{18,3},{19,4},{20,5},{21,6},{22,7},{23,8},{24,9},{25... | collective-permute-start | bytes 147464 | tf_op jit(solution)/shard_map/ppermute | solution.py:207
  187.1 2.3 window3.1
  190.1 46.0 %all-gather = f32[256,128]{1,0:T(8,128)S(1)} all-gather(f32[16,128]{1,0:T(8,128)S(1)} %pad_maximum_fusion), channel_id=2, replica_groups=mesh['gx'=48,'gy'=16] {'gy'}, dimensions={0}, use_global_device_ids=true | all-gather | bytes 139264 | tf_op jit(solution)/shard_map/all_gather | solution.py:251
  236.6 156.1 %psum.7.refs_0_ = f32[16,256]{1,0:T(8,128)S(1)} all-reduce(f32[16,256]{1,0:T(8,128)S(1)} %project.1), channel_id=1, replica_groups=mesh['gx'=48,'gy'=16] {'gx'}, use_global_device_ids=true, to_apply=%region_0.1 | all-reduce | flops 4096 | bytes 32768 | tf_op jit(solution)/shard_map/psum | solution.py:191
  (115 shorter events, 50.7 us)
Async XLA Ops:
  3.5 62.5 %collective-permute-start = (f32[12,32,384]{2,1,0:T(8,128)S(1)}, f32[12,32,384]{2,1,0:T(8,128)S(1)}, u32[]{:S(2)}, u32[]{:S(2)}) collective-permute-start(f32[12,32,384]{2,1,0:T(8,128)S(1)} %get-tuple-element.25.refs_0_), channel_id=1, source_target_pairs={{0,16},{16,32},{32,48},{48,64},{64,80},{80,96},{96,112},{112,128},... | collective-permute-start | bytes 1769480 | tf_op jit(solution)/shard_map/ppermute | solution.py:210
  5.4 60.6 %collective-permute-start.1 = (f32[12,32,384]{2,1,0:T(8,128)S(1)}, f32[12,32,384]{2,1,0:T(8,128)S(1)}, u32[]{:S(2)}, u32[]{:S(2)}) collective-permute-start(f32[12,32,384]{2,1,0:T(8,128)S(1)} %get-tuple-element.25.refs_0_), channel_id=1, source_target_pairs={{16,0},{32,16},{48,32},{64,48},{80,64},{96,80},{112,96},{128,112},... | collective-permute-start | bytes 1769480 | tf_op jit(solution)/shard_map/ppermute | solution.py:211
  19.4 32.8 %collective-permute-start.2 = (f32[8,8,384]{2,1,0:T(8,128)S(1)}, f32[8,8,384]{2,1,0:T(8,128)S(1)}, u32[]{:S(2)}, u32[]{:S(2)}) collective-permute-start(f32[8,8,384]{2,1,0:T(8,128)S(1)} %get-tuple-element.26), channel_id=1, source_target_pairs={{0,17},{1,18},{2,19},{3,20},{4,21},{5,22},{6,23},{7,24},{8,25},{9,... | collective-permute-start | bytes 294920 | tf_op jit(solution)/shard_map/ppermute | solution.py:207
  20.7 32.8 %collective-permute-start.3 = (f32[8,8,384]{2,1,0:T(8,128)S(1)}, f32[8,8,384]{2,1,0:T(8,128)S(1)}, u32[]{:S(2)}, u32[]{:S(2)}) collective-permute-start(f32[8,8,384]{2,1,0:T(8,128)S(1)} %get-tuple-element.26), channel_id=1, source_target_pairs={{0,1},{1,2},{2,3},{3,4},{4,5},{5,6},{6,7},{7,8},{8,9},{9,10},{10,1... | collective-permute-start | bytes 294920 | tf_op jit(solution)/shard_map/ppermute | solution.py:207
  25.8 29.0 %collective-permute-start.4 = (f32[8,8,384]{2,1,0:T(8,128)S(1)}, f32[8,8,384]{2,1,0:T(8,128)S(1)}, u32[]{:S(2)}, u32[]{:S(2)}) collective-permute-start(f32[8,8,384]{2,1,0:T(8,128)S(1)} %get-tuple-element.26), channel_id=1, source_target_pairs={{16,1},{17,2},{18,3},{19,4},{20,5},{21,6},{22,7},{23,8},{24,9},{25... | collective-permute-start | bytes 294920 | tf_op jit(solution)/shard_map/ppermute | solution.py:207
  52.2 8.0 %collective-permute-start.5 = (f32[8,8,384]{2,1,0:T(8,128)S(1)}, f32[8,8,384]{2,1,0:T(8,128)S(1)}, u32[]{:S(2)}, u32[]{:S(2)}) collective-permute-start(f32[8,8,384]{2,1,0:T(8,128)S(1)} %get-tuple-element.27), channel_id=1, source_target_pairs={{1,16},{2,17},{3,18},{4,19},{5,20},{6,21},{7,22},{8,23},{9,24},{10... | collective-permute-start | bytes 294920 | tf_op jit(solution)/shard_map/ppermute | solution.py:207
  53.5 11.2 %collective-permute-start.6 = (f32[8,8,384]{2,1,0:T(8,128)S(1)}, f32[8,8,384]{2,1,0:T(8,128)S(1)}, u32[]{:S(2)}, u32[]{:S(2)}) collective-permute-start(f32[8,8,384]{2,1,0:T(8,128)S(1)} %get-tuple-element.27), channel_id=1, source_target_pairs={{1,0},{2,1},{3,2},{4,3},{5,4},{6,5},{7,6},{8,7},{9,8},{10,9},{11,1... | collective-permute-start | bytes 294920 | tf_op jit(solution)/shard_map/ppermute | solution.py:207
  54.8 10.6 %collective-permute-start.7 = (f32[8,8,384]{2,1,0:T(8,128)S(1)}, f32[8,8,384]{2,1,0:T(8,128)S(1)}, u32[]{:S(2)}, u32[]{:S(2)}) collective-permute-start(f32[8,8,384]{2,1,0:T(8,128)S(1)} %get-tuple-element.27), channel_id=1, source_target_pairs={{17,0},{18,1},{19,2},{20,3},{21,4},{22,5},{23,6},{24,7},{25,8},{26... | collective-permute-start | bytes 294920 | tf_op jit(solution)/shard_map/ppermute | solution.py:207
  73.0 34.6 %collective-permute-start.8 = (f32[8,32,384]{2,1,0:T(8,128)S(1)}, f32[8,32,384]{2,1,0:T(8,128)S(1)}, u32[]{:S(2)}, u32[]{:S(2)}) collective-permute-start(f32[8,32,384]{2,1,0:T(8,128)S(1)} %get-tuple-element.28.refs_0_), channel_id=1, source_target_pairs={{0,16},{16,32},{32,48},{48,64},{64,80},{80,96},{96,112},{112,128},... | collective-permute-start | bytes 1179656 | tf_op jit(solution)/shard_map/ppermute | solution.py:210
  75.0 32.6 %collective-permute-start.9 = (f32[8,32,384]{2,1,0:T(8,128)S(1)}, f32[8,32,384]{2,1,0:T(8,128)S(1)}, u32[]{:S(2)}, u32[]{:S(2)}) collective-permute-start(f32[8,32,384]{2,1,0:T(8,128)S(1)} %get-tuple-element.28.refs_0_), channel_id=1, source_target_pairs={{16,0},{32,16},{48,32},{64,48},{80,64},{96,80},{112,96},{128,112},... | collective-permute-start | bytes 1179656 | tf_op jit(solution)/shard_map/ppermute | solution.py:211
  80.8 17.9 %collective-permute-start.10 = (f32[4,8,384]{2,1,0:T(8,128)}, f32[4,8,384]{2,1,0:T(8,128)S(1)}, u32[]{:S(2)}, u32[]{:S(2)}) collective-permute-start(f32[4,8,384]{2,1,0:T(8,128)} %get-tuple-element.29), channel_id=1, source_target_pairs={{0,17},{1,18},{2,19},{3,20},{4,21},{5,22},{6,23},{7,24},{8,25},{9,... | collective-permute-start | bytes 147464 | tf_op jit(solution)/shard_map/ppermute | solution.py:207
  82.1 17.9 %collective-permute-start.11 = (f32[4,8,384]{2,1,0:T(8,128)}, f32[4,8,384]{2,1,0:T(8,128)S(1)}, u32[]{:S(2)}, u32[]{:S(2)}) collective-permute-start(f32[4,8,384]{2,1,0:T(8,128)} %get-tuple-element.29), channel_id=1, source_target_pairs={{0,1},{1,2},{2,3},{3,4},{4,5},{5,6},{6,7},{7,8},{8,9},{9,10},{10,1... | collective-permute-start | bytes 147464 | tf_op jit(solution)/shard_map/ppermute | solution.py:207
  87.9 13.4 %collective-permute-start.12 = (f32[4,8,384]{2,1,0:T(8,128)}, f32[4,8,384]{2,1,0:T(8,128)S(1)}, u32[]{:S(2)}, u32[]{:S(2)}) collective-permute-start(f32[4,8,384]{2,1,0:T(8,128)} %get-tuple-element.29), channel_id=1, source_target_pairs={{16,1},{17,2},{18,3},{19,4},{20,5},{21,6},{22,7},{23,8},{24,9},{25... | collective-permute-start | bytes 147464 | tf_op jit(solution)/shard_map/ppermute | solution.py:207
  109.4 37.7 %collective-permute-start.16 = (f32[8,32,384]{2,1,0:T(8,128)S(1)}, f32[8,32,384]{2,1,0:T(8,128)S(1)}, u32[]{:S(2)}, u32[]{:S(2)}) collective-permute-start(f32[8,32,384]{2,1,0:T(8,128)S(1)} %get-tuple-element.33.refs_0_), channel_id=1, source_target_pairs={{0,16},{16,32},{32,48},{48,64},{64,80},{80,96},{96,112},{112,128},... | collective-permute-start | bytes 1179656 | tf_op jit(solution)/shard_map/ppermute | solution.py:210
  111.3 35.7 %collective-permute-start.17 = (f32[8,32,384]{2,1,0:T(8,128)S(1)}, f32[8,32,384]{2,1,0:T(8,128)S(1)}, u32[]{:S(2)}, u32[]{:S(2)}) collective-permute-start(f32[8,32,384]{2,1,0:T(8,128)S(1)} %get-tuple-element.33.refs_0_), channel_id=1, source_target_pairs={{16,0},{32,16},{48,32},{64,48},{80,64},{96,80},{112,96},{128,112},... | collective-permute-start | bytes 1179656 | tf_op jit(solution)/shard_map/ppermute | solution.py:211
  117.5 20.6 %collective-permute-start.18 = (f32[4,8,384]{2,1,0:T(8,128)S(1)}, f32[4,8,384]{2,1,0:T(8,128)S(1)}, u32[]{:S(2)}, u32[]{:S(2)}) collective-permute-start(f32[4,8,384]{2,1,0:T(8,128)S(1)} %get-tuple-element.34), channel_id=1, source_target_pairs={{0,17},{1,18},{2,19},{3,20},{4,21},{5,22},{6,23},{7,24},{8,25},{9,... | collective-permute-start | bytes 147464 | tf_op jit(solution)/shard_map/ppermute | solution.py:207
  120.0 19.4 %collective-permute-start.19 = (f32[4,8,384]{2,1,0:T(8,128)S(1)}, f32[4,8,384]{2,1,0:T(8,128)S(1)}, u32[]{:S(2)}, u32[]{:S(2)}) collective-permute-start(f32[4,8,384]{2,1,0:T(8,128)S(1)} %get-tuple-element.34), channel_id=1, source_target_pairs={{0,1},{1,2},{2,3},{3,4},{4,5},{5,6},{6,7},{7,8},{8,9},{9,10},{10,1... | collective-permute-start | bytes 147464 | tf_op jit(solution)/shard_map/ppermute | solution.py:207
  127.9 12.8 %collective-permute-start.20 = (f32[4,8,384]{2,1,0:T(8,128)S(1)}, f32[4,8,384]{2,1,0:T(8,128)S(1)}, u32[]{:S(2)}, u32[]{:S(2)}) collective-permute-start(f32[4,8,384]{2,1,0:T(8,128)S(1)} %get-tuple-element.34), channel_id=1, source_target_pairs={{16,1},{17,2},{18,3},{19,4},{20,5},{21,6},{22,7},{23,8},{24,9},{25... | collective-permute-start | bytes 147464 | tf_op jit(solution)/shard_map/ppermute | solution.py:207
  149.3 37.9 %collective-permute-start.24 = (f32[8,32,384]{2,1,0:T(8,128)S(1)}, f32[8,32,384]{2,1,0:T(8,128)S(1)}, u32[]{:S(2)}, u32[]{:S(2)}) collective-permute-start(f32[8,32,384]{2,1,0:T(8,128)S(1)} %get-tuple-element.36.refs_0_), channel_id=1, source_target_pairs={{0,16},{16,32},{32,48},{48,64},{64,80},{80,96},{96,112},{112,128},... | collective-permute-start | bytes 1179656 | tf_op jit(solution)/shard_map/ppermute | solution.py:210
  151.2 35.9 %collective-permute-start.25 = (f32[8,32,384]{2,1,0:T(8,128)S(1)}, f32[8,32,384]{2,1,0:T(8,128)S(1)}, u32[]{:S(2)}, u32[]{:S(2)}) collective-permute-start(f32[8,32,384]{2,1,0:T(8,128)S(1)} %get-tuple-element.36.refs_0_), channel_id=1, source_target_pairs={{16,0},{32,16},{48,32},{64,48},{80,64},{96,80},{112,96},{128,112},... | collective-permute-start | bytes 1179656 | tf_op jit(solution)/shard_map/ppermute | solution.py:211
  158.2 19.8 %collective-permute-start.26 = (f32[4,8,384]{2,1,0:T(8,128)S(1)}, f32[4,8,384]{2,1,0:T(8,128)S(1)}, u32[]{:S(2)}, u32[]{:S(2)}) collective-permute-start(f32[4,8,384]{2,1,0:T(8,128)S(1)} %get-tuple-element.37), channel_id=1, source_target_pairs={{0,17},{1,18},{2,19},{3,20},{4,21},{5,22},{6,23},{7,24},{8,25},{9,... | collective-permute-start | bytes 147464 | tf_op jit(solution)/shard_map/ppermute | solution.py:207
  160.7 18.5 %collective-permute-start.27 = (f32[4,8,384]{2,1,0:T(8,128)S(1)}, f32[4,8,384]{2,1,0:T(8,128)S(1)}, u32[]{:S(2)}, u32[]{:S(2)}) collective-permute-start(f32[4,8,384]{2,1,0:T(8,128)S(1)} %get-tuple-element.37), channel_id=1, source_target_pairs={{0,1},{1,2},{2,3},{3,4},{4,5},{5,6},{6,7},{7,8},{8,9},{9,10},{10,1... | collective-permute-start | bytes 147464 | tf_op jit(solution)/shard_map/ppermute | solution.py:207
  168.6 12.0 %collective-permute-start.28 = (f32[4,8,384]{2,1,0:T(8,128)S(1)}, f32[4,8,384]{2,1,0:T(8,128)S(1)}, u32[]{:S(2)}, u32[]{:S(2)}) collective-permute-start(f32[4,8,384]{2,1,0:T(8,128)S(1)} %get-tuple-element.37), channel_id=1, source_target_pairs={{16,1},{17,2},{18,3},{19,4},{20,5},{21,6},{22,7},{23,8},{24,9},{25... | collective-permute-start | bytes 147464 | tf_op jit(solution)/shard_map/ppermute | solution.py:207
  178.0 7.7 %collective-permute-start.29 = (f32[4,8,384]{2,1,0:T(8,128)}, f32[4,8,384]{2,1,0:T(8,128)S(1)}, u32[]{:S(2)}, u32[]{:S(2)}) collective-permute-start(f32[4,8,384]{2,1,0:T(8,128)} %get-tuple-element.38), channel_id=1, source_target_pairs={{1,16},{2,17},{3,18},{4,19},{5,20},{6,21},{7,22},{8,23},{9,24},{10... | collective-permute-start | bytes 147464 | tf_op jit(solution)/shard_map/ppermute | solution.py:207
  (27 other events, 273.5 us)

commit v2 on v0

v2 whole, which is shorter than its diff:
```python
import jax
import jax.numpy as jnp
from jax import lax
from jax.experimental import pallas as pl
from jax.experimental.pallas import tpu as pltpu
from jax.sharding import PartitionSpec as P

STEPS = 16
START = 3000
KAPPA = 0.37
W = 4
Y = 8
F32 = jnp.float32
BF16 = jnp.bfloat16
TURN = 6.283185307179586


def call(kernel, outs, scratch=(), name=None):
    return pl.pallas_call(
        kernel,
        out_shape=outs,
        scratch_shapes=list(scratch),
        compiler_params=pltpu.CompilerParams(vmem_limit_bytes=48 * 1024 * 1024),
        name=name,
    )


def edges(ref, ty):
    even = lax.axis_index("gy") % 2 == 0
    top, bottom = ty - Y, 0
    at = lambda row: ref[:, pl.ds(pl.multiple_of(row, 8), Y)]
    return at(jnp.where(even, top, bottom)), at(jnp.where(even, bottom, top))


def prepare_kernel(cur_ref, bef_ref, mat_ref, state_ref, a_ref, b_ref):
    tx, ty, _ = cur_ref.shape
    mat = mat_ref[...]
    state_ref[0:tx] = jnp.where(mat == 1, 0.0, cur_ref[...])
    state_ref[tx : 2 * tx] = jnp.where(mat == 1, 0.0, bef_ref[...])
    state_ref[2 * tx :] = jnp.where(mat == 1, 0.0, jnp.where(mat == 2, F32(1.0) / F32(1.5), F32(1.0)))
    a_ref[...], b_ref[...] = edges(state_ref, ty)


def shifted(v, axis, by, edge):
    n = v.shape[axis]
    moved = pltpu.roll(v, by % n, axis)
    if not edge:
        return moved
    ids = lax.broadcasted_iota(jnp.int32, v.shape, axis)
    return jnp.where(ids == (0 if by == 1 else n - 1), 0.0, moved)


def neighbours(plane, x):
    v = plane(x)
    total = plane(x - 1) + plane(x + 1)
    total = total + (shifted(v, 0, 1, False) + shifted(v, 0, -1, False))
    return v, total + (shifted(v, 1, 1, True) + shifted(v, 1, -1, True))


def narrow(v, ty):
    above, below = v[..., ty : ty + 8, :], v[..., ty + 8 :, :]
    low = lax.broadcasted_iota(jnp.int32, above.shape, above.ndim - 2) < 4
    return jnp.concatenate([v[..., 0:ty, :], jnp.where(low, above, below)], axis=-2)


def window_kernel(kind, tx, ty, *refs):
    refs = list(refs)
    take = lambda n: [refs.pop(0) for _ in range(n)]
    own, x_a, x_b = take(3)
    (cell_row,) = take(1)
    if kind != "first":
        gain_ref, count_ref = take(2)
    done = take(3) if kind == "last" else ()
    if kind == "last":
        out_cur, out_bef, series_ref = take(3)
    else:
        state_ref, *rest = take({"first": 1, "inner": 3, "wide": 1}[kind])
        (sample_ref,) = take(1)
    if kind == "first":
        gain_ref, count_ref, gain4_ref, count4_ref = take(4)
    one, two = take(2)
    nz = own.shape[2]
    odd = lax.axis_index("gx") % 2
    at_a = (1 - odd) * 2 * tx
    at_b = odd * 2 * tx
    for at, tiles in ((tx, own), (at_a, x_a), (at_b, x_b)):
        one[pl.ds(at, tx)] = tiles[0:tx]
        two[pl.ds(at, tx)] = tiles[tx : 2 * tx]
        if kind == "first":
            gain_ref[pl.ds(at, tx)] = tiles[2 * tx :]
    if kind == "first":
        count_ref[...] = jnp.zeros(count_ref.shape, F32)
        opened = lambda i: jnp.where(gain_ref[i] > 0.0, F32(1.0), F32(0.0))
        for x in range(1, 3 * tx - 1):
            count_ref[x] = neighbours(opened, x)[1]
        gain4_ref[...] = narrow(gain_ref[...], ty)
        count4_ref[...] = narrow(count_ref[...], ty)
    cell = cell_row[...]
    safe = jnp.maximum(cell, 0)
    lane = lax.broadcasted_iota(jnp.int32, (1, 128), 1)
    z_of = safe % nz + (lane >= 64).astype(jnp.int32)
    row_of = jnp.where(cell >= 0, safe // nz, -1)
    zhot = (lax.broadcasted_iota(jnp.int32, (nz, 128), 0) == z_of).astype(BF16)
    rhot = lax.broadcasted_iota(jnp.int32, (tx * ty, 128), 0) == row_of

    picks = []
    for step in range(1, W + 1):
        cur, bef = (one, two) if step % 2 else (two, one)
        for x in range(step, 3 * tx - step):
            v, total = neighbours(lambda i: cur[i], x)
            b = bef[x]
            inner = 0.25 * (total - count_ref[x] * v) + 2.0 * (v - b)
            bef[x] = gain_ref[x] * inner + b
        now = bef[tx : 2 * tx, 0:ty].reshape(tx * ty, nz)
        high = now.astype(BF16)
        low = (now - high.astype(F32)).astype(BF16)
        dot = lambda a: jnp.dot(a, zhot, preferred_element_type=F32)
        picked = jnp.where(rhot, dot(high) + dot(low), 0.0)
        picks.append(jnp.sum(picked, axis=0, keepdims=True))
    cur, bef = (one, two) if W % 2 == 0 else (two, one)
    cur, bef = cur.at[tx : 2 * tx], bef.at[tx : 2 * tx]
    if kind == "last":
        out_cur[...] = cur[:, 0:ty]
        out_bef[...] = bef[:, 0:ty]
        cells = jnp.broadcast_to(cell.astype(F32), (8, 128))
        series = jnp.concatenate([*(d[...] for d in done), *picks, cells])
        for d in range(series_ref.shape[0]):
            series_ref[d] = series
        return
    for k, pick in enumerate(picks):
        sample_ref[pl.ds(k, 1), :] = pick
    if kind == "inner":
        state_ref[0:tx] = cur[:, 0:ty]
        state_ref[tx:] = bef[:, 0:ty]
        rest[0][...], rest[1][...] = edges(state_ref, ty)
    else:
        state_ref[0:tx] = narrow(cur[...], ty)
        state_ref[tx:] = narrow(bef[...], ty)


def sin_cos_turns(p):
    r = p - jnp.floor(p + 0.5)
    q = r * r
    s = F32(-0.00702838626472677)
    for k in (0.0820504017189708, -0.599252197803835, 2.55016331894515, -5.16771276462447, 3.14159265353629):
        s = s * q + F32(k)
    s = s * r
    c = F32(-0.0243963243010939)
    for k in (0.234937313786045, -1.33521200304381, 4.0587091595557, -4.93480213707881, 0.999999999779904):
        c = c * q + F32(k)
    return 2.0 * s * c, 1.0 - 2.0 * s * s


def project_kernel(tx, ty, nz, own, series_ref, angle_ref, out_ref):
    slots = 64
    ndev, _, lanes = series_ref.shape
    at = pl.multiple_of(lax.axis_index("gy") * own, 128)
    sin_e, cos_e = sin_cos_turns(angle_ref[0:1, pl.ds(at, own)] * (1.0 / TURN))
    sin_a, cos_a = sin_cos_turns(angle_ref[1:2, pl.ds(at, own)] * (1.0 / TURN))
    ux, uy, uz = cos_e * cos_a, cos_e * sin_a, sin_e
    rows = [series_ref[d, STEPS : STEPS + 1, :] for d in range(ndev)]
    cells = jnp.concatenate([*rows, jnp.zeros((lanes - ndev, lanes), F32)]).T[0:slots]
    cells = jnp.maximum(cells, 0.0).astype(jnp.int32)
    device = lax.broadcasted_iota(jnp.int32, cells.shape, 1)
    x_of = (lax.axis_index("gx") * tx + cells // (ty * nz)).astype(F32)
    y_of = (device * ty + cells // nz % ty).astype(F32)
    z_of = (cells % nz).astype(F32)
    total = jnp.zeros((STEPS, own), F32)
    for d in range(ndev):
        column = lambda v: v[:, d : d + 1]
        turns = (KAPPA / TURN) * (ux * column(x_of) + uy * column(y_of) + uz * column(z_of))
        s, c = sin_cos_turns(turns)
        waves = jnp.concatenate([uz * s - c, c])
        wave_high = waves.astype(BF16)
        wave_low = (waves - wave_high.astype(F32)).astype(BF16)
        v = series_ref[d, 0:STEPS, :]
        high = v.astype(BF16)
        low = (v - high.astype(F32)).astype(BF16)
        dot = lambda a, b: jnp.dot(a, b, preferred_element_type=F32)
        total = total + dot(high, wave_high) + (dot(low, wave_high) + dot(high, wave_low))
    out_ref[...] = jnp.zeros(out_ref.shape, F32)
    for k in range(own // 128):
        out_ref[k * STEPS : (k + 1) * STEPS] = total[:, k * 128 : (k + 1) * 128]


def sum_kernel(part_ref, out_ref):
    total = jnp.sum(part_ref[...], axis=0, keepdims=True)
    out_ref[...] = jnp.broadcast_to(total, out_ref.shape)


def spectra_kernel(scale, bin_total, trace_ref, spec_ref, out_ref):
    bins = spec_ref.shape[1]
    period = 2 * (bin_total + 1)
    bin_of = lax.axis_index("gx") * bins + lax.broadcasted_iota(jnp.int32, (bins, STEPS), 0) + 1
    step_of = lax.broadcasted_iota(jnp.int32, (bins, STEPS), 1) + START
    turn = (step_of * bin_of).astype(F32)
    turn = turn - period * jnp.floor(turn * (1.0 / period))
    sin_t, cos_t = sin_cos_turns(turn * (1.0 / period))
    parts = [trace_ref[k * STEPS : (k + 1) * STEPS] for k in range(spec_ref.shape[2] // 128)]
    traces = jnp.concatenate(parts, axis=1) * F32(scale)
    dot = lambda a: jnp.dot(a, traces, preferred_element_type=F32, precision=lax.Precision.HIGHEST)
    out_ref[0] = spec_ref[0] + dot(cos_t)
    out_ref[1] = spec_ref[1] - dot(sin_t)


def swap(v, axis):
    count = lax.axis_size(axis)
    even_odd = [(i, i ^ 1) for i in range(count) if i ^ 1 < count]
    odd_even = [(i, ((i + 1) ^ 1) - 1) for i in range(1, count) if ((i + 1) ^ 1) - 1 < count]
    v_a, v_b = v
    got_b = lax.ppermute(v_b, axis, odd_even)
    return lax.ppermute(v_a, axis, even_odd), got_b


def body(pressure, previous, material, slot_cell, angles, spectra_in):
    tx, ty, nz = pressure.shape
    ngx, ngy = lax.axis_size("gx"), lax.axis_size("gy")
    even_y = lax.axis_index("gy") % 2 == 0
    shape = lambda *s: jax.ShapeDtypeStruct(s, F32)
    window = lambda kind: lambda *refs: window_kernel(kind, tx, ty, *refs)
    wide, thin = (3 * tx, ty + 2 * Y, nz), (3 * tx, ty + 2 * W, nz)
    scratch = lambda s: [pltpu.VMEM(s, F32)] * 2

    def exchange_y(state, a, b):
        a, b = swap((a, b), "gy")
        return jnp.concatenate([state, jnp.where(even_y, a, b), jnp.where(even_y, b, a)], axis=1)

    def exchange_x(state):
        return [state, *swap((state, state), "gx"), cells]

    cells = jnp.concatenate([slot_cell, slot_cell])[None, :]
    state, a, b = call(
        prepare_kernel, [shape(3 * tx, ty, nz), shape(3 * tx, Y, nz), shape(3 * tx, Y, nz)], name="prepare"
    )(pressure, previous, material)
    state = exchange_y(state, a, b)
    part = shape(W, 128)
    state, first, gain, count, gain4, count4 = call(
        window("first"),
        [shape(2 * tx, *thin[1:]), part, shape(*wide), shape(*wide), shape(*thin), shape(*thin)],
        scratch(wide),
        name="window_first",
    )(*exchange_x(state))
    state, a, b, second = call(
        window("inner"), [shape(2 * tx, ty, nz), shape(2 * tx, Y, nz), shape(2 * tx, Y, nz), part], scratch(thin), name="window_inner"
    )(*exchange_x(state), gain4, count4)
    state = exchange_y(state, a, b)
    state, third = call(window("wide"), [shape(2 * tx, *thin[1:]), part], scratch(wide), name="window_wide")(
        *exchange_x(state), gain, count
    )
    current, before, series = call(
        window("last"), [shape(tx, ty, nz), shape(tx, ty, nz), shape(ngy, STEPS + 8, 128)], scratch(thin), name="window_last"
    )(*exchange_x(state), gain4, count4, first, second, third)

    series = lax.all_to_all(series, "gy", 0, 0, tiled=True)
    own = spectra_in.shape[2]
    rows = pl.cdiv(STEPS * own // 128, ngx)
    partial = call(lambda *refs: project_kernel(tx, ty, nz, own, *refs), shape(ngx * rows, 128), name="project")(series, angles)
    partial = lax.all_to_all(partial, "gx", 0, 0, tiled=True).reshape(ngx, rows * 128)
    total = call(sum_kernel, shape(ngx, rows * 128), name="total")(partial)
    traces = lax.all_to_all(total.reshape(ngx * rows, 128), "gx", 0, 0, tiled=True)
    scale = float(slot_cell.shape[0] * ngx * ngy) ** -0.5
    bins = spectra_in.shape[1] * ngx
    spectra = call(lambda *refs: spectra_kernel(scale, bins, *refs), shape(*spectra_in.shape), name="spectra")(traces, spectra_in)
    return current, before, spectra


def solution(mesh):
    return jax.shard_map(
        body,
        mesh=mesh,
        in_specs=(
            P("gx", "gy", None),
            P("gx", "gy", None),
            P("gx", "gy", None),
            P(("gx", "gy")),
            P(),
            P(None, "gx", "gy"),
        ),
        out_specs=(P("gx", "gy", None), P("gx", "gy", None), P(None, "gx", "gy")),
        check_vma=False,
    )
```

time: 679 us -> 160 us (0.24)
  waiting for transfers between devices: 218 us -> 28.7 us
  starting transfers between devices: 225 us -> 43.3 us
  blocking collectives: 156 us -> 69.1 us
  local copies, waits for them, and re-layouts: 27.2 us -> 3.71 us
  matrix products: 21.7 us -> 0 us
  between operations: 14.3 us -> 0.81 us
  Pallas kernels: 0 us -> 12.9 us
  other arithmetic: 7.86 us -> 0.23 us
    ppermute x68 -> x12, starting transfers between devices: 225 us -> 43.3 us  [the longest x6 22.1 us: swap(): return (lax.ppermute(v_a, axis, even_odd), got_b)]
    psum x1 -> x0, blocking collectives: 156 us -> none  [body(): traces = lax.psum(trace_block, 'gx') / jnp.sqrt(jnp.float32(sample_total))]
    reduce_scatter x1 -> x0, waiting for transfers between devices: 129 us -> none  [body(): lax.psum_scatter(project(angles, coords, series_g, series_p), 'gy', scatt...]
    all_to_all x0 -> x3, blocking collectives: none -> 69.1 us  [the longest x1 28.5 us: body(): lax.all_to_all(partial, 'gx', 0, 0, tiled=True).reshape(ngx, rows * 128)]
    ppermute x68 -> x12, waiting for transfers between devices: 88.8 us -> 28.7 us  [the longest x6 21.2 us: swap(): got_b = lax.ppermute(v_b, axis, odd_even)]
    gather x32 -> x0, local copies, waits for them, and re-layouts: 24.7 us -> none  [the longest x16 12.4 us: sample_cells(): cell_value = flat_field[safe_cell]]
    dot_general x4 -> x0, matrix products: 21.7 us -> none  [the longest x1 11.9 us: project(): jnp.einsum('os,ts->ot', unit_z[:, None] * jnp.sin(phases), series_p, prec...]
    pallas_call x0 -> x8, Pallas kernels: none -> 12.9 us  [the longest x1 3.8 us: body(): call(window('first'), [shape(2 * tx, *thin[1:]), part, shape(*wide), shap...]
  transfers between devices with their start and end apart: 69 -> 12, of which waited for: 34 -> 6; matrix products, arithmetic and copies ran while one was open for 0% -> 0% of each run, Pallas kernels for 0% -> 0%
where the time goes in v2:
time: 160 us; the launch traced here: 159 us
  blocking collectives  69.1 us (43%)
  starting transfers between devices  43.3 us (27%)
  waiting for transfers between devices  28.7 us (18%)
  Pallas kernels  12.9 us (8%)
  local copies, waits for them, and re-layouts  3.71 us (2%)
    all_to_all x1, blocking collectives, body(): lax.all_to_all(partial, 'gx', 0, 0, tiled=True).reshape(ngx, rows * 128)  28.5 us
    all_to_all x1, blocking collectives, body(): series = lax.all_to_all(series, 'gy', 0, 0, tiled=True)  26.1 us
    ppermute x6, starting transfers between devices, swap(): return (lax.ppermute(v_a, axis, even_odd), got_b)  22.1 us
    ppermute x6, starting transfers between devices, swap(): got_b = lax.ppermute(v_b, axis, odd_even)  21.3 us
    ppermute x6, waiting for transfers between devices, swap(): got_b = lax.ppermute(v_b, axis, odd_even)  21.2 us
    all_to_all x1, blocking collectives, body(): lax.all_to_all(total.reshape(ngx * rows, 128), 'gx', 0, 0, tiled=True)  14.5 us
    ppermute x6, waiting for transfers between devices, swap(): return (lax.ppermute(v_a, axis, even_odd), got_b)  7.49 us
    pallas_call x1, Pallas kernels, body(): call(window('first'), [shape(2 * tx, *thin[1:]), part, shape(*wide), shap...  3.8 us
  transfers between devices with their start and end apart: 12, of which 6 were waited for; matrix products, arithmetic and copies ran while one was open for 0% of the time, Pallas kernels for 0%

profile of v2, /device:TPU:1, one launch (start us, length us, event | category | flops | bytes accessed | tf_op | source)
XLA Modules:
  0.0 158.9 jit_solution(18333327422092864996)
XLA Ops:
  3.5 5.0 %collective-permute-start = (f32[12,8,384]{2,1,0:T(8,128)S(1)}, f32[12,8,384]{2,1,0:T(8,128)S(1)}, u32[]{:S(2)}, u32[]{:S(2)}) collective-permute-start(f32[12,8,384]{2,1,0:T(8,128)S(1)} %get-tuple-element.22), channel_id=1, source_target_pairs={{0,1},{1,0},{2,3},{3,2},{4,5},{5,4},{6,7},{7,6},{8,9},{9,8},{10,11... | collective-permute-start | bytes 442376 | tf_op jit(solution)/shard_map/ppermute | solution.py:212
  9.3 5.0 %collective-permute-done = f32[12,8,384]{2,1,0:T(8,128)S(1)} collective-permute-done((f32[12,8,384]{2,1,0:T(8,128)S(1)}, f32[12,8,384]{2,1,0:T(8,128)S(1)}, u32[]{:S(2)}, u32[]{:S(2)}) %collective-permute-start) | collective-permute-done | bytes 147488 | tf_op jit(solution)/shard_map/ppermute | solution.py:212
  14.4 6.2 %collective-permute-start.3 = (f32[12,48,384]{2,1,0:T(8,128)S(1)}, f32[12,48,384]{2,1,0:T(8,128)S(1)}, u32[]{:S(2)}, u32[]{:S(2)}) collective-permute-start(f32[12,48,384]{2,1,0:T(8,128)S(1)} %pad_maximum_fusion.refs_0_), channel_id=1, source_target_pairs={{16,32},{32,16},{48,64},{64,48},{80,96},{96,80},{112,128},{128,112... | collective-permute-start | bytes 2654216 | tf_op jit(solution)/shard_map/ppermute | solution.py:211
  20.6 4.1 %collective-permute-start.2 = (f32[12,48,384]{2,1,0:T(8,128)S(1)}, f32[12,48,384]{2,1,0:T(8,128)S(1)}, u32[]{:S(2)}, u32[]{:S(2)}) collective-permute-start(f32[12,48,384]{2,1,0:T(8,128)S(1)} %pad_maximum_fusion.refs_0_), channel_id=1, source_target_pairs={{0,16},{16,0},{32,48},{48,32},{64,80},{80,64},{96,112},{112,96},{1... | collective-permute-start | bytes 2654216 | tf_op jit(solution)/shard_map/ppermute | solution.py:212
  24.8 6.5 %collective-permute-done.3.refs_2_ = f32[12,48,384]{2,1,0:T(8,128)S(1)} collective-permute-done((f32[12,48,384]{2,1,0:T(8,128)S(1)}, f32[12,48,384]{2,1,0:T(8,128)S(1)}, u32[]{:S(2)}, u32[]{:S(2)}) %collective-permute-start.3) | collective-permute-done | bytes 884768 | tf_op jit(solution)/shard_map/ppermute | solution.py:211
  32.2 3.8 %window_first.1 = (f32[8,40,384]{2,1,0:T(8,128)S(1)}, f32[4,128]{1,0:T(4,128)S(1)}, f32[12,48,384]{2,1,0:T(8,128)S(1)}, f32[12,48,384]{2,1,0:T(8,128)S(1)}, f32[...) custom-call(f32[12,48,384]{2,1,0:T(8,128)S(1)} %pad_maximum_fusion.refs_0_, ...), custom_call_target="tpu_custom_call" | custom-call | tf_op jit(solution)/shard_map/window_first/pallas_call | solution.py:237
  36.0 3.6 %collective-permute-start.5 = (f32[8,40,384]{2,1,0:T(8,128)S(1)}, f32[8,40,384]{2,1,0:T(8,128)S(1)}, u32[]{:S(2)}, u32[]{:S(2)}) collective-permute-start(f32[8,40,384]{2,1,0:T(8,128)S(1)} %get-tuple-element.24.refs_0_), channel_id=1, source_target_pairs={{16,32},{32,16},{48,64},{64,48},{80,96},{96,80},{112,128},{128,112... | collective-permute-start | bytes 1474568 | tf_op jit(solution)/shard_map/ppermute | solution.py:211
  39.7 1.9 %collective-permute-start.4 = (f32[8,40,384]{2,1,0:T(8,128)S(1)}, f32[8,40,384]{2,1,0:T(8,128)S(1)}, u32[]{:S(2)}, u32[]{:S(2)}) collective-permute-start(f32[8,40,384]{2,1,0:T(8,128)S(1)} %get-tuple-element.24.refs_0_), channel_id=1, source_target_pairs={{0,16},{16,0},{32,48},{48,32},{64,80},{80,64},{96,112},{112,96},{1... | collective-permute-start | bytes 1474568 | tf_op jit(solution)/shard_map/ppermute | solution.py:212
  41.6 4.6 %collective-permute-done.5.refs_2_ = f32[8,40,384]{2,1,0:T(8,128)S(1)} collective-permute-done((f32[8,40,384]{2,1,0:T(8,128)S(1)}, f32[8,40,384]{2,1,0:T(8,128)S(1)}, u32[]{:S(2)}, u32[]{:S(2)}) %collective-permute-start.5) | collective-permute-done | bytes 491552 | tf_op jit(solution)/shard_map/ppermute | solution.py:211
  46.2 1.9 %window_inner.1 = (f32[8,32,384]{2,1,0:T(8,128)S(1)}, f32[8,8,384]{2,1,0:T(8,128)S(1)}, f32[8,8,384]{2,1,0:T(8,128)S(1)}, f32[4,128]{1,0:T(4,128)S(1)}) custom-call(f32[8,40,384]{2,1,0:T(8,128)S(1)} %get-tuple-element.24.refs_0_, f32[8,40,384]{2,1,0:T(8,128)S(1)} %collective-permute-done.4.refs_1_, f32[8,40,384]{2,1,0:T(8,128)S(1)} %collective-permute-done.5.refs_2_, ...), custom_call_target="tpu_custom_call" | custom-call | tf_op jit(solution)/shard_map/window_inner/pallas_call | solution.py:243
  48.1 7.1 %collective-permute-start.6 = (f32[8,8,384]{2,1,0:T(8,128)S(1)}, f32[8,8,384]{2,1,0:T(8,128)S(1)}, u32[]{:S(2)}, u32[]{:S(2)}) collective-permute-start(f32[8,8,384]{2,1,0:T(8,128)S(1)} %get-tuple-element.28), channel_id=1, source_target_pairs={{0,1},{1,0},{2,3},{3,2},{4,5},{5,4},{6,7},{7,6},{8,9},{9,8},{10,11... | collective-permute-start | bytes 294920 | tf_op jit(solution)/shard_map/ppermute | solution.py:212
  55.9 2.5 %collective-permute-done.6 = f32[8,8,384]{2,1,0:T(8,128)S(1)} collective-permute-done((f32[8,8,384]{2,1,0:T(8,128)S(1)}, f32[8,8,384]{2,1,0:T(8,128)S(1)}, u32[]{:S(2)}, u32[]{:S(2)}) %collective-permute-start.6) | collective-permute-done | bytes 98336 | tf_op jit(solution)/shard_map/ppermute | solution.py:212
  58.4 6.4 %collective-permute-start.9 = (f32[8,48,384]{2,1,0:T(8,128)S(1)}, f32[8,48,384]{2,1,0:T(8,128)S(1)}, u32[]{:S(2)}, u32[]{:S(2)}) collective-permute-start(f32[8,48,384]{2,1,0:T(8,128)S(1)} %pad_maximum_fusion.1.refs_0_), channel_id=1, source_target_pairs={{16,32},{32,16},{48,64},{64,48},{80,96},{96,80},{112,128},{128,112... | collective-permute-start | bytes 1769480 | tf_op jit(solution)/shard_map/ppermute | solution.py:211
  64.9 1.9 %collective-permute-start.8 = (f32[8,48,384]{2,1,0:T(8,128)S(1)}, f32[8,48,384]{2,1,0:T(8,128)S(1)}, u32[]{:S(2)}, u32[]{:S(2)}) collective-permute-start(f32[8,48,384]{2,1,0:T(8,128)S(1)} %pad_maximum_fusion.1.refs_0_), channel_id=1, source_target_pairs={{0,16},{16,0},{32,48},{48,32},{64,80},{80,64},{96,112},{112,96},{1... | collective-permute-start | bytes 1769480 | tf_op jit(solution)/shard_map/ppermute | solution.py:212
  66.8 5.6 %collective-permute-done.9.refs_2_ = f32[8,48,384]{2,1,0:T(8,128)S(1)} collective-permute-done((f32[8,48,384]{2,1,0:T(8,128)S(1)}, f32[8,48,384]{2,1,0:T(8,128)S(1)}, u32[]{:S(2)}, u32[]{:S(2)}) %collective-permute-start.9) | collective-permute-done | bytes 589856 | tf_op jit(solution)/shard_map/ppermute | solution.py:211
  72.4 2.1 %window_wide.1 = (f32[8,40,384]{2,1,0:T(8,128)S(1)}, f32[4,128]{1,0:T(4,128)S(1)}) custom-call(f32[8,48,384]{2,1,0:T(8,128)S(1)} %pad_maximum_fusion.1.refs_0_, f32[8,48,384]{2,1,0:T(8,128)S(1)} %collective-permute-done.8.refs_1_, f32[8,48,384]{2,1,0:T(8,128)S(1)} %collective-permute-done.9.refs_2_, s32[1,128]{1,0:T(1,128)S(1)} %add_bitcast_fusion.refs_3_, ...), custom_call_target="tpu_custom_call" | custom-call | tf_op jit(solution)/shard_map/window_wide/pallas_call | solution.py:247
  74.5 3.6 %collective-permute-start.11 = (f32[8,40,384]{2,1,0:T(8,128)S(1)}, f32[8,40,384]{2,1,0:T(8,128)S(1)}, u32[]{:S(2)}, u32[]{:S(2)}) collective-permute-start(f32[8,40,384]{2,1,0:T(8,128)S(1)} %get-tuple-element.32.refs_0_), channel_id=1, source_target_pairs={{16,32},{32,16},{48,64},{64,48},{80,96},{96,80},{112,128},{128,112... | collective-permute-start | bytes 1474568 | tf_op jit(solution)/shard_map/ppermute | solution.py:211
  78.2 1.9 %collective-permute-start.10 = (f32[8,40,384]{2,1,0:T(8,128)S(1)}, f32[8,40,384]{2,1,0:T(8,128)S(1)}, u32[]{:S(2)}, u32[]{:S(2)}) collective-permute-start(f32[8,40,384]{2,1,0:T(8,128)S(1)} %get-tuple-element.32.refs_0_), channel_id=1, source_target_pairs={{0,16},{16,0},{32,48},{48,32},{64,80},{80,64},{96,112},{112,96},{1... | collective-permute-start | bytes 1474568 | tf_op jit(solution)/shard_map/ppermute | solution.py:212
  80.1 4.6 %collective-permute-done.11.refs_2_ = f32[8,40,384]{2,1,0:T(8,128)S(1)} collective-permute-done((f32[8,40,384]{2,1,0:T(8,128)S(1)}, f32[8,40,384]{2,1,0:T(8,128)S(1)}, u32[]{:S(2)}, u32[]{:S(2)}) %collective-permute-start.11) | collective-permute-done | bytes 491552 | tf_op jit(solution)/shard_map/ppermute | solution.py:211
  84.7 2.4 %window_last.1 = (f32[4,32,384]{2,1,0:T(8,128)}, f32[4,32,384]{2,1,0:T(8,128)}, f32[16,24,128]{2,1,0:T(8,128)S(1)}) custom-call(f32[8,40,384]{2,1,0:T(8,128)S(1)} %get-tuple-element.32.refs_0_, f32[8,40,384]{2,1,0:T(8,128)S(1)} %collective-permute-done.10.refs_1_, f32[8,40,384]{2,1,0:T(8,128)S(1)} %collective-permute-done.11.refs_2_, ...), custom_call_target="tpu_custom_call" | custom-call | tf_op jit(solution)/shard_map/window_last/pallas_call | solution.py:250
  87.1 26.1 %all_to_all.27.refs_0_ = f32[16,24,128]{2,1,0:T(8,128)S(1)} all-to-all(f32[16,24,128]{2,1,0:T(8,128)S(1)} %get-tuple-element.38), channel_id=1, replica_groups=mesh['gx'=48,'gy'=16] {'gy'}, dimensions={0} | all-to-all | bytes 393216 | tf_op jit(solution)/shard_map/all_to_all | solution.py:254
  113.2 1.8 %project.1 = f32[48,128]{1,0:T(8,128)S(1)} custom-call(f32[16,24,128]{2,1,0:T(8,128)S(1)} %all_to_all.27.refs_0_, f32[2,4096]{1,0:T(2,128)S(1)} %copy-done.3), custom_call_target="tpu_custom_call" | custom-call | tf_op jit(solution)/shard_map/project/pallas_call | solution.py:257
  115.0 28.5 %all_to_all.28 = f32[48,1,128]{2,1,0:T(1,128)S(1)} all-to-all(f32[48,1,128]{2,1,0:T(1,128)S(1)} %bitcast.13), channel_id=1, replica_groups=mesh['gx'=48,'gy'=16] {'gx'}, dimensions={0} | all-to-all | bytes 49152 | tf_op jit(solution)/shard_map/all_to_all | solution.py:258
  143.6 14.5 %all_to_all.29 = f32[48,1,128]{2,1,0:T(1,128)S(1)} all-to-all(f32[48,1,128]{2,1,0:T(1,128)S(1)} %bitcast.11), channel_id=1, replica_groups=mesh['gx'=48,'gy'=16] {'gx'}, dimensions={0} | all-to-all | bytes 49152 | tf_op jit(solution)/shard_map/all_to_all | solution.py:260
  (30 shorter events, 6.2 us)
Async XLA Ops:
  0.6 0.9 copy-start
  1.6 0.9 copy-start.1
  2.5 0.9 copy-start.2
  3.5 10.7 %collective-permute-start = (f32[12,8,384]{2,1,0:T(8,128)S(1)}, f32[12,8,384]{2,1,0:T(8,128)S(1)}, u32[]{:S(2)}, u32[]{:S(2)}) collective-permute-start(f32[12,8,384]{2,1,0:T(8,128)S(1)} %get-tuple-element.22), channel_id=1, source_target_pairs={{0,1},{1,0},{2,3},{3,2},{4,5},{5,4},{6,7},{7,6},{8,9},{9,8},{10,11... | collective-permute-start | bytes 442376 | tf_op jit(solution)/shard_map/ppermute | solution.py:212
  8.6 5.7 %collective-permute-start.1 = (f32[12,8,384]{2,1,0:T(8,128)S(1)}, f32[12,8,384]{2,1,0:T(8,128)S(1)}, u32[]{:S(2)}, u32[]{:S(2)}) collective-permute-start(f32[12,8,384]{2,1,0:T(8,128)S(1)} %get-tuple-element.23), channel_id=1, source_target_pairs={{1,2},{2,1},{3,4},{4,3},{5,6},{6,5},{7,8},{8,7},{9,10},{10,9},{11,... | collective-permute-start | bytes 442376 | tf_op jit(solution)/shard_map/ppermute | solution.py:211
  14.3 10.4 %copy-start.6 = (s32[64]{0:T(128)S(1)}, s32[64]{0:T(128)}, u32[]{:S(2)}) copy-start(s32[64]{0:T(128)} %param.9) | copy-start | bytes 772
  14.4 16.9 %collective-permute-start.3 = (f32[12,48,384]{2,1,0:T(8,128)S(1)}, f32[12,48,384]{2,1,0:T(8,128)S(1)}, u32[]{:S(2)}, u32[]{:S(2)}) collective-permute-start(f32[12,48,384]{2,1,0:T(8,128)S(1)} %pad_maximum_fusion.refs_0_), channel_id=1, source_target_pairs={{16,32},{32,16},{48,64},{64,48},{80,96},{96,80},{112,128},{128,112... | collective-permute-start | bytes 2654216 | tf_op jit(solution)/shard_map/ppermute | solution.py:211
  20.6 10.7 %collective-permute-start.2 = (f32[12,48,384]{2,1,0:T(8,128)S(1)}, f32[12,48,384]{2,1,0:T(8,128)S(1)}, u32[]{:S(2)}, u32[]{:S(2)}) collective-permute-start(f32[12,48,384]{2,1,0:T(8,128)S(1)} %pad_maximum_fusion.refs_0_), channel_id=1, source_target_pairs={{0,16},{16,0},{32,48},{48,32},{64,80},{80,64},{96,112},{112,96},{1... | collective-permute-start | bytes 2654216 | tf_op jit(solution)/shard_map/ppermute | solution.py:212
  31.3 0.9 copy-start.5
  36.0 10.1 %collective-permute-start.5 = (f32[8,40,384]{2,1,0:T(8,128)S(1)}, f32[8,40,384]{2,1,0:T(8,128)S(1)}, u32[]{:S(2)}, u32[]{:S(2)}) collective-permute-start(f32[8,40,384]{2,1,0:T(8,128)S(1)} %get-tuple-element.24.refs_0_), channel_id=1, source_target_pairs={{16,32},{32,16},{48,64},{64,48},{80,96},{96,80},{112,128},{128,112... | collective-permute-start | bytes 1474568 | tf_op jit(solution)/shard_map/ppermute | solution.py:211
  39.7 6.5 %collective-permute-start.4 = (f32[8,40,384]{2,1,0:T(8,128)S(1)}, f32[8,40,384]{2,1,0:T(8,128)S(1)}, u32[]{:S(2)}, u32[]{:S(2)}) collective-permute-start(f32[8,40,384]{2,1,0:T(8,128)S(1)} %get-tuple-element.24.refs_0_), channel_id=1, source_target_pairs={{0,16},{16,0},{32,48},{48,32},{64,80},{80,64},{96,112},{112,96},{1... | collective-permute-start | bytes 1474568 | tf_op jit(solution)/shard_map/ppermute | solution.py:212
  48.1 10.3 %collective-permute-start.6 = (f32[8,8,384]{2,1,0:T(8,128)S(1)}, f32[8,8,384]{2,1,0:T(8,128)S(1)}, u32[]{:S(2)}, u32[]{:S(2)}) collective-permute-start(f32[8,8,384]{2,1,0:T(8,128)S(1)} %get-tuple-element.28), channel_id=1, source_target_pairs={{0,1},{1,0},{2,3},{3,2},{4,5},{5,4},{6,7},{7,6},{8,9},{9,8},{10,11... | collective-permute-start | bytes 294920 | tf_op jit(solution)/shard_map/ppermute | solution.py:212
  55.2 3.2 %collective-permute-start.7 = (f32[8,8,384]{2,1,0:T(8,128)S(1)}, f32[8,8,384]{2,1,0:T(8,128)S(1)}, u32[]{:S(2)}, u32[]{:S(2)}) collective-permute-start(f32[8,8,384]{2,1,0:T(8,128)S(1)} %get-tuple-element.29), channel_id=1, source_target_pairs={{1,2},{2,1},{3,4},{4,3},{5,6},{6,5},{7,8},{8,7},{9,10},{10,9},{11,... | collective-permute-start | bytes 294920 | tf_op jit(solution)/shard_map/ppermute | solution.py:211
  58.4 14.0 %collective-permute-start.9 = (f32[8,48,384]{2,1,0:T(8,128)S(1)}, f32[8,48,384]{2,1,0:T(8,128)S(1)}, u32[]{:S(2)}, u32[]{:S(2)}) collective-permute-start(f32[8,48,384]{2,1,0:T(8,128)S(1)} %pad_maximum_fusion.1.refs_0_), channel_id=1, source_target_pairs={{16,32},{32,16},{48,64},{64,48},{80,96},{96,80},{112,128},{128,112... | collective-permute-start | bytes 1769480 | tf_op jit(solution)/shard_map/ppermute | solution.py:211
  64.9 7.6 %collective-permute-start.8 = (f32[8,48,384]{2,1,0:T(8,128)S(1)}, f32[8,48,384]{2,1,0:T(8,128)S(1)}, u32[]{:S(2)}, u32[]{:S(2)}) collective-permute-start(f32[8,48,384]{2,1,0:T(8,128)S(1)} %pad_maximum_fusion.1.refs_0_), channel_id=1, source_target_pairs={{0,16},{16,0},{32,48},{48,32},{64,80},{80,64},{96,112},{112,96},{1... | collective-permute-start | bytes 1769480 | tf_op jit(solution)/shard_map/ppermute | solution.py:212
  74.5 10.1 %collective-permute-start.11 = (f32[8,40,384]{2,1,0:T(8,128)S(1)}, f32[8,40,384]{2,1,0:T(8,128)S(1)}, u32[]{:S(2)}, u32[]{:S(2)}) collective-permute-start(f32[8,40,384]{2,1,0:T(8,128)S(1)} %get-tuple-element.32.refs_0_), channel_id=1, source_target_pairs={{16,32},{32,16},{48,64},{64,48},{80,96},{96,80},{112,128},{128,112... | collective-permute-start | bytes 1474568 | tf_op jit(solution)/shard_map/ppermute | solution.py:211
  78.2 6.5 %collective-permute-start.10 = (f32[8,40,384]{2,1,0:T(8,128)S(1)}, f32[8,40,384]{2,1,0:T(8,128)S(1)}, u32[]{:S(2)}, u32[]{:S(2)}) collective-permute-start(f32[8,40,384]{2,1,0:T(8,128)S(1)} %get-tuple-element.32.refs_0_), channel_id=1, source_target_pairs={{0,16},{16,0},{32,48},{48,32},{64,80},{80,64},{96,112},{112,96},{1... | collective-permute-start | bytes 1474568 | tf_op jit(solution)/shard_map/ppermute | solution.py:212
  87.1 26.1 %copy-start.3 = (f32[2,4096]{1,0:T(2,128)S(1)}, f32[2,4096]{1,0:T(2,128)}, u32[]{:S(2)}) copy-start(f32[2,4096]{1,0:T(2,128)} %refs_1_.2) | copy-start | bytes 98308
  143.6 14.5 %copy-start.4 = (f32[2,8,256]{2,1,0:T(8,128)S(1)}, f32[2,8,256]{2,1,0:T(8,128)}, u32[]{:S(2)}) copy-start(f32[2,8,256]{2,1,0:T(8,128)} %refs_1_.3) | copy-start | bytes 49156

commit v3 on v2

--- a/solution.py
+++ b/solution.py
@@ -15,13 +15,15 @@
 TURN = 6.283185307179586
 
 
-def call(kernel, outs, scratch=(), name=None):
+def call(kernel, outs, scratch=(), name=None, specs=None):
+    more = {} if specs is None else {"in_specs": specs}
     return pl.pallas_call(
         kernel,
         out_shape=outs,
         scratch_shapes=list(scratch),
-        compiler_params=pltpu.CompilerParams(vmem_limit_bytes=48 * 1024 * 1024),
+        compiler_params=pltpu.CompilerParams(vmem_limit_bytes=16 * 1024 * 1024),
         name=name,
+        **more,
     )
 
 
@@ -32,13 +34,67 @@
     return at(jnp.where(even, top, bottom)), at(jnp.where(even, bottom, top))
 
 
-def prepare_kernel(cur_ref, bef_ref, mat_ref, state_ref, a_ref, b_ref):
+def prepare_kernel(cur_hbm, bef_hbm, mat_hbm, state_ref, a_ref, b_ref, cur_ref, bef_ref, mat_ref, sems):
     tx, ty, _ = cur_ref.shape
+    pairs = ((mat_hbm, mat_ref), (cur_hbm, cur_ref), (bef_hbm, bef_ref))
+    copies = [pltpu.make_async_copy(src, dst, sems.at[k]) for k, (src, dst) in enumerate(pairs)]
+    for copy in copies:
+        copy.start()
+    copies[0].wait()
     mat = mat_ref[...]
+    state_ref[2 * tx :] = jnp.where(mat == 1, 0.0, jnp.where(mat == 2, F32(1.0) / F32(1.5), F32(1.0)))
+    copies[1].wait()
     state_ref[0:tx] = jnp.where(mat == 1, 0.0, cur_ref[...])
+    copies[2].wait()
     state_ref[tx : 2 * tx] = jnp.where(mat == 1, 0.0, bef_ref[...])
-    state_ref[2 * tx :] = jnp.where(mat == 1, 0.0, jnp.where(mat == 2, F32(1.0) / F32(1.5), F32(1.0)))
     a_ref[...], b_ref[...] = edges(state_ref, ty)
+
+
+def message_tiles(fields, tx, ty, reach):
+    tiles = []
+    for field in range(fields):
+        late = 1 if field == 1 else 0
+        for d in range(1, W + 1 - late):
+            tiles += [(field, d, 8 * k, False) for k in range(ty // 8)]
+            rows = reach - d - late
+            if rows > 4:
+                tiles += [(field, d, ty, False), (field, d, ty + 8, False)]
+            elif rows > 0:
+                tiles.append((field, d, ty, True))
+    return tiles
+
+
+def write_messages(own, a_ref, b_ref, fields, tx, ty, reach):
+    odd = lax.axis_index("gx") % 2
+    wide = own.shape[1] == ty + 16
+    low = lax.broadcasted_iota(jnp.int32, (8, own.shape[2]), 0) < 4
+    for k, (field, d, row, packed) in enumerate(message_tiles(fields, tx, ty, reach)):
+        for ref, below in ((a_ref, odd), (b_ref, 1 - odd)):
+            plane = field * tx + below * (d - 1) + (1 - below) * (tx - d)
+            tile = own[plane, row : row + 8]
+            if packed and wide:
+                tile = jnp.where(low, tile, own[plane, row + 8 : row + 16])
+            ref[k] = tile
+
+
+def read_messages(targets, a_ref, b_ref, tx, ty, reach):
+    odd = lax.axis_index("gx") % 2
+    wide = targets[0].shape[1] == ty + 16
+    for k, (field, d, row, packed) in enumerate(message_tiles(len(targets), tx, ty, reach)):
+        for ref, below in ((a_ref, odd), (b_ref, 1 - odd)):
+            plane = below * (tx - d) + (1 - below) * (2 * tx + d - 1)
+            tile = ref[k]
+            targets[field][plane, row : row + 8] = tile
+            if packed and wide:
+                targets[field][plane, row + 8 : row + 16] = tile
+
+
+def join_kernel(fields, tx, ty, state_ref, y_a, y_b, own_ref, a_ref, b_ref):
+    odd = lax.axis_index("gy") % 2
+    own_ref[:, 0:ty] = state_ref[...]
+    own_ref[:, pl.ds(pl.multiple_of(ty + 8 * odd, 8), 8)] = y_a[...]
+    own_ref[:, pl.ds(pl.multiple_of(ty + 8 - 8 * odd, 8), 8)] = y_b[...]
+    write_messages(own_ref, a_ref, b_ref, fields, tx, ty, 2 * W)
 
 
 def shifted(v, axis, by, edge):
@@ -74,20 +130,17 @@
     if kind == "last":
         out_cur, out_bef, series_ref = take(3)
     else:
-        state_ref, *rest = take({"first": 1, "inner": 3, "wide": 1}[kind])
+        state_ref, *rest = take(3)
         (sample_ref,) = take(1)
     if kind == "first":
         gain_ref, count_ref, gain4_ref, count4_ref = take(4)
     one, two = take(2)
     nz = own.shape[2]
-    odd = lax.axis_index("gx") % 2
-    at_a = (1 - odd) * 2 * tx
-    at_b = odd * 2 * tx
-    for at, tiles in ((tx, own), (at_a, x_a), (at_b, x_b)):
-        one[pl.ds(at, tx)] = tiles[0:tx]
-        two[pl.ds(at, tx)] = tiles[tx : 2 * tx]
-        if kind == "first":
-            gain_ref[pl.ds(at, tx)] = tiles[2 * tx :]
+    targets = [one, two] + ([gain_ref] if kind == "first" else [])
+    for field, target in enumerate(targets):
+        target[tx : 2 * tx] = own[field * tx : (field + 1) * tx]
+    reach = 2 * W if kind in ("first", "wide") else W
+    read_messages(targets, x_a, x_b, tx, ty, reach)
     if kind == "first":
         count_ref[...] = jnp.zeros(count_ref.shape, F32)
         opened = lambda i: jnp.where(gain_ref[i] > 0.0, F32(1.0), F32(0.0))
@@ -136,6 +189,7 @@
     else:
         state_ref[0:tx] = narrow(cur[...], ty)
         state_ref[tx:] = narrow(bef[...], ty)
+        write_messages(state_ref, *rest, 2, tx, ty, W)
 
 
 def sin_cos_turns(p):
@@ -178,17 +232,15 @@
         low = (v - high.astype(F32)).astype(BF16)
         dot = lambda a, b: jnp.dot(a, b, preferred_element_type=F32)
         total = total + dot(high, wave_high) + (dot(low, wave_high) + dot(high, wave_low))
-    out_ref[...] = jnp.zeros(out_ref.shape, F32)
-    for k in range(own // 128):
-        out_ref[k * STEPS : (k + 1) * STEPS] = total[:, k * 128 : (k + 1) * 128]
-
-
-def sum_kernel(part_ref, out_ref):
-    total = jnp.sum(part_ref[...], axis=0, keepdims=True)
-    out_ref[...] = jnp.broadcast_to(total, out_ref.shape)
-
-
-def spectra_kernel(scale, bin_total, trace_ref, spec_ref, out_ref):
+    for k in range(out_ref.shape[0]):
+        out_ref[k] = total
+
+
+def total_kernel(part_ref, out_ref):
+    out_ref[...] = jnp.sum(part_ref[...], axis=0)
+
+
+def spectra_kernel(scale, bin_total, trace_ref, other_ref, spec_ref, out_ref):
     bins = spec_ref.shape[1]
     period = 2 * (bin_total + 1)
     bin_of = lax.axis_index("gx") * bins + lax.broadcasted_iota(jnp.int32, (bins, STEPS), 0) + 1
@@ -196,8 +248,7 @@
     turn = (step_of * bin_of).astype(F32)
     turn = turn - period * jnp.floor(turn * (1.0 / period))
     sin_t, cos_t = sin_cos_turns(turn * (1.0 / period))
-    parts = [trace_ref[k * STEPS : (k + 1) * STEPS] for k in range(spec_ref.shape[2] // 128)]
-    traces = jnp.concatenate(parts, axis=1) * F32(scale)
+    traces = (trace_ref[...] + other_ref[...]) * F32(scale)
     dot = lambda a: jnp.dot(a, traces, preferred_element_type=F32, precision=lax.Precision.HIGHEST)
     out_ref[0] = spec_ref[0] + dot(cos_t)
     out_ref[1] = spec_ref[1] - dot(sin_t)
@@ -215,52 +266,60 @@
 def body(pressure, previous, material, slot_cell, angles, spectra_in):
     tx, ty, nz = pressure.shape
     ngx, ngy = lax.axis_size("gx"), lax.axis_size("gy")
-    even_y = lax.axis_index("gy") % 2 == 0
     shape = lambda *s: jax.ShapeDtypeStruct(s, F32)
     window = lambda kind: lambda *refs: window_kernel(kind, tx, ty, *refs)
     wide, thin = (3 * tx, ty + 2 * Y, nz), (3 * tx, ty + 2 * W, nz)
     scratch = lambda s: [pltpu.VMEM(s, F32)] * 2
 
-    def exchange_y(state, a, b):
-        a, b = swap((a, b), "gy")
-        return jnp.concatenate([state, jnp.where(even_y, a, b), jnp.where(even_y, b, a)], axis=1)
-
-    def exchange_x(state):
-        return [state, *swap((state, state), "gx"), cells]
+    def exchange_y(fields, state, a, b):
+        size = shape(len(message_tiles(fields, tx, ty, 2 * W)), 8, nz)
+        return call(
+            lambda *refs: join_kernel(fields, tx, ty, *refs), [shape(fields * tx, *wide[1:]), size, size], name="join"
+        )(state, *swap((a, b), "gy"))
+
+    def exchange_x(own, a, b):
+        return [own, *swap((a, b), "gx"), cells]
 
     cells = jnp.concatenate([slot_cell, slot_cell])[None, :]
-    state, a, b = call(
-        prepare_kernel, [shape(3 * tx, ty, nz), shape(3 * tx, Y, nz), shape(3 * tx, Y, nz)], name="prepare"
-    )(pressure, previous, material)
-    state = exchange_y(state, a, b)
+    tile, edge = (tx, ty, nz), (tx, Y, nz)
+    hbm = pl.BlockSpec(memory_space=pltpu.HBM)
+    state = call(
+        prepare_kernel,
+        [shape(3 * tx, ty, nz), shape(3 * tx, Y, nz), shape(3 * tx, Y, nz)],
+        [pltpu.VMEM(tile, F32), pltpu.VMEM(tile, F32), pltpu.VMEM(tile, jnp.int32), pltpu.SemaphoreType.DMA((3,))],
+        name="prepare",
+        specs=[hbm] * 3,
+    )(*(pltpu.with_memory_space_constraint(v, pltpu.HBM) for v in (pressure, previous, material)))
+    own = exchange_y(3, *state)
     part = shape(W, 128)
-    state, first, gain, count, gain4, count4 = call(
-        window("first"),
-        [shape(2 * tx, *thin[1:]), part, shape(*wide), shape(*wide), shape(*thin), shape(*thin)],
-        scratch(wide),
-        name="window_first",
-    )(*exchange_x(state))
-    state, a, b, second = call(
+    message = shape(len(message_tiles(2, tx, ty, W)), 8, nz)
+    between = [shape(2 * tx, *thin[1:]), message, message, part]
+    *own, first, gain, count, gain4, count4 = call(
+        window("first"), between + [shape(*wide), shape(*wide), shape(*thin), shape(*thin)], scratch(wide), name="window_first"
+    )(*exchange_x(*own))
+    *state, second = call(
         window("inner"), [shape(2 * tx, ty, nz), shape(2 * tx, Y, nz), shape(2 * tx, Y, nz), part], scratch(thin), name="window_inner"
-    )(*exchange_x(state), gain4, count4)
-    state = exchange_y(state, a, b)
-    state, third = call(window("wide"), [shape(2 * tx, *thin[1:]), part], scratch(wide), name="window_wide")(
-        *exchange_x(state), gain, count
-    )
+    )(*exchange_x(*own), gain4, count4)
+    own = exchange_y(2, *state)
+    *own, third = call(window("wide"), between, scratch(wide), name="window_wide")(*exchange_x(*own), gain, count)
     current, before, series = call(
-        window("last"), [shape(tx, ty, nz), shape(tx, ty, nz), shape(ngy, STEPS + 8, 128)], scratch(thin), name="window_last"
-    )(*exchange_x(state), gain4, count4, first, second, third)
+        window("last"), [shape(*tile), shape(*tile), shape(ngy, STEPS + 8, 128)], scratch(thin), name="window_last"
+    )(*exchange_x(*own), gain4, count4, first, second, third)
 
     series = lax.all_to_all(series, "gy", 0, 0, tiled=True)
     own = spectra_in.shape[2]
-    rows = pl.cdiv(STEPS * own // 128, ngx)
-    partial = call(lambda *refs: project_kernel(tx, ty, nz, own, *refs), shape(ngx * rows, 128), name="project")(series, angles)
-    partial = lax.all_to_all(partial, "gx", 0, 0, tiled=True).reshape(ngx, rows * 128)
-    total = call(sum_kernel, shape(ngx, rows * 128), name="total")(partial)
-    traces = lax.all_to_all(total.reshape(ngx * rows, 128), "gx", 0, 0, tiled=True)
+    depth = ngx // 4
+    groups = [[half * 2 * depth + 2 * z + core for z in range(depth)] for half in range(2) for core in range(2)]
+    partial = call(lambda *refs: project_kernel(tx, ty, nz, own, *refs), shape(depth, STEPS, own), name="project")(series, angles)
+    partial = lax.all_to_all(partial, "gx", 0, 0, tiled=True, axis_index_groups=groups)
+    traces = call(total_kernel, shape(STEPS, own), name="total")(partial)
+    traces = traces + lax.ppermute(traces, "gx", [(i, i ^ 1) for i in range(ngx)])
+    other = lax.ppermute(traces, "gx", [(i, (i + 2 * depth) % ngx) for i in range(ngx)])
     scale = float(slot_cell.shape[0] * ngx * ngy) ** -0.5
     bins = spectra_in.shape[1] * ngx
-    spectra = call(lambda *refs: spectra_kernel(scale, bins, *refs), shape(*spectra_in.shape), name="spectra")(traces, spectra_in)
+    spectra = call(lambda *refs: spectra_kernel(scale, bins, *refs), shape(*spectra_in.shape), name="spectra")(
+        traces, other, spectra_in
+    )
     return current, before, spectra
 
 

time: 160 us -> 158 us (0.988)
  blocking collectives: 69.1 us -> 54.7 us
  waiting for transfers between devices: 28.7 us -> 40.2 us
  starting transfers between devices: 43.3 us -> 47.8 us
  local copies, waits for them, and re-layouts: 3.71 us -> 0.02 us
    all_to_all x2 -> x1, blocking collectives: 43 us -> 31 us  [body(): lax.all_to_all(partial, 'gx', 0, 0, tiled=True, axis_index_groups=groups)]
    ppermute x6, waiting for transfers between devices: 21.2 us -> 30.5 us  [swap(): got_b = lax.ppermute(v_b, axis, odd_even)]
    ppermute x6, starting transfers between devices: 21.3 us -> 13.5 us  [swap(): got_b = lax.ppermute(v_b, axis, odd_even)]
    ppermute x0 -> x2, starting transfers between devices: none -> 6.18 us  [the longest x1 4.28 us: body(): lax.ppermute(traces, 'gx', [(i, i ^ 1) for i in range(ngx)])]
    ppermute x6, starting transfers between devices: 22.1 us -> 28.1 us  [swap(): return (lax.ppermute(v_a, axis, even_odd), got_b)]
    unnamed x14 -> x6, local copies, waits for them, and re-layouts: 3.71 us -> 0.02 us
    ppermute x0 -> x2, waiting for transfers between devices: none -> 3.37 us  [the longest x1 2.55 us: body(): lax.ppermute(traces, 'gx', [(i, (i + 2 * depth) % ngx) for i in range(ngx)])]
    all_to_all x1, blocking collectives: 26.1 us -> 23.8 us  [body(): series = lax.all_to_all(series, 'gy', 0, 0, tiled=True)]
  transfers between devices with their start and end apart: 12 -> 14, of which waited for: 6 -> 8; matrix products, arithmetic and copies ran while one was open for 0% -> 0% of each run, Pallas kernels for 0% -> 0%
where the time goes in v3:
time: 158 us; the launch traced here: 157 us
  blocking collectives  54.7 us (35%)
  starting transfers between devices  47.8 us (30%)
  waiting for transfers between devices  40.2 us (25%)
  Pallas kernels  13.2 us (8%)
    all_to_all x1, blocking collectives, body(): lax.all_to_all(partial, 'gx', 0, 0, tiled=True, axis_index_groups=groups)  31 us
    ppermute x6, waiting for transfers between devices, swap(): got_b = lax.ppermute(v_b, axis, odd_even)  30.5 us
    ppermute x6, starting transfers between devices, swap(): return (lax.ppermute(v_a, axis, even_odd), got_b)  28.1 us
    all_to_all x1, blocking collectives, body(): series = lax.all_to_all(series, 'gy', 0, 0, tiled=True)  23.8 us
    ppermute x6, starting transfers between devices, swap(): got_b = lax.ppermute(v_b, axis, odd_even)  13.5 us
    ppermute x6, waiting for transfers between devices, swap(): return (lax.ppermute(v_a, axis, even_odd), got_b)  6.33 us
    ppermute x1, starting transfers between devices, body(): lax.ppermute(traces, 'gx', [(i, i ^ 1) for i in range(ngx)])  4.28 us
  transfers between devices with their start and end apart: 14, of which 8 were waited for; matrix products, arithmetic and copies ran while one was open for 0% of the time, Pallas kernels for 0%

profile of v3, /device:TPU:1, one launch (start us, length us, event | category | flops | bytes accessed | tf_op | source)
XLA Modules:
  0.0 156.9 jit_solution(5103542377928405364)
XLA Ops:
  1.8 5.0 %collective-permute-start = (f32[12,8,384]{2,1,0:T(8,128)S(1)}, f32[12,8,384]{2,1,0:T(8,128)S(1)}, u32[]{:S(2)}, u32[]{:S(2)}) collective-permute-start(f32[12,8,384]{2,1,0:T(8,128)S(1)} %get-tuple-element.32), channel_id=1, source_target_pairs={{0,1},{1,0},{2,3},{3,2},{4,5},{5,4},{6,7},{7,6},{8,9},{9,8},{10,11... | collective-permute-start | bytes 442376 | tf_op jit(solution)/shard_map/ppermute | solution.py:263
  7.6 5.0 %collective-permute-done.refs_1_ = f32[12,8,384]{2,1,0:T(8,128)S(1)} collective-permute-done((f32[12,8,384]{2,1,0:T(8,128)S(1)}, f32[12,8,384]{2,1,0:T(8,128)S(1)}, u32[]{:S(2)}, u32[]{:S(2)}) %collective-permute-start) | collective-permute-done | bytes 147488 | tf_op jit(solution)/shard_map/ppermute | solution.py:263
  12.7 9.6 %collective-permute-start.2 = (f32[63,8,384]{2,1,0:T(8,128)S(1)}, f32[63,8,384]{2,1,0:T(8,128)S(1)}, u32[]{:S(2)}, u32[]{:S(2)}) collective-permute-start(f32[63,8,384]{2,1,0:T(8,128)S(1)} %get-tuple-element.35), channel_id=1, source_target_pairs={{0,16},{16,0},{32,48},{48,32},{64,80},{80,64},{96,112},{112,96},{1... | collective-permute-start | bytes 2322440 | tf_op jit(solution)/shard_map/ppermute | solution.py:263
  22.4 1.9 %collective-permute-start.3 = (f32[63,8,384]{2,1,0:T(8,128)S(1)}, f32[63,8,384]{2,1,0:T(8,128)S(1)}, u32[]{:S(2)}, u32[]{:S(2)}) collective-permute-start(f32[63,8,384]{2,1,0:T(8,128)S(1)} %get-tuple-element.36), channel_id=1, source_target_pairs={{16,32},{32,16},{48,64},{64,48},{80,96},{96,80},{112,128},{128,112... | collective-permute-start | bytes 2322440 | tf_op jit(solution)/shard_map/ppermute | solution.py:262
  24.4 11.2 %collective-permute-done.3.refs_2_ = f32[63,8,384]{2,1,0:T(8,128)S(1)} collective-permute-done((f32[63,8,384]{2,1,0:T(8,128)S(1)}, f32[63,8,384]{2,1,0:T(8,128)S(1)}, u32[]{:S(2)}, u32[]{:S(2)}) %collective-permute-start.3) | collective-permute-done | bytes 774176 | tf_op jit(solution)/shard_map/ppermute | solution.py:262
  35.6 2.7 %window_first.1 = (f32[8,40,384]{2,1,0:T(8,128)S(1)}, f32[33,8,384]{2,1,0:T(8,128)S(1)}, f32[33,8,384]{2,1,0:T(8,128)S(1)}, f32[4,128]{1,0:T(4,128)S(1)}, f32[12...) custom-call(f32[12,48,384]{2,1,0:T(8,128)S(1)} %get-tuple-element.34, ...), custom_call_target="tpu_custom_call" | custom-call | tf_op jit(solution)/shard_map/window_first/pallas_call | solution.py:297
  38.3 1.9 %collective-permute-start.4 = (f32[33,8,384]{2,1,0:T(8,128)S(1)}, f32[33,8,384]{2,1,0:T(8,128)S(1)}, u32[]{:S(2)}, u32[]{:S(2)}) collective-permute-start(f32[33,8,384]{2,1,0:T(8,128)S(1)} %get-tuple-element.38), channel_id=1, source_target_pairs={{0,16},{16,0},{32,48},{48,32},{64,80},{80,64},{96,112},{112,96},{1... | collective-permute-start | bytes 1216520 | tf_op jit(solution)/shard_map/ppermute | solution.py:263
  40.2 1.9 %collective-permute-start.5 = (f32[33,8,384]{2,1,0:T(8,128)S(1)}, f32[33,8,384]{2,1,0:T(8,128)S(1)}, u32[]{:S(2)}, u32[]{:S(2)}) collective-permute-start(f32[33,8,384]{2,1,0:T(8,128)S(1)} %get-tuple-element.39), channel_id=1, source_target_pairs={{16,32},{32,16},{48,64},{64,48},{80,96},{96,80},{112,128},{128,112... | collective-permute-start | bytes 1216520 | tf_op jit(solution)/shard_map/ppermute | solution.py:262
  42.2 7.3 %collective-permute-done.5.refs_2_ = f32[33,8,384]{2,1,0:T(8,128)S(1)} collective-permute-done((f32[33,8,384]{2,1,0:T(8,128)S(1)}, f32[33,8,384]{2,1,0:T(8,128)S(1)}, u32[]{:S(2)}, u32[]{:S(2)}) %collective-permute-start.5) | collective-permute-done | bytes 405536 | tf_op jit(solution)/shard_map/ppermute | solution.py:262
  49.4 1.9 %window_inner.1 = (f32[8,32,384]{2,1,0:T(8,128)S(1)}, f32[8,8,384]{2,1,0:T(8,128)S(1)}, f32[8,8,384]{2,1,0:T(8,128)S(1)}, f32[4,128]{1,0:T(4,128)S(1)}) custom-call(f32[8,40,384]{2,1,0:T(8,128)S(1)} %get-tuple-element.37.refs_0_, f32[33,8,384]{2,1,0:T(8,128)S(1)} %collective-permute-done.4.refs_1_, f32[33,8,384]{2,1,0:T(8,128)S(1)} %collective-permute-done.5.refs_2_, ...), custom_call_target="tpu_custom_call" | custom-call | tf_op jit(solution)/shard_map/window_inner/pallas_call | solution.py:300
  51.3 7.7 %collective-permute-start.6 = (f32[8,8,384]{2,1,0:T(8,128)S(1)}, f32[8,8,384]{2,1,0:T(8,128)S(1)}, u32[]{:S(2)}, u32[]{:S(2)}) collective-permute-start(f32[8,8,384]{2,1,0:T(8,128)S(1)} %get-tuple-element.43), channel_id=1, source_target_pairs={{0,1},{1,0},{2,3},{3,2},{4,5},{5,4},{6,7},{7,6},{8,9},{9,8},{10,11... | collective-permute-start | bytes 294920 | tf_op jit(solution)/shard_map/ppermute | solution.py:263
  61.1 1.9 %collective-permute-start.8 = (f32[40,8,384]{2,1,0:T(8,128)S(1)}, f32[40,8,384]{2,1,0:T(8,128)S(1)}, u32[]{:S(2)}, u32[]{:S(2)}) collective-permute-start(f32[40,8,384]{2,1,0:T(8,128)S(1)} %get-tuple-element.46), channel_id=1, source_target_pairs={{0,16},{16,0},{32,48},{48,32},{64,80},{80,64},{96,112},{112,96},{1... | collective-permute-start | bytes 1474568 | tf_op jit(solution)/shard_map/ppermute | solution.py:263
  63.0 3.7 %collective-permute-start.9 = (f32[40,8,384]{2,1,0:T(8,128)S(1)}, f32[40,8,384]{2,1,0:T(8,128)S(1)}, u32[]{:S(2)}, u32[]{:S(2)}) collective-permute-start(f32[40,8,384]{2,1,0:T(8,128)S(1)} %get-tuple-element.47), channel_id=1, source_target_pairs={{16,32},{32,16},{48,64},{64,48},{80,96},{96,80},{112,128},{128,112... | collective-permute-start | bytes 1474568 | tf_op jit(solution)/shard_map/ppermute | solution.py:262
  66.7 6.5 %collective-permute-done.9.refs_2_ = f32[40,8,384]{2,1,0:T(8,128)S(1)} collective-permute-done((f32[40,8,384]{2,1,0:T(8,128)S(1)}, f32[40,8,384]{2,1,0:T(8,128)S(1)}, u32[]{:S(2)}, u32[]{:S(2)}) %collective-permute-start.9) | collective-permute-done | bytes 491552 | tf_op jit(solution)/shard_map/ppermute | solution.py:262
  73.2 2.1 %window_wide.1 = (f32[8,40,384]{2,1,0:T(8,128)S(1)}, f32[33,8,384]{2,1,0:T(8,128)S(1)}, f32[33,8,384]{2,1,0:T(8,128)S(1)}, f32[4,128]{1,0:T(4,128)S(1)}) custom-call(f32[8,48,384]{2,1,0:T(8,128)S(1)} %get-tuple-element.45.refs_0_, f32[40,8,384]{2,1,0:T(8,128)S(1)} %collective-permute-done.8.refs_1_, f32[40,8,384]{2,1,0:T(8,128)S(1)} %collective-permute-done.9.refs_2_, ...), custom_call_target="tpu_custom_call" | custom-call | tf_op jit(solution)/shard_map/window_wide/pallas_call | solution.py:304
  75.3 1.9 %collective-permute-start.10 = (f32[33,8,384]{2,1,0:T(8,128)S(1)}, f32[33,8,384]{2,1,0:T(8,128)S(1)}, u32[]{:S(2)}, u32[]{:S(2)}) collective-permute-start(f32[33,8,384]{2,1,0:T(8,128)S(1)} %get-tuple-element.51), channel_id=1, source_target_pairs={{0,16},{16,0},{32,48},{48,32},{64,80},{80,64},{96,112},{112,96},{1... | collective-permute-start | bytes 1216520 | tf_op jit(solution)/shard_map/ppermute | solution.py:263
  77.3 4.7 %collective-permute-start.11 = (f32[33,8,384]{2,1,0:T(8,128)S(1)}, f32[33,8,384]{2,1,0:T(8,128)S(1)}, u32[]{:S(2)}, u32[]{:S(2)}) collective-permute-start(f32[33,8,384]{2,1,0:T(8,128)S(1)} %get-tuple-element.52), channel_id=1, source_target_pairs={{16,32},{32,16},{48,64},{64,48},{80,96},{96,80},{112,128},{128,112... | collective-permute-start | bytes 1216520 | tf_op jit(solution)/shard_map/ppermute | solution.py:262
  81.9 5.6 %collective-permute-done.11.refs_2_ = f32[33,8,384]{2,1,0:T(8,128)S(1)} collective-permute-done((f32[33,8,384]{2,1,0:T(8,128)S(1)}, f32[33,8,384]{2,1,0:T(8,128)S(1)}, u32[]{:S(2)}, u32[]{:S(2)}) %collective-permute-start.11) | collective-permute-done | bytes 405536 | tf_op jit(solution)/shard_map/ppermute | solution.py:262
  87.5 2.4 %window_last.1 = (f32[4,32,384]{2,1,0:T(8,128)}, f32[4,32,384]{2,1,0:T(8,128)}, f32[16,24,128]{2,1,0:T(8,128)S(1)}) custom-call(f32[8,40,384]{2,1,0:T(8,128)S(1)} %get-tuple-element.50.refs_0_, f32[33,8,384]{2,1,0:T(8,128)S(1)} %collective-permute-done.10.refs_1_, f32[33,8,384]{2,1,0:T(8,128)S(1)} %collective-permute-done.11.refs_2_, ...), custom_call_target="tpu_custom_call" | custom-call | tf_op jit(solution)/shard_map/window_last/pallas_call | solution.py:305
  89.9 23.8 %all_to_all.10.refs_0_ = f32[16,24,128]{2,1,0:T(8,128)S(1)} all-to-all(f32[16,24,128]{2,1,0:T(8,128)S(1)} %get-tuple-element.58), channel_id=1, replica_groups=mesh['gx'=48,'gy'=16] {'gy'}, dimensions={0} | all-to-all | bytes 393216 | tf_op jit(solution)/shard_map/all_to_all | solution.py:309
  115.5 31.0 %all_to_all.11.part_ref = f32[12,16,256]{2,1,0:T(8,128)S(1)} all-to-all(f32[12,16,256]{2,1,0:T(8,128)S(1)} %project.1), channel_id=1, replica_groups={{0,32,64,96,128,160,192,224,256,288,320,352},{16,48,80,112,144,176,208,..., dimensions={0} | all-to-all | bytes 393216 | tf_op jit(solution)/shard_map/all_to_all | solution.py:314
  146.5 4.3 %collective-permute-start.12 = (f32[16,256]{1,0:T(8,128)S(1)}, f32[16,256]{1,0:T(8,128)S(1)}, u32[]{:S(2)}, u32[]{:S(2)}) collective-permute-start(f32[16,256]{1,0:T(8,128)S(1)} %total.1), channel_id=1, source_target_pairs={{0,16},{16,0},{32,48},{48,32},{64,80},{80,64},{96,112},{112,96},{1... | collective-permute-start | bytes 49160 | tf_op jit(solution)/shard_map/ppermute | solution.py:316
  151.6 1.9 %collective-permute-start.13 = (f32[16,256]{1,0:T(8,128)S(1)}, f32[16,256]{1,0:T(8,128)S(1)}, u32[]{:S(2)}, u32[]{:S(2)}) collective-permute-start(f32[16,256]{1,0:T(8,128)S(1)} %add.3.refs_0_), channel_id=1, source_target_pairs={{0,384},{16,400},{32,416},{48,432},{64,448},{80,464},{96,480},{112... | collective-permute-start | bytes 49160 | tf_op jit(solution)/shard_map/ppermute | solution.py:317
  153.5 2.6 %collective-permute-done.13.refs_1_ = f32[16,256]{1,0:T(8,128)S(1)} collective-permute-done((f32[16,256]{1,0:T(8,128)S(1)}, f32[16,256]{1,0:T(8,128)S(1)}, u32[]{:S(2)}, u32[]{:S(2)}) %collective-permute-start.13) | collective-permute-done | bytes 16416 | tf_op jit(solution)/shard_map/ppermute | solution.py:317
  (24 shorter events, 7.7 us)
Async XLA Ops:
  1.8 10.7 %collective-permute-start = (f32[12,8,384]{2,1,0:T(8,128)S(1)}, f32[12,8,384]{2,1,0:T(8,128)S(1)}, u32[]{:S(2)}, u32[]{:S(2)}) collective-permute-start(f32[12,8,384]{2,1,0:T(8,128)S(1)} %get-tuple-element.32), channel_id=1, source_target_pairs={{0,1},{1,0},{2,3},{3,2},{4,5},{5,4},{6,7},{7,6},{8,9},{9,8},{10,11... | collective-permute-start | bytes 442376 | tf_op jit(solution)/shard_map/ppermute | solution.py:263
  6.9 5.7 %collective-permute-start.1 = (f32[12,8,384]{2,1,0:T(8,128)S(1)}, f32[12,8,384]{2,1,0:T(8,128)S(1)}, u32[]{:S(2)}, u32[]{:S(2)}) collective-permute-start(f32[12,8,384]{2,1,0:T(8,128)S(1)} %get-tuple-element.33), channel_id=1, source_target_pairs={{1,2},{2,1},{3,4},{4,3},{5,6},{6,5},{7,8},{8,7},{9,10},{10,9},{11,... | collective-permute-start | bytes 442376 | tf_op jit(solution)/shard_map/ppermute | solution.py:262
  12.7 11.6 %copy-start.2 = (s32[64]{0:T(128)S(1)}, s32[64]{0:T(128)}, u32[]{:S(2)}) copy-start(s32[64]{0:T(128)} %param.9) | copy-start | bytes 772
  12.7 11.7 %collective-permute-start.2 = (f32[63,8,384]{2,1,0:T(8,128)S(1)}, f32[63,8,384]{2,1,0:T(8,128)S(1)}, u32[]{:S(2)}, u32[]{:S(2)}) collective-permute-start(f32[63,8,384]{2,1,0:T(8,128)S(1)} %get-tuple-element.35), channel_id=1, source_target_pairs={{0,16},{16,0},{32,48},{48,32},{64,80},{80,64},{96,112},{112,96},{1... | collective-permute-start | bytes 2322440 | tf_op jit(solution)/shard_map/ppermute | solution.py:263
  22.4 13.2 %collective-permute-start.3 = (f32[63,8,384]{2,1,0:T(8,128)S(1)}, f32[63,8,384]{2,1,0:T(8,128)S(1)}, u32[]{:S(2)}, u32[]{:S(2)}) collective-permute-start(f32[63,8,384]{2,1,0:T(8,128)S(1)} %get-tuple-element.36), channel_id=1, source_target_pairs={{16,32},{32,16},{48,64},{64,48},{80,96},{96,80},{112,128},{128,112... | collective-permute-start | bytes 2322440 | tf_op jit(solution)/shard_map/ppermute | solution.py:262
  38.3 3.9 %collective-permute-start.4 = (f32[33,8,384]{2,1,0:T(8,128)S(1)}, f32[33,8,384]{2,1,0:T(8,128)S(1)}, u32[]{:S(2)}, u32[]{:S(2)}) collective-permute-start(f32[33,8,384]{2,1,0:T(8,128)S(1)} %get-tuple-element.38), channel_id=1, source_target_pairs={{0,16},{16,0},{32,48},{48,32},{64,80},{80,64},{96,112},{112,96},{1... | collective-permute-start | bytes 1216520 | tf_op jit(solution)/shard_map/ppermute | solution.py:263
  40.2 9.2 %collective-permute-start.5 = (f32[33,8,384]{2,1,0:T(8,128)S(1)}, f32[33,8,384]{2,1,0:T(8,128)S(1)}, u32[]{:S(2)}, u32[]{:S(2)}) collective-permute-start(f32[33,8,384]{2,1,0:T(8,128)S(1)} %get-tuple-element.39), channel_id=1, source_target_pairs={{16,32},{32,16},{48,64},{64,48},{80,96},{96,80},{112,128},{128,112... | collective-permute-start | bytes 1216520 | tf_op jit(solution)/shard_map/ppermute | solution.py:262
  51.3 9.7 %collective-permute-start.6 = (f32[8,8,384]{2,1,0:T(8,128)S(1)}, f32[8,8,384]{2,1,0:T(8,128)S(1)}, u32[]{:S(2)}, u32[]{:S(2)}) collective-permute-start(f32[8,8,384]{2,1,0:T(8,128)S(1)} %get-tuple-element.43), channel_id=1, source_target_pairs={{0,1},{1,0},{2,3},{3,2},{4,5},{5,4},{6,7},{7,6},{8,9},{9,8},{10,11... | collective-permute-start | bytes 294920 | tf_op jit(solution)/shard_map/ppermute | solution.py:263
  59.0 2.0 %collective-permute-start.7 = (f32[8,8,384]{2,1,0:T(8,128)S(1)}, f32[8,8,384]{2,1,0:T(8,128)S(1)}, u32[]{:S(2)}, u32[]{:S(2)}) collective-permute-start(f32[8,8,384]{2,1,0:T(8,128)S(1)} %get-tuple-element.44), channel_id=1, source_target_pairs={{1,2},{2,1},{3,4},{4,3},{5,6},{6,5},{7,8},{8,7},{9,10},{10,9},{11,... | collective-permute-start | bytes 294920 | tf_op jit(solution)/shard_map/ppermute | solution.py:262
  61.1 5.6 %collective-permute-start.8 = (f32[40,8,384]{2,1,0:T(8,128)S(1)}, f32[40,8,384]{2,1,0:T(8,128)S(1)}, u32[]{:S(2)}, u32[]{:S(2)}) collective-permute-start(f32[40,8,384]{2,1,0:T(8,128)S(1)} %get-tuple-element.46), channel_id=1, source_target_pairs={{0,16},{16,0},{32,48},{48,32},{64,80},{80,64},{96,112},{112,96},{1... | collective-permute-start | bytes 1474568 | tf_op jit(solution)/shard_map/ppermute | solution.py:263
  63.0 10.2 %collective-permute-start.9 = (f32[40,8,384]{2,1,0:T(8,128)S(1)}, f32[40,8,384]{2,1,0:T(8,128)S(1)}, u32[]{:S(2)}, u32[]{:S(2)}) collective-permute-start(f32[40,8,384]{2,1,0:T(8,128)S(1)} %get-tuple-element.47), channel_id=1, source_target_pairs={{16,32},{32,16},{48,64},{64,48},{80,96},{96,80},{112,128},{128,112... | collective-permute-start | bytes 1474568 | tf_op jit(solution)/shard_map/ppermute | solution.py:262
  75.3 6.6 %collective-permute-start.10 = (f32[33,8,384]{2,1,0:T(8,128)S(1)}, f32[33,8,384]{2,1,0:T(8,128)S(1)}, u32[]{:S(2)}, u32[]{:S(2)}) collective-permute-start(f32[33,8,384]{2,1,0:T(8,128)S(1)} %get-tuple-element.51), channel_id=1, source_target_pairs={{0,16},{16,0},{32,48},{48,32},{64,80},{80,64},{96,112},{112,96},{1... | collective-permute-start | bytes 1216520 | tf_op jit(solution)/shard_map/ppermute | solution.py:263
  77.3 10.2 %collective-permute-start.11 = (f32[33,8,384]{2,1,0:T(8,128)S(1)}, f32[33,8,384]{2,1,0:T(8,128)S(1)}, u32[]{:S(2)}, u32[]{:S(2)}) collective-permute-start(f32[33,8,384]{2,1,0:T(8,128)S(1)} %get-tuple-element.52), channel_id=1, source_target_pairs={{16,32},{32,16},{48,64},{64,48},{80,96},{96,80},{112,128},{128,112... | collective-permute-start | bytes 1216520 | tf_op jit(solution)/shard_map/ppermute | solution.py:262
  89.9 23.8 %copy-start = (f32[2,4096]{1,0:T(2,128)S(1)}, f32[2,4096]{1,0:T(2,128)}, u32[]{:S(2)}) copy-start(f32[2,4096]{1,0:T(2,128)} %refs_1_.1) | copy-start | bytes 98308
  146.5 9.6 %copy-start.1 = (f32[2,8,256]{2,1,0:T(8,128)S(1)}, f32[2,8,256]{2,1,0:T(8,128)}, u32[]{:S(2)}) copy-start(f32[2,8,256]{2,1,0:T(8,128)} %refs_2_.1) | copy-start | bytes 49156
  146.5 5.1 %collective-permute-start.12 = (f32[16,256]{1,0:T(8,128)S(1)}, f32[16,256]{1,0:T(8,128)S(1)}, u32[]{:S(2)}, u32[]{:S(2)}) collective-permute-start(f32[16,256]{1,0:T(8,128)S(1)} %total.1), channel_id=1, source_target_pairs={{0,16},{16,0},{32,48},{48,32},{64,80},{80,64},{96,112},{112,96},{1... | collective-permute-start | bytes 49160 | tf_op jit(solution)/shard_map/ppermute | solution.py:316
  151.6 4.5 %collective-permute-start.13 = (f32[16,256]{1,0:T(8,128)S(1)}, f32[16,256]{1,0:T(8,128)S(1)}, u32[]{:S(2)}, u32[]{:S(2)}) collective-permute-start(f32[16,256]{1,0:T(8,128)S(1)} %add.3.refs_0_), channel_id=1, source_target_pairs={{0,384},{16,400},{32,416},{48,432},{64,448},{80,464},{96,480},{112... | collective-permute-start | bytes 49160 | tf_op jit(solution)/shard_map/ppermute | solution.py:317

commit v4 on v3

--- a/solution.py
+++ b/solution.py
@@ -27,14 +27,19 @@
     )
 
 
-def edges(ref, ty):
+def plane_sets(fields, tx):
+    return [(0, tx), (tx + 1, 2 * tx + 1)] if fields == 2 else [(k * tx, (k + 1) * tx) for k in range(fields)]
+
+
+def write_edges(state, b_ref, a_ref, fields, tx, ty):
     even = lax.axis_index("gy") % 2 == 0
     top, bottom = ty - Y, 0
-    at = lambda row: ref[:, pl.ds(pl.multiple_of(row, 8), Y)]
-    return at(jnp.where(even, top, bottom)), at(jnp.where(even, bottom, top))
-
-
-def prepare_kernel(cur_hbm, bef_hbm, mat_hbm, state_ref, a_ref, b_ref, cur_ref, bef_ref, mat_ref, sems):
+    for ref, row in ((a_ref, jnp.where(even, top, bottom)), (b_ref, jnp.where(even, bottom, top))):
+        for k, (lo, hi) in enumerate(plane_sets(fields, tx)):
+            ref[k * tx : (k + 1) * tx] = state[lo:hi, pl.ds(pl.multiple_of(row, 8), Y)]
+
+
+def prepare_kernel(cur_hbm, bef_hbm, mat_hbm, state_ref, odd_even_ref, even_odd_ref, cur_ref, bef_ref, mat_ref, sems):
     tx, ty, _ = cur_ref.shape
     pairs = ((mat_hbm, mat_ref), (cur_hbm, cur_ref), (bef_hbm, bef_ref))
     copies = [pltpu.make_async_copy(src, dst, sems.at[k]) for k, (src, dst) in enumerate(pairs)]
@@ -47,7 +52,7 @@
     state_ref[0:tx] = jnp.where(mat == 1, 0.0, cur_ref[...])
     copies[2].wait()
     state_ref[tx : 2 * tx] = jnp.where(mat == 1, 0.0, bef_ref[...])
-    a_ref[...], b_ref[...] = edges(state_ref, ty)
+    write_edges(state_ref, odd_even_ref, even_odd_ref, 3, tx, ty)
 
 
 def message_tiles(fields, tx, ty, reach):
@@ -55,29 +60,31 @@
     for field in range(fields):
         late = 1 if field == 1 else 0
         for d in range(1, W + 1 - late):
-            tiles += [(field, d, 8 * k, False) for k in range(ty // 8)]
+            known = fields == 2 and late and d == 1
+            if not known:
+                tiles += [(field, d, 8 * k, False) for k in range(ty // 8)]
             rows = reach - d - late
             if rows > 4:
                 tiles += [(field, d, ty, False), (field, d, ty + 8, False)]
-            elif rows > 0:
+            elif rows > 0 and not known:
                 tiles.append((field, d, ty, True))
     return tiles
 
 
-def write_messages(own, a_ref, b_ref, fields, tx, ty, reach):
+def write_messages(own, b_ref, a_ref, fields, tx, ty, reach):
     odd = lax.axis_index("gx") % 2
     wide = own.shape[1] == ty + 16
     low = lax.broadcasted_iota(jnp.int32, (8, own.shape[2]), 0) < 4
     for k, (field, d, row, packed) in enumerate(message_tiles(fields, tx, ty, reach)):
         for ref, below in ((a_ref, odd), (b_ref, 1 - odd)):
-            plane = field * tx + below * (d - 1) + (1 - below) * (tx - d)
+            plane = plane_sets(fields, tx)[field][0] + below * (d - 1) + (1 - below) * (tx - d)
             tile = own[plane, row : row + 8]
             if packed and wide:
                 tile = jnp.where(low, tile, own[plane, row + 8 : row + 16])
             ref[k] = tile
 
 
-def read_messages(targets, a_ref, b_ref, tx, ty, reach):
+def read_messages(targets, b_ref, a_ref, tx, ty, reach):
     odd = lax.axis_index("gx") % 2
     wide = targets[0].shape[1] == ty + 16
     for k, (field, d, row, packed) in enumerate(message_tiles(len(targets), tx, ty, reach)):
@@ -89,28 +96,26 @@
                 targets[field][plane, row + 8 : row + 16] = tile
 
 
-def join_kernel(fields, tx, ty, state_ref, y_a, y_b, own_ref, a_ref, b_ref):
+def join_kernel(fields, tx, ty, state_ref, y_b, y_a, own_ref, odd_even_ref, even_odd_ref):
     odd = lax.axis_index("gy") % 2
     own_ref[:, 0:ty] = state_ref[...]
-    own_ref[:, pl.ds(pl.multiple_of(ty + 8 * odd, 8), 8)] = y_a[...]
-    own_ref[:, pl.ds(pl.multiple_of(ty + 8 - 8 * odd, 8), 8)] = y_b[...]
-    write_messages(own_ref, a_ref, b_ref, fields, tx, ty, 2 * W)
-
-
-def shifted(v, axis, by, edge):
-    n = v.shape[axis]
-    moved = pltpu.roll(v, by % n, axis)
-    if not edge:
-        return moved
-    ids = lax.broadcasted_iota(jnp.int32, v.shape, axis)
-    return jnp.where(ids == (0 if by == 1 else n - 1), 0.0, moved)
-
-
-def neighbours(plane, x):
+    for ref, row in ((y_a, ty + 8 * odd), (y_b, ty + 8 - 8 * odd)):
+        for k, (lo, hi) in enumerate(plane_sets(fields, tx)):
+            own_ref[lo:hi, pl.ds(pl.multiple_of(row, 8), 8)] = ref[k * tx : (k + 1) * tx]
+    write_messages(own_ref, odd_even_ref, even_odd_ref, fields, tx, ty, 2 * W)
+
+
+def around(plane, x):
     v = plane(x)
-    total = plane(x - 1) + plane(x + 1)
-    total = total + (shifted(v, 0, 1, False) + shifted(v, 0, -1, False))
-    return v, total + (shifted(v, 1, 1, True) + shifted(v, 1, -1, True))
+    lane = lax.broadcasted_iota(jnp.int32, (v.shape[0], 128), 1)
+    parts = [v[:, k : k + 128] for k in range(0, v.shape[1], 128)]
+    ahead = [pltpu.roll(p, 1, 1) for p in parts]
+    back = [pltpu.roll(p, 127, 1) for p in parts]
+    below = [jnp.where(lane == 0, a, b) for a, b in zip([0.0, *ahead[:-1]], ahead)]
+    above = [jnp.where(lane == 127, a, b) for a, b in zip([*back[1:], 0.0], back)]
+    z_sum = jnp.concatenate([a + b for a, b in zip(below, above)], axis=1)
+    y_sum = pltpu.roll(v, 1, 0) + pltpu.roll(v, v.shape[0] - 1, 0)
+    return v, (plane(x - 1) + plane(x + 1)) + (y_sum + z_sum)
 
 
 def narrow(v, ty):
@@ -122,10 +127,10 @@
 def window_kernel(kind, tx, ty, *refs):
     refs = list(refs)
     take = lambda n: [refs.pop(0) for _ in range(n)]
-    own, x_a, x_b = take(3)
+    own, x_b, x_a = take(3)
     (cell_row,) = take(1)
     if kind != "first":
-        gain_ref, count_ref = take(2)
+        coefs = take(3)
     done = take(3) if kind == "last" else ()
     if kind == "last":
         out_cur, out_bef, series_ref = take(3)
@@ -133,21 +138,31 @@
         state_ref, *rest = take(3)
         (sample_ref,) = take(1)
     if kind == "first":
-        gain_ref, count_ref, gain4_ref, count4_ref = take(4)
+        coefs, coefs4 = take(3), take(3)
+        gain_ref = coefs[2]
     one, two = take(2)
     nz = own.shape[2]
     targets = [one, two] + ([gain_ref] if kind == "first" else [])
-    for field, target in enumerate(targets):
-        target[tx : 2 * tx] = own[field * tx : (field + 1) * tx]
+    if kind == "first":
+        for field, target in enumerate(targets):
+            target[tx : 2 * tx] = own[field * tx : (field + 1) * tx]
+    else:
+        one[tx : 2 * tx] = own[0:tx]
+        two[tx - 1 : 2 * tx + 1] = own[tx:]
     reach = 2 * W if kind in ("first", "wide") else W
-    read_messages(targets, x_a, x_b, tx, ty, reach)
+    read_messages(targets, x_b, x_a, tx, ty, reach)
     if kind == "first":
-        count_ref[...] = jnp.zeros(count_ref.shape, F32)
+        for k in (0, 1):
+            coefs[k][...] = jnp.zeros(coefs[k].shape, F32)
         opened = lambda i: jnp.where(gain_ref[i] > 0.0, F32(1.0), F32(0.0))
         for x in range(1, 3 * tx - 1):
-            count_ref[x] = neighbours(opened, x)[1]
-        gain4_ref[...] = narrow(gain_ref[...], ty)
-        count4_ref[...] = narrow(count_ref[...], ty)
+            gain = gain_ref[x]
+            coefs[0][x] = gain * (2.0 - 0.25 * around(opened, x)[1])
+            coefs[1][x] = 0.25 * gain
+        for x in range(3 * tx):
+            gain_ref[x] = 1.0 - 2.0 * gain_ref[x]
+        for k in range(3):
+            coefs4[k][...] = narrow(coefs[k][...], ty)
     cell = cell_row[...]
     safe = jnp.maximum(cell, 0)
     lane = lax.broadcasted_iota(jnp.int32, (1, 128), 1)
@@ -160,10 +175,8 @@
     for step in range(1, W + 1):
         cur, bef = (one, two) if step % 2 else (two, one)
         for x in range(step, 3 * tx - step):
-            v, total = neighbours(lambda i: cur[i], x)
-            b = bef[x]
-            inner = 0.25 * (total - count_ref[x] * v) + 2.0 * (v - b)
-            bef[x] = gain_ref[x] * inner + b
+            v, total = around(lambda i: cur[i], x)
+            bef[x] = coefs[0][x] * v + coefs[1][x] * total + coefs[2][x] * bef[x]
         now = bef[tx : 2 * tx, 0:ty].reshape(tx * ty, nz)
         high = now.astype(BF16)
         low = (now - high.astype(F32)).astype(BF16)
@@ -171,10 +184,9 @@
         picked = jnp.where(rhot, dot(high) + dot(low), 0.0)
         picks.append(jnp.sum(picked, axis=0, keepdims=True))
     cur, bef = (one, two) if W % 2 == 0 else (two, one)
-    cur, bef = cur.at[tx : 2 * tx], bef.at[tx : 2 * tx]
     if kind == "last":
-        out_cur[...] = cur[:, 0:ty]
-        out_bef[...] = bef[:, 0:ty]
+        out_cur[...] = cur[tx : 2 * tx, 0:ty]
+        out_bef[...] = bef[tx : 2 * tx, 0:ty]
         cells = jnp.broadcast_to(cell.astype(F32), (8, 128))
         series = jnp.concatenate([*(d[...] for d in done), *picks, cells])
         for d in range(series_ref.shape[0]):
@@ -182,13 +194,12 @@
         return
     for k, pick in enumerate(picks):
         sample_ref[pl.ds(k, 1), :] = pick
+    cut = (lambda v: v[:, 0:ty]) if kind == "inner" else (lambda v: narrow(v, ty))
+    state_ref[0:tx] = cut(cur[tx : 2 * tx])
+    state_ref[tx:] = cut(bef[tx - 1 : 2 * tx + 1])
     if kind == "inner":
-        state_ref[0:tx] = cur[:, 0:ty]
-        state_ref[tx:] = bef[:, 0:ty]
-        rest[0][...], rest[1][...] = edges(state_ref, ty)
+        write_edges(state_ref, *rest, 2, tx, ty)
     else:
-        state_ref[0:tx] = narrow(cur[...], ty)
-        state_ref[tx:] = narrow(bef[...], ty)
         write_messages(state_ref, *rest, 2, tx, ty, W)
 
 
@@ -254,13 +265,11 @@
     out_ref[1] = spec_ref[1] - dot(sin_t)
 
 
-def swap(v, axis):
+def swap(odd_even, even_odd, axis):
     count = lax.axis_size(axis)
-    even_odd = [(i, i ^ 1) for i in range(count) if i ^ 1 < count]
-    odd_even = [(i, ((i + 1) ^ 1) - 1) for i in range(1, count) if ((i + 1) ^ 1) - 1 < count]
-    v_a, v_b = v
-    got_b = lax.ppermute(v_b, axis, odd_even)
-    return lax.ppermute(v_a, axis, even_odd), got_b
+    pairs = [(i, ((i + 1) ^ 1) - 1) for i in range(1, count) if ((i + 1) ^ 1) - 1 < count]
+    got = lax.ppermute(odd_even, axis, pairs)
+    return got, lax.ppermute(even_odd, axis, [(i, i ^ 1) for i in range(count) if i ^ 1 < count])
 
 
 def body(pressure, previous, material, slot_cell, angles, spectra_in):
@@ -271,14 +280,14 @@
     wide, thin = (3 * tx, ty + 2 * Y, nz), (3 * tx, ty + 2 * W, nz)
     scratch = lambda s: [pltpu.VMEM(s, F32)] * 2
 
-    def exchange_y(fields, state, a, b):
+    def exchange_y(fields, state, *edges):
         size = shape(len(message_tiles(fields, tx, ty, 2 * W)), 8, nz)
         return call(
-            lambda *refs: join_kernel(fields, tx, ty, *refs), [shape(fields * tx, *wide[1:]), size, size], name="join"
-        )(state, *swap((a, b), "gy"))
-
-    def exchange_x(own, a, b):
-        return [own, *swap((a, b), "gx"), cells]
+            lambda *refs: join_kernel(fields, tx, ty, *refs), [shape(*state.shape[:1], *wide[1:]), size, size], name="join"
+        )(state, *swap(*edges, "gy"))
+
+    def exchange_x(own, *messages):
+        return [own, *swap(*messages, "gx"), cells]
 
     cells = jnp.concatenate([slot_cell, slot_cell])[None, :]
     tile, edge = (tx, ty, nz), (tx, Y, nz)
@@ -293,18 +302,18 @@
     own = exchange_y(3, *state)
     part = shape(W, 128)
     message = shape(len(message_tiles(2, tx, ty, W)), 8, nz)
-    between = [shape(2 * tx, *thin[1:]), message, message, part]
-    *own, first, gain, count, gain4, count4 = call(
-        window("first"), between + [shape(*wide), shape(*wide), shape(*thin), shape(*thin)], scratch(wide), name="window_first"
+    between = [shape(2 * tx + 2, *thin[1:]), message, message, part]
+    *own, first, p, q, r, p4, q4, r4 = call(
+        window("first"), between + [shape(*wide)] * 3 + [shape(*thin)] * 3, scratch(wide), name="window_first"
     )(*exchange_x(*own))
     *state, second = call(
-        window("inner"), [shape(2 * tx, ty, nz), shape(2 * tx, Y, nz), shape(2 * tx, Y, nz), part], scratch(thin), name="window_inner"
-    )(*exchange_x(*own), gain4, count4)
+        window("inner"), [shape(2 * tx + 2, ty, nz), shape(2 * tx, Y, nz), shape(2 * tx, Y, nz), part], scratch(thin), name="window_inner"
+    )(*exchange_x(*own), p4, q4, r4)
     own = exchange_y(2, *state)
-    *own, third = call(window("wide"), between, scratch(wide), name="window_wide")(*exchange_x(*own), gain, count)
+    *own, third = call(window("wide"), between, scratch(wide), name="window_wide")(*exchange_x(*own), p, q, r)
     current, before, series = call(
         window("last"), [shape(*tile), shape(*tile), shape(ngy, STEPS + 8, 128)], scratch(thin), name="window_last"
-    )(*exchange_x(*own), gain4, count4, first, second, third)
+    )(*exchange_x(*own), p4, q4, r4, first, second, third)
 
     series = lax.all_to_all(series, "gy", 0, 0, tiled=True)
     own = spectra_in.shape[2]

time: 158 us -> 144 us (0.911)
  waiting for transfers between devices: 40.2 us -> 33.7 us
  blocking collectives: 54.7 us -> 50.1 us
  starting transfers between devices: 47.8 us -> 45.1 us
    ppermute x12, waiting for transfers between devices: 36.8 us -> 30.5 us  [the longest x6 19.3 us: swap(): got = lax.ppermute(odd_even, axis, pairs)]
    ppermute x12, starting transfers between devices: 41.6 us -> 39.1 us  [the longest x6 23.1 us: swap(): lax.ppermute(even_odd, axis, [(i, i ^ 1) for i in range(count) if i ^ 1 <...]
    all_to_all x1, blocking collectives: 23.8 us -> 21.3 us  [body(): series = lax.all_to_all(series, 'gy', 0, 0, tiled=True)]
    all_to_all x1, blocking collectives: 31 us -> 28.8 us  [body(): lax.all_to_all(partial, 'gx', 0, 0, tiled=True, axis_index_groups=groups)]
where the time goes in v4:
time: 144 us; the launch traced here: 143 us
  blocking collectives  50.1 us (35%)
  starting transfers between devices  45.1 us (31%)
  waiting for transfers between devices  33.7 us (23%)
  Pallas kernels  13.4 us (9%)
    all_to_all x1, blocking collectives, body(): lax.all_to_all(partial, 'gx', 0, 0, tiled=True, axis_index_groups=groups)  28.8 us
    ppermute x6, starting transfers between devices, swap(): lax.ppermute(even_odd, axis, [(i, i ^ 1) for i in range(count) if i ^ 1 <...  23.1 us
    all_to_all x1, blocking collectives, body(): series = lax.all_to_all(series, 'gy', 0, 0, tiled=True)  21.3 us
    ppermute x6, waiting for transfers between devices, swap(): got = lax.ppermute(odd_even, axis, pairs)  19.3 us
    ppermute x6, starting transfers between devices, swap(): got = lax.ppermute(odd_even, axis, pairs)  16 us
    ppermute x6, waiting for transfers between devices, swap(): lax.ppermute(even_odd, axis, [(i, i ^ 1) for i in range(count) if i ^ 1 <...  11.2 us
    ppermute x1, starting transfers between devices, body(): lax.ppermute(traces, 'gx', [(i, i ^ 1) for i in range(ngx)])  3.86 us
  transfers between devices with their start and end apart: 14, of which 8 were waited for; matrix products, arithmetic and copies ran while one was open for 0% of the time, Pallas kernels for 0%

profile of v4, /device:TPU:1, one launch (start us, length us, event | category | flops | bytes accessed | tf_op | source)
XLA Modules:
  0.0 143.2 jit_solution(1471993307459924370)
XLA Ops:
  2.5 9.8 %collective-permute-start.1 = (f32[12,8,384]{2,1,0:T(8,128)S(1)}, f32[12,8,384]{2,1,0:T(8,128)S(1)}, u32[]{:S(2)}, u32[]{:S(2)}) collective-permute-start(f32[12,8,384]{2,1,0:T(8,128)S(1)} %get-tuple-element.35), channel_id=1, source_target_pairs={{0,1},{1,0},{2,3},{3,2},{4,5},{5,4},{6,7},{7,6},{8,9},{9,8},{10,11... | collective-permute-start | bytes 442376 | tf_op jit(solution)/shard_map/ppermute | solution.py:272
  12.3 6.3 %collective-permute-done.1.refs_2_ = f32[12,8,384]{2,1,0:T(8,128)S(1)} collective-permute-done((f32[12,8,384]{2,1,0:T(8,128)S(1)}, f32[12,8,384]{2,1,0:T(8,128)S(1)}, u32[]{:S(2)}, u32[]{:S(2)}) %collective-permute-start.1) | collective-permute-done | bytes 147488 | tf_op jit(solution)/shard_map/ppermute | solution.py:272
  18.8 5.5 %collective-permute-start.2 = (f32[63,8,384]{2,1,0:T(8,128)S(1)}, f32[63,8,384]{2,1,0:T(8,128)S(1)}, u32[]{:S(2)}, u32[]{:S(2)}) collective-permute-start(f32[63,8,384]{2,1,0:T(8,128)S(1)} %get-tuple-element.37), channel_id=1, source_target_pairs={{16,32},{32,16},{48,64},{64,48},{80,96},{96,80},{112,128},{128,112... | collective-permute-start | bytes 2322440 | tf_op jit(solution)/shard_map/ppermute | solution.py:271
  24.3 1.9 %collective-permute-start.3 = (f32[63,8,384]{2,1,0:T(8,128)S(1)}, f32[63,8,384]{2,1,0:T(8,128)S(1)}, u32[]{:S(2)}, u32[]{:S(2)}) collective-permute-start(f32[63,8,384]{2,1,0:T(8,128)S(1)} %get-tuple-element.38), channel_id=1, source_target_pairs={{0,16},{16,0},{32,48},{48,32},{64,80},{80,64},{96,112},{112,96},{1... | collective-permute-start | bytes 2322440 | tf_op jit(solution)/shard_map/ppermute | solution.py:272
  26.4 7.5 %collective-permute-done.2.refs_1_ = f32[63,8,384]{2,1,0:T(8,128)S(1)} collective-permute-done((f32[63,8,384]{2,1,0:T(8,128)S(1)}, f32[63,8,384]{2,1,0:T(8,128)S(1)}, u32[]{:S(2)}, u32[]{:S(2)}) %collective-permute-start.2) | collective-permute-done | bytes 774176 | tf_op jit(solution)/shard_map/ppermute | solution.py:271
  33.9 2.8 %window_first.1 = (f32[10,40,384]{2,1,0:T(8,128)S(1)}, f32[28,8,384]{2,1,0:T(8,128)S(1)}, f32[28,8,384]{2,1,0:T(8,128)S(1)}, f32[4,128]{1,0:T(4,128)S(1)}, f32[1...) custom-call(f32[12,48,384]{2,1,0:T(8,128)S(1)} %get-tuple-element.36, ...), custom_call_target="tpu_custom_call" | custom-call | tf_op jit(solution)/shard_map/window_first/pallas_call | solution.py:306
  36.7 3.6 %collective-permute-start.4 = (f32[28,8,384]{2,1,0:T(8,128)S(1)}, f32[28,8,384]{2,1,0:T(8,128)S(1)}, u32[]{:S(2)}, u32[]{:S(2)}) collective-permute-start(f32[28,8,384]{2,1,0:T(8,128)S(1)} %get-tuple-element.40), channel_id=1, source_target_pairs={{16,32},{32,16},{48,64},{64,48},{80,96},{96,80},{112,128},{128,112... | collective-permute-start | bytes 1032200 | tf_op jit(solution)/shard_map/ppermute | solution.py:271
  40.3 1.9 %collective-permute-start.5 = (f32[28,8,384]{2,1,0:T(8,128)S(1)}, f32[28,8,384]{2,1,0:T(8,128)S(1)}, u32[]{:S(2)}, u32[]{:S(2)}) collective-permute-start(f32[28,8,384]{2,1,0:T(8,128)S(1)} %get-tuple-element.41), channel_id=1, source_target_pairs={{0,16},{16,0},{32,48},{48,32},{64,80},{80,64},{96,112},{112,96},{1... | collective-permute-start | bytes 1032200 | tf_op jit(solution)/shard_map/ppermute | solution.py:272
  42.2 3.0 %collective-permute-done.4.refs_1_ = f32[28,8,384]{2,1,0:T(8,128)S(1)} collective-permute-done((f32[28,8,384]{2,1,0:T(8,128)S(1)}, f32[28,8,384]{2,1,0:T(8,128)S(1)}, u32[]{:S(2)}, u32[]{:S(2)}) %collective-permute-start.4) | collective-permute-done | bytes 344096 | tf_op jit(solution)/shard_map/ppermute | solution.py:271
  47.8 5.6 %collective-permute-start.7 = (f32[8,8,384]{2,1,0:T(8,128)S(1)}, f32[8,8,384]{2,1,0:T(8,128)S(1)}, u32[]{:S(2)}, u32[]{:S(2)}) collective-permute-start(f32[8,8,384]{2,1,0:T(8,128)S(1)} %get-tuple-element.47), channel_id=1, source_target_pairs={{0,1},{1,0},{2,3},{3,2},{4,5},{5,4},{6,7},{7,6},{8,9},{9,8},{10,11... | collective-permute-start | bytes 294920 | tf_op jit(solution)/shard_map/ppermute | solution.py:272
  53.4 4.9 %collective-permute-done.7.refs_2_ = f32[8,8,384]{2,1,0:T(8,128)S(1)} collective-permute-done((f32[8,8,384]{2,1,0:T(8,128)S(1)}, f32[8,8,384]{2,1,0:T(8,128)S(1)}, u32[]{:S(2)}, u32[]{:S(2)}) %collective-permute-start.7) | collective-permute-done | bytes 98336 | tf_op jit(solution)/shard_map/ppermute | solution.py:272
  58.4 2.8 %collective-permute-start.8 = (f32[36,8,384]{2,1,0:T(8,128)S(1)}, f32[36,8,384]{2,1,0:T(8,128)S(1)}, u32[]{:S(2)}, u32[]{:S(2)}) collective-permute-start(f32[36,8,384]{2,1,0:T(8,128)S(1)} %get-tuple-element.49), channel_id=1, source_target_pairs={{16,32},{32,16},{48,64},{64,48},{80,96},{96,80},{112,128},{128,112... | collective-permute-start | bytes 1327112 | tf_op jit(solution)/shard_map/ppermute | solution.py:271
  61.2 1.9 %collective-permute-start.9 = (f32[36,8,384]{2,1,0:T(8,128)S(1)}, f32[36,8,384]{2,1,0:T(8,128)S(1)}, u32[]{:S(2)}, u32[]{:S(2)}) collective-permute-start(f32[36,8,384]{2,1,0:T(8,128)S(1)} %get-tuple-element.50), channel_id=1, source_target_pairs={{0,16},{16,0},{32,48},{48,32},{64,80},{80,64},{96,112},{112,96},{1... | collective-permute-start | bytes 1327112 | tf_op jit(solution)/shard_map/ppermute | solution.py:272
  63.1 4.9 %collective-permute-done.8.refs_1_ = f32[36,8,384]{2,1,0:T(8,128)S(1)} collective-permute-done((f32[36,8,384]{2,1,0:T(8,128)S(1)}, f32[36,8,384]{2,1,0:T(8,128)S(1)}, u32[]{:S(2)}, u32[]{:S(2)}) %collective-permute-start.8) | collective-permute-done | bytes 442400 | tf_op jit(solution)/shard_map/ppermute | solution.py:271
  68.0 2.2 %window_wide.1 = (f32[10,40,384]{2,1,0:T(8,128)S(1)}, f32[28,8,384]{2,1,0:T(8,128)S(1)}, f32[28,8,384]{2,1,0:T(8,128)S(1)}, f32[4,128]{1,0:T(4,128)S(1)}) custom-call(f32[10,48,384]{2,1,0:T(8,128)S(1)} %get-tuple-element.48.refs_0_, f32[36,8,384]{2,1,0:T(8,128)S(1)} %collective-permute-done.8.refs_1_, f32[36,8,384]{2,1,0:T(8,128)S(1)} %collective-permute-done.9.refs_2_, ...), custom_call_target="tpu_custom_call" | custom-call | tf_op jit(solution)/shard_map/window_wide/pallas_call | solution.py:313
  70.2 2.8 %collective-permute-start.10 = (f32[28,8,384]{2,1,0:T(8,128)S(1)}, f32[28,8,384]{2,1,0:T(8,128)S(1)}, u32[]{:S(2)}, u32[]{:S(2)}) collective-permute-start(f32[28,8,384]{2,1,0:T(8,128)S(1)} %get-tuple-element.55), channel_id=1, source_target_pairs={{16,32},{32,16},{48,64},{64,48},{80,96},{96,80},{112,128},{128,112... | collective-permute-start | bytes 1032200 | tf_op jit(solution)/shard_map/ppermute | solution.py:271
  73.0 1.9 %collective-permute-start.11 = (f32[28,8,384]{2,1,0:T(8,128)S(1)}, f32[28,8,384]{2,1,0:T(8,128)S(1)}, u32[]{:S(2)}, u32[]{:S(2)}) collective-permute-start(f32[28,8,384]{2,1,0:T(8,128)S(1)} %get-tuple-element.56), channel_id=1, source_target_pairs={{0,16},{16,0},{32,48},{48,32},{64,80},{80,64},{96,112},{112,96},{1... | collective-permute-start | bytes 1032200 | tf_op jit(solution)/shard_map/ppermute | solution.py:272
  74.9 3.8 %collective-permute-done.10.refs_1_ = f32[28,8,384]{2,1,0:T(8,128)S(1)} collective-permute-done((f32[28,8,384]{2,1,0:T(8,128)S(1)}, f32[28,8,384]{2,1,0:T(8,128)S(1)}, u32[]{:S(2)}, u32[]{:S(2)}) %collective-permute-start.10) | collective-permute-done | bytes 344096 | tf_op jit(solution)/shard_map/ppermute | solution.py:271
  78.8 2.5 %window_last.1 = (f32[4,32,384]{2,1,0:T(8,128)}, f32[4,32,384]{2,1,0:T(8,128)}, f32[16,24,128]{2,1,0:T(8,128)S(1)}) custom-call(f32[10,40,384]{2,1,0:T(8,128)S(1)} %get-tuple-element.54.refs_0_, f32[28,8,384]{2,1,0:T(8,128)S(1)} %collective-permute-done.10.refs_1_, f32[28,8,384]{2,1,0:T(8,128)S(1)} %collective-permute-done.11.refs_2_, ...), custom_call_target="tpu_custom_call" | custom-call | tf_op jit(solution)/shard_map/window_last/pallas_call | solution.py:314
  81.3 21.3 %all_to_all.10.refs_0_ = f32[16,24,128]{2,1,0:T(8,128)S(1)} all-to-all(f32[16,24,128]{2,1,0:T(8,128)S(1)} %get-tuple-element.62), channel_id=1, replica_groups=mesh['gx'=48,'gy'=16] {'gy'}, dimensions={0} | all-to-all | bytes 393216 | tf_op jit(solution)/shard_map/all_to_all | solution.py:318
  104.5 28.8 %all_to_all.11.part_ref = f32[12,16,256]{2,1,0:T(8,128)S(1)} all-to-all(f32[12,16,256]{2,1,0:T(8,128)S(1)} %project.1), channel_id=1, replica_groups={{0,32,64,96,128,160,192,224,256,288,320,352},{16,48,80,112,144,176,208,..., dimensions={0} | all-to-all | bytes 393216 | tf_op jit(solution)/shard_map/all_to_all | solution.py:323
  133.3 3.9 %collective-permute-start.12 = (f32[16,256]{1,0:T(8,128)S(1)}, f32[16,256]{1,0:T(8,128)S(1)}, u32[]{:S(2)}, u32[]{:S(2)}) collective-permute-start(f32[16,256]{1,0:T(8,128)S(1)} %total.1), channel_id=1, source_target_pairs={{0,16},{16,0},{32,48},{48,32},{64,80},{80,64},{96,112},{112,96},{1... | collective-permute-start | bytes 49160 | tf_op jit(solution)/shard_map/ppermute | solution.py:325
  138.0 2.1 %collective-permute-start.13 = (f32[16,256]{1,0:T(8,128)S(1)}, f32[16,256]{1,0:T(8,128)S(1)}, u32[]{:S(2)}, u32[]{:S(2)}) collective-permute-start(f32[16,256]{1,0:T(8,128)S(1)} %add.3.refs_0_), channel_id=1, source_target_pairs={{0,384},{16,400},{32,416},{48,432},{64,448},{80,464},{96,480},{112... | collective-permute-start | bytes 49160 | tf_op jit(solution)/shard_map/ppermute | solution.py:326
  140.1 2.3 %collective-permute-done.13.refs_1_ = f32[16,256]{1,0:T(8,128)S(1)} collective-permute-done((f32[16,256]{1,0:T(8,128)S(1)}, f32[16,256]{1,0:T(8,128)S(1)}, u32[]{:S(2)}, u32[]{:S(2)}) %collective-permute-start.13) | collective-permute-done | bytes 16416 | tf_op jit(solution)/shard_map/ppermute | solution.py:326
  (24 shorter events, 8.2 us)
Async XLA Ops:
  1.8 10.5 %collective-permute-start = (f32[12,8,384]{2,1,0:T(8,128)S(1)}, f32[12,8,384]{2,1,0:T(8,128)S(1)}, u32[]{:S(2)}, u32[]{:S(2)}) collective-permute-start(f32[12,8,384]{2,1,0:T(8,128)S(1)} %get-tuple-element.34), channel_id=1, source_target_pairs={{1,2},{2,1},{3,4},{4,3},{5,6},{6,5},{7,8},{8,7},{9,10},{10,9},{11,... | collective-permute-start | bytes 442376 | tf_op jit(solution)/shard_map/ppermute | solution.py:271
  2.5 16.2 %collective-permute-start.1 = (f32[12,8,384]{2,1,0:T(8,128)S(1)}, f32[12,8,384]{2,1,0:T(8,128)S(1)}, u32[]{:S(2)}, u32[]{:S(2)}) collective-permute-start(f32[12,8,384]{2,1,0:T(8,128)S(1)} %get-tuple-element.35), channel_id=1, source_target_pairs={{0,1},{1,0},{2,3},{3,2},{4,5},{5,4},{6,7},{7,6},{8,9},{9,8},{10,11... | collective-permute-start | bytes 442376 | tf_op jit(solution)/shard_map/ppermute | solution.py:272
  18.8 7.4 %copy-start.2 = (s32[64]{0:T(128)S(1)}, s32[64]{0:T(128)}, u32[]{:S(2)}) copy-start(s32[64]{0:T(128)} %param.9) | copy-start | bytes 772
  18.8 15.0 %collective-permute-start.2 = (f32[63,8,384]{2,1,0:T(8,128)S(1)}, f32[63,8,384]{2,1,0:T(8,128)S(1)}, u32[]{:S(2)}, u32[]{:S(2)}) collective-permute-start(f32[63,8,384]{2,1,0:T(8,128)S(1)} %get-tuple-element.37), channel_id=1, source_target_pairs={{16,32},{32,16},{48,64},{64,48},{80,96},{96,80},{112,128},{128,112... | collective-permute-start | bytes 2322440 | tf_op jit(solution)/shard_map/ppermute | solution.py:271
  24.3 9.5 %collective-permute-start.3 = (f32[63,8,384]{2,1,0:T(8,128)S(1)}, f32[63,8,384]{2,1,0:T(8,128)S(1)}, u32[]{:S(2)}, u32[]{:S(2)}) collective-permute-start(f32[63,8,384]{2,1,0:T(8,128)S(1)} %get-tuple-element.38), channel_id=1, source_target_pairs={{0,16},{16,0},{32,48},{48,32},{64,80},{80,64},{96,112},{112,96},{1... | collective-permute-start | bytes 2322440 | tf_op jit(solution)/shard_map/ppermute | solution.py:272
  36.7 8.6 %collective-permute-start.4 = (f32[28,8,384]{2,1,0:T(8,128)S(1)}, f32[28,8,384]{2,1,0:T(8,128)S(1)}, u32[]{:S(2)}, u32[]{:S(2)}) collective-permute-start(f32[28,8,384]{2,1,0:T(8,128)S(1)} %get-tuple-element.40), channel_id=1, source_target_pairs={{16,32},{32,16},{48,64},{64,48},{80,96},{96,80},{112,128},{128,112... | collective-permute-start | bytes 1032200 | tf_op jit(solution)/shard_map/ppermute | solution.py:271
  40.3 4.9 %collective-permute-start.5 = (f32[28,8,384]{2,1,0:T(8,128)S(1)}, f32[28,8,384]{2,1,0:T(8,128)S(1)}, u32[]{:S(2)}, u32[]{:S(2)}) collective-permute-start(f32[28,8,384]{2,1,0:T(8,128)S(1)} %get-tuple-element.41), channel_id=1, source_target_pairs={{0,16},{16,0},{32,48},{48,32},{64,80},{80,64},{96,112},{112,96},{1... | collective-permute-start | bytes 1032200 | tf_op jit(solution)/shard_map/ppermute | solution.py:272
  47.1 6.3 %collective-permute-start.6 = (f32[8,8,384]{2,1,0:T(8,128)S(1)}, f32[8,8,384]{2,1,0:T(8,128)S(1)}, u32[]{:S(2)}, u32[]{:S(2)}) collective-permute-start(f32[8,8,384]{2,1,0:T(8,128)S(1)} %get-tuple-element.46), channel_id=1, source_target_pairs={{1,2},{2,1},{3,4},{4,3},{5,6},{6,5},{7,8},{8,7},{9,10},{10,9},{11,... | collective-permute-start | bytes 294920 | tf_op jit(solution)/shard_map/ppermute | solution.py:271
  47.8 10.5 %collective-permute-start.7 = (f32[8,8,384]{2,1,0:T(8,128)S(1)}, f32[8,8,384]{2,1,0:T(8,128)S(1)}, u32[]{:S(2)}, u32[]{:S(2)}) collective-permute-start(f32[8,8,384]{2,1,0:T(8,128)S(1)} %get-tuple-element.47), channel_id=1, source_target_pairs={{0,1},{1,0},{2,3},{3,2},{4,5},{5,4},{6,7},{7,6},{8,9},{9,8},{10,11... | collective-permute-start | bytes 294920 | tf_op jit(solution)/shard_map/ppermute | solution.py:272
  58.4 9.6 %collective-permute-start.8 = (f32[36,8,384]{2,1,0:T(8,128)S(1)}, f32[36,8,384]{2,1,0:T(8,128)S(1)}, u32[]{:S(2)}, u32[]{:S(2)}) collective-permute-start(f32[36,8,384]{2,1,0:T(8,128)S(1)} %get-tuple-element.49), channel_id=1, source_target_pairs={{16,32},{32,16},{48,64},{64,48},{80,96},{96,80},{112,128},{128,112... | collective-permute-start | bytes 1327112 | tf_op jit(solution)/shard_map/ppermute | solution.py:271
  61.2 6.8 %collective-permute-start.9 = (f32[36,8,384]{2,1,0:T(8,128)S(1)}, f32[36,8,384]{2,1,0:T(8,128)S(1)}, u32[]{:S(2)}, u32[]{:S(2)}) collective-permute-start(f32[36,8,384]{2,1,0:T(8,128)S(1)} %get-tuple-element.50), channel_id=1, source_target_pairs={{0,16},{16,0},{32,48},{48,32},{64,80},{80,64},{96,112},{112,96},{1... | collective-permute-start | bytes 1327112 | tf_op jit(solution)/shard_map/ppermute | solution.py:272
  70.2 8.6 %collective-permute-start.10 = (f32[28,8,384]{2,1,0:T(8,128)S(1)}, f32[28,8,384]{2,1,0:T(8,128)S(1)}, u32[]{:S(2)}, u32[]{:S(2)}) collective-permute-start(f32[28,8,384]{2,1,0:T(8,128)S(1)} %get-tuple-element.55), channel_id=1, source_target_pairs={{16,32},{32,16},{48,64},{64,48},{80,96},{96,80},{112,128},{128,112... | collective-permute-start | bytes 1032200 | tf_op jit(solution)/shard_map/ppermute | solution.py:271
  73.0 5.8 %collective-permute-start.11 = (f32[28,8,384]{2,1,0:T(8,128)S(1)}, f32[28,8,384]{2,1,0:T(8,128)S(1)}, u32[]{:S(2)}, u32[]{:S(2)}) collective-permute-start(f32[28,8,384]{2,1,0:T(8,128)S(1)} %get-tuple-element.56), channel_id=1, source_target_pairs={{0,16},{16,0},{32,48},{48,32},{64,80},{80,64},{96,112},{112,96},{1... | collective-permute-start | bytes 1032200 | tf_op jit(solution)/shard_map/ppermute | solution.py:272
  81.3 21.3 %copy-start = (f32[2,4096]{1,0:T(2,128)S(1)}, f32[2,4096]{1,0:T(2,128)}, u32[]{:S(2)}) copy-start(f32[2,4096]{1,0:T(2,128)} %refs_1_.1) | copy-start | bytes 98308
  133.3 9.2 %copy-start.1 = (f32[2,8,256]{2,1,0:T(8,128)S(1)}, f32[2,8,256]{2,1,0:T(8,128)}, u32[]{:S(2)}) copy-start(f32[2,8,256]{2,1,0:T(8,128)} %refs_2_.1) | copy-start | bytes 49156
  133.3 4.7 %collective-permute-start.12 = (f32[16,256]{1,0:T(8,128)S(1)}, f32[16,256]{1,0:T(8,128)S(1)}, u32[]{:S(2)}, u32[]{:S(2)}) collective-permute-start(f32[16,256]{1,0:T(8,128)S(1)} %total.1), channel_id=1, source_target_pairs={{0,16},{16,0},{32,48},{48,32},{64,80},{80,64},{96,112},{112,96},{1... | collective-permute-start | bytes 49160 | tf_op jit(solution)/shard_map/ppermute | solution.py:325
  138.0 4.5 %collective-permute-start.13 = (f32[16,256]{1,0:T(8,128)S(1)}, f32[16,256]{1,0:T(8,128)S(1)}, u32[]{:S(2)}, u32[]{:S(2)}) collective-permute-start(f32[16,256]{1,0:T(8,128)S(1)} %add.3.refs_0_), channel_id=1, source_target_pairs={{0,384},{16,400},{32,416},{48,432},{64,448},{80,464},{96,480},{112... | collective-permute-start | bytes 49160 | tf_op jit(solution)/shard_map/ppermute | solution.py:326

commit v5 on v4

--- a/solution.py
+++ b/solution.py
@@ -116,6 +116,33 @@
     z_sum = jnp.concatenate([a + b for a, b in zip(below, above)], axis=1)
     y_sum = pltpu.roll(v, 1, 0) + pltpu.roll(v, v.shape[0] - 1, 0)
     return v, (plane(x - 1) + plane(x + 1)) + (y_sum + z_sum)
+
+
+def advance_step(cur, bef, coefs, lo, hi):
+    rows = cur.shape[1] // 8
+    row = lax.broadcasted_iota(jnp.int32, (8, 128), 0)
+    lane = lax.broadcasted_iota(jnp.int32, (8, 128), 1)
+    n = cur.shape[2] // 128
+    for k in range(rows):
+        before, after = (k - 1) % rows, (k + 1) % rows
+        at = slice(8 * k, 8 * k + 8)
+        load = lambda x, i, j: cur[x, 8 * i : 8 * i + 8, 128 * j : 128 * j + 128]
+        line = lambda x: [load(x, k, j) for j in range(n)]
+        down, here = line(lo - 1), line(lo)
+        for x in range(lo, hi):
+            up = line(x + 1)
+            ahead = [pltpu.roll(p, 1, 1) for p in here]
+            back = [pltpu.roll(p, 127, 1) for p in here]
+            for j in range(n):
+                cols = slice(128 * j, 128 * j + 128)
+                z = jnp.where(lane == 0, ahead[j - 1] if j else 0.0, ahead[j])
+                z = z + jnp.where(lane == 127, back[j + 1] if j + 1 < n else 0.0, back[j])
+                y = pltpu.roll(jnp.where(row == 7, load(x, before, j), here[j]), 1, 0)
+                y = y + pltpu.roll(jnp.where(row == 0, load(x, after, j), here[j]), 7, 0)
+                total = (down[j] + up[j]) + (y + z)
+                new = coefs[0][x, at, cols] * here[j] + coefs[1][x, at, cols] * total
+                bef[x, at, cols] = new + coefs[2][x, at, cols] * bef[x, at, cols]
+            down, here = here, up
 
 
 def narrow(v, ty):
@@ -174,9 +201,7 @@
     picks = []
     for step in range(1, W + 1):
         cur, bef = (one, two) if step % 2 else (two, one)
-        for x in range(step, 3 * tx - step):
-            v, total = around(lambda i: cur[i], x)
-            bef[x] = coefs[0][x] * v + coefs[1][x] * total + coefs[2][x] * bef[x]
+        advance_step(cur, bef, coefs, step, 3 * tx - step)
         now = bef[tx : 2 * tx, 0:ty].reshape(tx * ty, nz)
         high = now.astype(BF16)
         low = (now - high.astype(F32)).astype(BF16)
@@ -187,10 +212,7 @@
     if kind == "last":
         out_cur[...] = cur[tx : 2 * tx, 0:ty]
         out_bef[...] = bef[tx : 2 * tx, 0:ty]
-        cells = jnp.broadcast_to(cell.astype(F32), (8, 128))
-        series = jnp.concatenate([*(d[...] for d in done), *picks, cells])
-        for d in range(series_ref.shape[0]):
-            series_ref[d] = series
+        series_ref[...] = jnp.concatenate([*(d[...] for d in done), *picks])
         return
     for k, pick in enumerate(picks):
         sample_ref[pl.ds(k, 1), :] = pick
@@ -216,39 +238,46 @@
     return 2.0 * s * c, 1.0 - 2.0 * s * s
 
 
-def project_kernel(tx, ty, nz, own, series_ref, angle_ref, out_ref):
-    slots = 64
-    ndev, _, lanes = series_ref.shape
-    at = pl.multiple_of(lax.axis_index("gy") * own, 128)
-    sin_e, cos_e = sin_cos_turns(angle_ref[0:1, pl.ds(at, own)] * (1.0 / TURN))
-    sin_a, cos_a = sin_cos_turns(angle_ref[1:2, pl.ds(at, own)] * (1.0 / TURN))
-    ux, uy, uz = cos_e * cos_a, cos_e * sin_a, sin_e
-    rows = [series_ref[d, STEPS : STEPS + 1, :] for d in range(ndev)]
-    cells = jnp.concatenate([*rows, jnp.zeros((lanes - ndev, lanes), F32)]).T[0:slots]
+def waves_kernel(tx, ty, nz, cell_ref, angle_ref, high_ref, low_ref):
+    slots = cell_ref.shape[1] // 2
+    cells = jnp.broadcast_to(cell_ref[...], (8, 2 * slots)).astype(F32)
+    cells = jnp.concatenate([cells] * (2 * slots // 8)).T[0:slots, 0:1]
     cells = jnp.maximum(cells, 0.0).astype(jnp.int32)
-    device = lax.broadcasted_iota(jnp.int32, cells.shape, 1)
     x_of = (lax.axis_index("gx") * tx + cells // (ty * nz)).astype(F32)
-    y_of = (device * ty + cells // nz % ty).astype(F32)
+    y_of = (lax.axis_index("gy") * ty + cells // nz % ty).astype(F32)
     z_of = (cells % nz).astype(F32)
-    total = jnp.zeros((STEPS, own), F32)
-    for d in range(ndev):
-        column = lambda v: v[:, d : d + 1]
-        turns = (KAPPA / TURN) * (ux * column(x_of) + uy * column(y_of) + uz * column(z_of))
-        s, c = sin_cos_turns(turns)
-        waves = jnp.concatenate([uz * s - c, c])
-        wave_high = waves.astype(BF16)
-        wave_low = (waves - wave_high.astype(F32)).astype(BF16)
-        v = series_ref[d, 0:STEPS, :]
-        high = v.astype(BF16)
-        low = (v - high.astype(F32)).astype(BF16)
-        dot = lambda a, b: jnp.dot(a, b, preferred_element_type=F32)
-        total = total + dot(high, wave_high) + (dot(low, wave_high) + dot(high, wave_low))
+    width = 512
+    for k in range(0, angle_ref.shape[1], width):
+        cols = slice(k, k + width)
+        sin_e, cos_e = sin_cos_turns(angle_ref[0:1, cols] * (1.0 / TURN))
+        sin_a, cos_a = sin_cos_turns(angle_ref[1:2, cols] * (1.0 / TURN))
+        ux, uy, uz = cos_e * cos_a, cos_e * sin_a, sin_e
+        s, c = sin_cos_turns((KAPPA / TURN) * (ux * x_of + uy * y_of + uz * z_of))
+        for half, v in enumerate((uz * s - c, c)):
+            rows = slice(half * slots, (half + 1) * slots)
+            high = v.astype(BF16)
+            high_ref[rows, cols] = high
+            low_ref[rows, cols] = (v - high.astype(F32)).astype(BF16)
+
+
+def project_kernel(series_ref, high_ref, low_ref, out_ref):
+    v = series_ref[...]
+    high = v.astype(BF16)
+    low = (v - high.astype(F32)).astype(BF16)
+    dot = lambda a, b: jnp.dot(a, b, preferred_element_type=F32)
+    both = dot(jnp.concatenate([high, low]), high_ref[...])
+    total = (both[STEPS:] + dot(high, low_ref[...])) + both[0:STEPS]
+    ngy = out_ref.shape[0] // 2
+    for core in range(2):
+        for j in range(ngy):
+            at = (2 * j + core) * 128
+            out_ref[core * ngy + j] = total[:, at : at + 128]
+
+
+def total_kernel(part_ref, out_ref):
+    total = jnp.sum(part_ref[...], axis=0)
     for k in range(out_ref.shape[0]):
         out_ref[k] = total
-
-
-def total_kernel(part_ref, out_ref):
-    out_ref[...] = jnp.sum(part_ref[...], axis=0)
 
 
 def spectra_kernel(scale, bin_total, trace_ref, other_ref, spec_ref, out_ref):
@@ -259,10 +288,13 @@
     turn = (step_of * bin_of).astype(F32)
     turn = turn - period * jnp.floor(turn * (1.0 / period))
     sin_t, cos_t = sin_cos_turns(turn * (1.0 / period))
-    traces = (trace_ref[...] + other_ref[...]) * F32(scale)
-    dot = lambda a: jnp.dot(a, traces, preferred_element_type=F32, precision=lax.Precision.HIGHEST)
-    out_ref[0] = spec_ref[0] + dot(cos_t)
-    out_ref[1] = spec_ref[1] - dot(sin_t)
+    dot = lambda a, b: jnp.dot(a, b, preferred_element_type=F32, precision=lax.Precision.HIGHEST)
+    core = lax.axis_index("gx") % 2
+    for traces, half in ((trace_ref[0], core), (other_ref[0], 1 - core)):
+        at = pl.ds(pl.multiple_of(half * 128, 128), 128)
+        traces = traces * F32(scale)
+        out_ref[0, :, at] = spec_ref[0, :, at] + dot(cos_t, traces)
+        out_ref[1, :, at] = spec_ref[1, :, at] - dot(sin_t, traces)
 
 
 def swap(odd_even, even_odd, axis):
@@ -312,18 +344,20 @@
     own = exchange_y(2, *state)
     *own, third = call(window("wide"), between, scratch(wide), name="window_wide")(*exchange_x(*own), p, q, r)
     current, before, series = call(
-        window("last"), [shape(*tile), shape(*tile), shape(ngy, STEPS + 8, 128)], scratch(thin), name="window_last"
+        window("last"), [shape(*tile), shape(*tile), shape(STEPS, 128)], scratch(thin), name="window_last"
     )(*exchange_x(*own), p4, q4, r4, first, second, third)
 
-    series = lax.all_to_all(series, "gy", 0, 0, tiled=True)
-    own = spectra_in.shape[2]
-    depth = ngx // 4
-    groups = [[half * 2 * depth + 2 * z + core for z in range(depth)] for half in range(2) for core in range(2)]
-    partial = call(lambda *refs: project_kernel(tx, ty, nz, own, *refs), shape(depth, STEPS, own), name="project")(series, angles)
-    partial = lax.all_to_all(partial, "gx", 0, 0, tiled=True, axis_index_groups=groups)
-    traces = call(total_kernel, shape(STEPS, own), name="total")(partial)
-    traces = traces + lax.ppermute(traces, "gx", [(i, i ^ 1) for i in range(ngx)])
-    other = lax.ppermute(traces, "gx", [(i, (i + 2 * depth) % ngx) for i in range(ngx)])
+    observers = angles.shape[1]
+    half = jax.ShapeDtypeStruct((128, observers), BF16)
+    high, low = call(lambda *refs: waves_kernel(tx, ty, nz, *refs), [half, half], name="waves")(cells, angles)
+    share = call(project_kernel, shape(2 * ngy, STEPS, 128), name="project")(series, high, low)
+    rows = [list(range(k, k + 2 * ngy)) for k in range(0, ngx * ngy, 2 * ngy)]
+    share = lax.all_to_all(share, ("gx", "gy"), 0, 0, tiled=True, axis_index_groups=rows)
+    share = call(total_kernel, shape(ngx // 2, STEPS, 128), name="row_total")(share)
+    chips = [list(range(core, ngx, 2)) for core in range(2)]
+    share = lax.all_to_all(share, "gx", 0, 0, tiled=True, axis_index_groups=chips)
+    traces = call(total_kernel, shape(1, STEPS, 128), name="total")(share)
+    other = lax.ppermute(traces, "gx", [(i, i ^ 1) for i in range(ngx)])
     scale = float(slot_cell.shape[0] * ngx * ngy) ** -0.5
     bins = spectra_in.shape[1] * ngx
     spectra = call(lambda *refs: spectra_kernel(scale, bins, *refs), shape(*spectra_in.shape), name="spectra")(

time: 144 us -> 139 us (0.965)
  waiting for transfers between devices: 33.7 us -> 29.5 us
    ppermute x2 -> x1, waiting for transfers between devices: 3.15 us -> 0.81 us  [body(): other = lax.ppermute(traces, 'gx', [(i, i ^ 1) for i in range(ngx)])]
    ppermute x6, waiting for transfers between devices: 19.3 us -> 17.4 us  [swap(): got = lax.ppermute(odd_even, axis, pairs)]
    ppermute x2 -> x1, starting transfers between devices: 5.98 us -> 5.32 us  [body(): other = lax.ppermute(traces, 'gx', [(i, i ^ 1) for i in range(ngx)])]
    pallas_call x3 -> x5, Pallas kernels: 4.35 us -> 4.8 us  [the longest x1 2.33 us: body(): call(window('last'), [shape(*tile), shape(*tile), shape(STEPS, 128)], scr...]
  transfers between devices with their start and end apart: 14 -> 13, of which waited for: 8 -> 7; matrix products, arithmetic and copies ran while one was open for 0% -> 0% of each run, Pallas kernels for 0% -> 1%
where the time goes in v5:
time: 139 us; the launch traced here: 138 us
  blocking collectives  50 us (36%)
  starting transfers between devices  44.3 us (32%)
  waiting for transfers between devices  29.5 us (21%)
  Pallas kernels  13.5 us (10%)
    all_to_all x1, blocking collectives, body(): lax.all_to_all(share, 'gx', 0, 0, tiled=True, axis_index_groups=chips)  26.9 us
    all_to_all x1, blocking collectives, body(): lax.all_to_all(share, ('gx', 'gy'), 0, 0, tiled=True, axis_index_groups=r...  23.1 us
    ppermute x6, starting transfers between devices, swap(): lax.ppermute(even_odd, axis, [(i, i ^ 1) for i in range(count) if i ^ 1 <...  23.1 us
    ppermute x6, waiting for transfers between devices, swap(): got = lax.ppermute(odd_even, axis, pairs)  17.4 us
    ppermute x6, starting transfers between devices, swap(): got = lax.ppermute(odd_even, axis, pairs)  15.9 us
    ppermute x6, waiting for transfers between devices, swap(): lax.ppermute(even_odd, axis, [(i, i ^ 1) for i in range(count) if i ^ 1 <...  11.3 us
    ppermute x1, starting transfers between devices, body(): other = lax.ppermute(traces, 'gx', [(i, i ^ 1) for i in range(ngx)])  5.32 us
  transfers between devices with their start and end apart: 13, of which 7 were waited for; matrix products, arithmetic and copies ran while one was open for 0% of the time, Pallas kernels for 1%

profile of v5, /device:TPU:1, one launch (start us, length us, event | category | flops | bytes accessed | tf_op | source)
XLA Modules:
  0.0 138.3 jit_solution(11846080529449128263)
XLA Ops:
  2.5 9.8 %collective-permute-start.1 = (f32[12,8,384]{2,1,0:T(8,128)S(1)}, f32[12,8,384]{2,1,0:T(8,128)S(1)}, u32[]{:S(2)}, u32[]{:S(2)}) collective-permute-start(f32[12,8,384]{2,1,0:T(8,128)S(1)} %get-tuple-element.37), channel_id=1, source_target_pairs={{0,1},{1,0},{2,3},{3,2},{4,5},{5,4},{6,7},{7,6},{8,9},{9,8},{10,11... | collective-permute-start | bytes 442376 | tf_op jit(solution)/shard_map/ppermute | solution.py:304
  12.3 6.3 %collective-permute-done.1.refs_2_ = f32[12,8,384]{2,1,0:T(8,128)S(1)} collective-permute-done((f32[12,8,384]{2,1,0:T(8,128)S(1)}, f32[12,8,384]{2,1,0:T(8,128)S(1)}, u32[]{:S(2)}, u32[]{:S(2)}) %collective-permute-start.1) | collective-permute-done | bytes 147488 | tf_op jit(solution)/shard_map/ppermute | solution.py:304
  18.8 5.5 %collective-permute-start.2 = (f32[63,8,384]{2,1,0:T(8,128)S(1)}, f32[63,8,384]{2,1,0:T(8,128)S(1)}, u32[]{:S(2)}, u32[]{:S(2)}) collective-permute-start(f32[63,8,384]{2,1,0:T(8,128)S(1)} %get-tuple-element.39), channel_id=1, source_target_pairs={{16,32},{32,16},{48,64},{64,48},{80,96},{96,80},{112,128},{128,112... | collective-permute-start | bytes 2322440 | tf_op jit(solution)/shard_map/ppermute | solution.py:303
  24.3 1.9 %collective-permute-start.3 = (f32[63,8,384]{2,1,0:T(8,128)S(1)}, f32[63,8,384]{2,1,0:T(8,128)S(1)}, u32[]{:S(2)}, u32[]{:S(2)}) collective-permute-start(f32[63,8,384]{2,1,0:T(8,128)S(1)} %get-tuple-element.40), channel_id=1, source_target_pairs={{0,16},{16,0},{32,48},{48,32},{64,80},{80,64},{96,112},{112,96},{1... | collective-permute-start | bytes 2322440 | tf_op jit(solution)/shard_map/ppermute | solution.py:304
  26.4 7.5 %collective-permute-done.2.refs_1_ = f32[63,8,384]{2,1,0:T(8,128)S(1)} collective-permute-done((f32[63,8,384]{2,1,0:T(8,128)S(1)}, f32[63,8,384]{2,1,0:T(8,128)S(1)}, u32[]{:S(2)}, u32[]{:S(2)}) %collective-permute-start.2) | collective-permute-done | bytes 774176 | tf_op jit(solution)/shard_map/ppermute | solution.py:303
  33.9 2.7 %window_first.1 = (f32[10,40,384]{2,1,0:T(8,128)S(1)}, f32[28,8,384]{2,1,0:T(8,128)S(1)}, f32[28,8,384]{2,1,0:T(8,128)S(1)}, f32[4,128]{1,0:T(4,128)S(1)}, f32[1...) custom-call(f32[12,48,384]{2,1,0:T(8,128)S(1)} %get-tuple-element.38, ...), custom_call_target="tpu_custom_call" | custom-call | tf_op jit(solution)/shard_map/window_first/pallas_call | solution.py:338
  36.6 3.6 %collective-permute-start.4 = (f32[28,8,384]{2,1,0:T(8,128)S(1)}, f32[28,8,384]{2,1,0:T(8,128)S(1)}, u32[]{:S(2)}, u32[]{:S(2)}) collective-permute-start(f32[28,8,384]{2,1,0:T(8,128)S(1)} %get-tuple-element.42), channel_id=1, source_target_pairs={{16,32},{32,16},{48,64},{64,48},{80,96},{96,80},{112,128},{128,112... | collective-permute-start | bytes 1032200 | tf_op jit(solution)/shard_map/ppermute | solution.py:303
  40.2 1.9 %collective-permute-start.5 = (f32[28,8,384]{2,1,0:T(8,128)S(1)}, f32[28,8,384]{2,1,0:T(8,128)S(1)}, u32[]{:S(2)}, u32[]{:S(2)}) collective-permute-start(f32[28,8,384]{2,1,0:T(8,128)S(1)} %get-tuple-element.43), channel_id=1, source_target_pairs={{0,16},{16,0},{32,48},{48,32},{64,80},{80,64},{96,112},{112,96},{1... | collective-permute-start | bytes 1032200 | tf_op jit(solution)/shard_map/ppermute | solution.py:304
  42.1 3.0 %collective-permute-done.4.refs_1_ = f32[28,8,384]{2,1,0:T(8,128)S(1)} collective-permute-done((f32[28,8,384]{2,1,0:T(8,128)S(1)}, f32[28,8,384]{2,1,0:T(8,128)S(1)}, u32[]{:S(2)}, u32[]{:S(2)}) %collective-permute-start.4) | collective-permute-done | bytes 344096 | tf_op jit(solution)/shard_map/ppermute | solution.py:303
  45.1 1.8 %window_inner.1 = (f32[10,32,384]{2,1,0:T(8,128)S(1)}, f32[8,8,384]{2,1,0:T(8,128)S(1)}, f32[8,8,384]{2,1,0:T(8,128)S(1)}, f32[4,128]{1,0:T(4,128)S(1)}) custom-call(f32[10,40,384]{2,1,0:T(8,128)S(1)} %get-tuple-element.41.refs_0_, f32[28,8,384]{2,1,0:T(8,128)S(1)} %collective-permute-done.4.refs_1_, f32[28,8,384]{2,1,0:T(8,128)S(1)} %collective-permute-done.5.refs_2_, ...), custom_call_target="tpu_custom_call" | custom-call | tf_op jit(solution)/shard_map/window_inner/pallas_call | solution.py:341
  47.6 5.6 %collective-permute-start.7 = (f32[8,8,384]{2,1,0:T(8,128)S(1)}, f32[8,8,384]{2,1,0:T(8,128)S(1)}, u32[]{:S(2)}, u32[]{:S(2)}) collective-permute-start(f32[8,8,384]{2,1,0:T(8,128)S(1)} %get-tuple-element.49), channel_id=1, source_target_pairs={{0,1},{1,0},{2,3},{3,2},{4,5},{5,4},{6,7},{7,6},{8,9},{9,8},{10,11... | collective-permute-start | bytes 294920 | tf_op jit(solution)/shard_map/ppermute | solution.py:304
  53.2 5.0 %collective-permute-done.7.refs_2_ = f32[8,8,384]{2,1,0:T(8,128)S(1)} collective-permute-done((f32[8,8,384]{2,1,0:T(8,128)S(1)}, f32[8,8,384]{2,1,0:T(8,128)S(1)}, u32[]{:S(2)}, u32[]{:S(2)}) %collective-permute-start.7) | collective-permute-done | bytes 98336 | tf_op jit(solution)/shard_map/ppermute | solution.py:304
  58.3 2.7 %collective-permute-start.8 = (f32[36,8,384]{2,1,0:T(8,128)S(1)}, f32[36,8,384]{2,1,0:T(8,128)S(1)}, u32[]{:S(2)}, u32[]{:S(2)}) collective-permute-start(f32[36,8,384]{2,1,0:T(8,128)S(1)} %get-tuple-element.51), channel_id=1, source_target_pairs={{16,32},{32,16},{48,64},{64,48},{80,96},{96,80},{112,128},{128,112... | collective-permute-start | bytes 1327112 | tf_op jit(solution)/shard_map/ppermute | solution.py:303
  61.0 1.9 %collective-permute-start.9 = (f32[36,8,384]{2,1,0:T(8,128)S(1)}, f32[36,8,384]{2,1,0:T(8,128)S(1)}, u32[]{:S(2)}, u32[]{:S(2)}) collective-permute-start(f32[36,8,384]{2,1,0:T(8,128)S(1)} %get-tuple-element.52), channel_id=1, source_target_pairs={{0,16},{16,0},{32,48},{48,32},{64,80},{80,64},{96,112},{112,96},{1... | collective-permute-start | bytes 1327112 | tf_op jit(solution)/shard_map/ppermute | solution.py:304
  62.9 5.0 %collective-permute-done.8.refs_1_ = f32[36,8,384]{2,1,0:T(8,128)S(1)} collective-permute-done((f32[36,8,384]{2,1,0:T(8,128)S(1)}, f32[36,8,384]{2,1,0:T(8,128)S(1)}, u32[]{:S(2)}, u32[]{:S(2)}) %collective-permute-start.8) | collective-permute-done | bytes 442400 | tf_op jit(solution)/shard_map/ppermute | solution.py:303
  67.9 2.0 %window_wide.1 = (f32[10,40,384]{2,1,0:T(8,128)S(1)}, f32[28,8,384]{2,1,0:T(8,128)S(1)}, f32[28,8,384]{2,1,0:T(8,128)S(1)}, f32[4,128]{1,0:T(4,128)S(1)}) custom-call(f32[10,48,384]{2,1,0:T(8,128)S(1)} %get-tuple-element.50.refs_0_, f32[36,8,384]{2,1,0:T(8,128)S(1)} %collective-permute-done.8.refs_1_, f32[36,8,384]{2,1,0:T(8,128)S(1)} %collective-permute-done.9.refs_2_, ...), custom_call_target="tpu_custom_call" | custom-call | tf_op jit(solution)/shard_map/window_wide/pallas_call | solution.py:345
  69.9 2.7 %collective-permute-start.10 = (f32[28,8,384]{2,1,0:T(8,128)S(1)}, f32[28,8,384]{2,1,0:T(8,128)S(1)}, u32[]{:S(2)}, u32[]{:S(2)}) collective-permute-start(f32[28,8,384]{2,1,0:T(8,128)S(1)} %get-tuple-element.57), channel_id=1, source_target_pairs={{16,32},{32,16},{48,64},{64,48},{80,96},{96,80},{112,128},{128,112... | collective-permute-start | bytes 1032200 | tf_op jit(solution)/shard_map/ppermute | solution.py:303
  72.6 1.9 %collective-permute-start.11 = (f32[28,8,384]{2,1,0:T(8,128)S(1)}, f32[28,8,384]{2,1,0:T(8,128)S(1)}, u32[]{:S(2)}, u32[]{:S(2)}) collective-permute-start(f32[28,8,384]{2,1,0:T(8,128)S(1)} %get-tuple-element.58), channel_id=1, source_target_pairs={{0,16},{16,0},{32,48},{48,32},{64,80},{80,64},{96,112},{112,96},{1... | collective-permute-start | bytes 1032200 | tf_op jit(solution)/shard_map/ppermute | solution.py:304
  74.5 2.0 %waves.1 = (bf16[128,4096]{1,0:T(8,128)(2,1)S(1)}, bf16[128,4096]{1,0:T(8,128)(2,1)S(1)}) custom-call(s32[1,128]{1,0:T(1,128)S(1)} %add_bitcast_fusion.refs_3_.refs_0_, f32[2,4096]{1,0:T(2,128)S(1)} %copy-done), custom_call_target="tpu_custom_call" | custom-call | tf_op jit(solution)/shard_map/waves/pallas_call | solution.py:352
  76.6 1.9 %collective-permute-done.10.refs_1_ = f32[28,8,384]{2,1,0:T(8,128)S(1)} collective-permute-done((f32[28,8,384]{2,1,0:T(8,128)S(1)}, f32[28,8,384]{2,1,0:T(8,128)S(1)}, u32[]{:S(2)}, u32[]{:S(2)}) %collective-permute-start.10) | collective-permute-done | bytes 344096 | tf_op jit(solution)/shard_map/ppermute | solution.py:303
  78.5 2.3 %window_last.1 = (f32[4,32,384]{2,1,0:T(8,128)}, f32[4,32,384]{2,1,0:T(8,128)}, f32[16,128]{1,0:T(8,128)S(1)}) custom-call(f32[10,40,384]{2,1,0:T(8,128)S(1)} %get-tuple-element.56.refs_0_, f32[28,8,384]{2,1,0:T(8,128)S(1)} %collective-permute-done.10.refs_1_, f32[28,8,384]{2,1,0:T(8,128)S(1)} %collective-permute-done.11.refs_2_, ...), custom_call_target="tpu_custom_call" | custom-call | tf_op jit(solution)/shard_map/window_last/pallas_call | solution.py:346
  81.2 23.1 %all_to_all.10.part_ref = f32[32,16,128]{2,1,0:T(8,128)S(1)} all-to-all(f32[32,16,128]{2,1,0:T(8,128)S(1)} %project.1), channel_id=1, replica_groups={{0,1,2,3,4,5,6,7,8,9,10,11,12,13,14,15,16,17,18,19,20,21,22,23,24,25,26..., dimensions={0} | all-to-all | bytes 524288 | tf_op jit(solution)/shard_map/all_to_all | solution.py:355
  104.4 26.9 %all_to_all.11.part_ref = f32[24,16,128]{2,1,0:T(8,128)S(1)} all-to-all(f32[24,16,128]{2,1,0:T(8,128)S(1)} %row_total.1), channel_id=1, replica_groups={{0,32,64,96,128,160,192,224,256,288,320,352,384,416,448,480,512,544,576..., dimensions={0} | all-to-all | bytes 393216 | tf_op jit(solution)/shard_map/all_to_all | solution.py:358
  131.3 5.3 %collective-permute-start.12 = (f32[1,16,128]{2,1,0:T(8,128)S(1)}, f32[1,16,128]{2,1,0:T(8,128)S(1)}, u32[]{:S(2)}, u32[]{:S(2)}) collective-permute-start(f32[1,16,128]{2,1,0:T(8,128)S(1)} %total.1.refs_0_), channel_id=1, source_target_pairs={{0,16},{16,0},{32,48},{48,32},{64,80},{80,64},{96,112},{112,96},{1... | collective-permute-start | bytes 24584 | tf_op jit(solution)/shard_map/ppermute | solution.py:360
  (23 shorter events, 5.0 us)
Async XLA Ops:
  1.8 10.5 %collective-permute-start = (f32[12,8,384]{2,1,0:T(8,128)S(1)}, f32[12,8,384]{2,1,0:T(8,128)S(1)}, u32[]{:S(2)}, u32[]{:S(2)}) collective-permute-start(f32[12,8,384]{2,1,0:T(8,128)S(1)} %get-tuple-element.36), channel_id=1, source_target_pairs={{1,2},{2,1},{3,4},{4,3},{5,6},{6,5},{7,8},{8,7},{9,10},{10,9},{11,... | collective-permute-start | bytes 442376 | tf_op jit(solution)/shard_map/ppermute | solution.py:303
  2.5 16.2 %collective-permute-start.1 = (f32[12,8,384]{2,1,0:T(8,128)S(1)}, f32[12,8,384]{2,1,0:T(8,128)S(1)}, u32[]{:S(2)}, u32[]{:S(2)}) collective-permute-start(f32[12,8,384]{2,1,0:T(8,128)S(1)} %get-tuple-element.37), channel_id=1, source_target_pairs={{0,1},{1,0},{2,3},{3,2},{4,5},{5,4},{6,7},{7,6},{8,9},{9,8},{10,11... | collective-permute-start | bytes 442376 | tf_op jit(solution)/shard_map/ppermute | solution.py:304
  18.8 7.4 %copy-start.2 = (s32[64]{0:T(128)S(1)}, s32[64]{0:T(128)}, u32[]{:S(2)}) copy-start(s32[64]{0:T(128)} %param.9) | copy-start | bytes 772
  18.8 15.0 %collective-permute-start.2 = (f32[63,8,384]{2,1,0:T(8,128)S(1)}, f32[63,8,384]{2,1,0:T(8,128)S(1)}, u32[]{:S(2)}, u32[]{:S(2)}) collective-permute-start(f32[63,8,384]{2,1,0:T(8,128)S(1)} %get-tuple-element.39), channel_id=1, source_target_pairs={{16,32},{32,16},{48,64},{64,48},{80,96},{96,80},{112,128},{128,112... | collective-permute-start | bytes 2322440 | tf_op jit(solution)/shard_map/ppermute | solution.py:303
  24.3 9.5 %collective-permute-start.3 = (f32[63,8,384]{2,1,0:T(8,128)S(1)}, f32[63,8,384]{2,1,0:T(8,128)S(1)}, u32[]{:S(2)}, u32[]{:S(2)}) collective-permute-start(f32[63,8,384]{2,1,0:T(8,128)S(1)} %get-tuple-element.40), channel_id=1, source_target_pairs={{0,16},{16,0},{32,48},{48,32},{64,80},{80,64},{96,112},{112,96},{1... | collective-permute-start | bytes 2322440 | tf_op jit(solution)/shard_map/ppermute | solution.py:304
  36.6 8.6 %collective-permute-start.4 = (f32[28,8,384]{2,1,0:T(8,128)S(1)}, f32[28,8,384]{2,1,0:T(8,128)S(1)}, u32[]{:S(2)}, u32[]{:S(2)}) collective-permute-start(f32[28,8,384]{2,1,0:T(8,128)S(1)} %get-tuple-element.42), channel_id=1, source_target_pairs={{16,32},{32,16},{48,64},{64,48},{80,96},{96,80},{112,128},{128,112... | collective-permute-start | bytes 1032200 | tf_op jit(solution)/shard_map/ppermute | solution.py:303
  40.2 4.9 %collective-permute-start.5 = (f32[28,8,384]{2,1,0:T(8,128)S(1)}, f32[28,8,384]{2,1,0:T(8,128)S(1)}, u32[]{:S(2)}, u32[]{:S(2)}) collective-permute-start(f32[28,8,384]{2,1,0:T(8,128)S(1)} %get-tuple-element.43), channel_id=1, source_target_pairs={{0,16},{16,0},{32,48},{48,32},{64,80},{80,64},{96,112},{112,96},{1... | collective-permute-start | bytes 1032200 | tf_op jit(solution)/shard_map/ppermute | solution.py:304
  46.9 6.3 %collective-permute-start.6 = (f32[8,8,384]{2,1,0:T(8,128)S(1)}, f32[8,8,384]{2,1,0:T(8,128)S(1)}, u32[]{:S(2)}, u32[]{:S(2)}) collective-permute-start(f32[8,8,384]{2,1,0:T(8,128)S(1)} %get-tuple-element.48), channel_id=1, source_target_pairs={{1,2},{2,1},{3,4},{4,3},{5,6},{6,5},{7,8},{8,7},{9,10},{10,9},{11,... | collective-permute-start | bytes 294920 | tf_op jit(solution)/shard_map/ppermute | solution.py:303
  47.6 10.6 %collective-permute-start.7 = (f32[8,8,384]{2,1,0:T(8,128)S(1)}, f32[8,8,384]{2,1,0:T(8,128)S(1)}, u32[]{:S(2)}, u32[]{:S(2)}) collective-permute-start(f32[8,8,384]{2,1,0:T(8,128)S(1)} %get-tuple-element.49), channel_id=1, source_target_pairs={{0,1},{1,0},{2,3},{3,2},{4,5},{5,4},{6,7},{7,6},{8,9},{9,8},{10,11... | collective-permute-start | bytes 294920 | tf_op jit(solution)/shard_map/ppermute | solution.py:304
  58.3 9.6 %collective-permute-start.8 = (f32[36,8,384]{2,1,0:T(8,128)S(1)}, f32[36,8,384]{2,1,0:T(8,128)S(1)}, u32[]{:S(2)}, u32[]{:S(2)}) collective-permute-start(f32[36,8,384]{2,1,0:T(8,128)S(1)} %get-tuple-element.51), channel_id=1, source_target_pairs={{16,32},{32,16},{48,64},{64,48},{80,96},{96,80},{112,128},{128,112... | collective-permute-start | bytes 1327112 | tf_op jit(solution)/shard_map/ppermute | solution.py:303
  61.0 6.9 %collective-permute-start.9 = (f32[36,8,384]{2,1,0:T(8,128)S(1)}, f32[36,8,384]{2,1,0:T(8,128)S(1)}, u32[]{:S(2)}, u32[]{:S(2)}) collective-permute-start(f32[36,8,384]{2,1,0:T(8,128)S(1)} %get-tuple-element.52), channel_id=1, source_target_pairs={{0,16},{16,0},{32,48},{48,32},{64,80},{80,64},{96,112},{112,96},{1... | collective-permute-start | bytes 1327112 | tf_op jit(solution)/shard_map/ppermute | solution.py:304
  67.9 6.6 %copy-start = (f32[2,4096]{1,0:T(2,128)S(1)}, f32[2,4096]{1,0:T(2,128)}, u32[]{:S(2)}) copy-start(f32[2,4096]{1,0:T(2,128)} %refs_1_.1) | copy-start | bytes 98308
  69.9 8.6 %collective-permute-start.10 = (f32[28,8,384]{2,1,0:T(8,128)S(1)}, f32[28,8,384]{2,1,0:T(8,128)S(1)}, u32[]{:S(2)}, u32[]{:S(2)}) collective-permute-start(f32[28,8,384]{2,1,0:T(8,128)S(1)} %get-tuple-element.57), channel_id=1, source_target_pairs={{16,32},{32,16},{48,64},{64,48},{80,96},{96,80},{112,128},{128,112... | collective-permute-start | bytes 1032200 | tf_op jit(solution)/shard_map/ppermute | solution.py:303
  72.6 5.9 %collective-permute-start.11 = (f32[28,8,384]{2,1,0:T(8,128)S(1)}, f32[28,8,384]{2,1,0:T(8,128)S(1)}, u32[]{:S(2)}, u32[]{:S(2)}) collective-permute-start(f32[28,8,384]{2,1,0:T(8,128)S(1)} %get-tuple-element.58), channel_id=1, source_target_pairs={{0,16},{16,0},{32,48},{48,32},{64,80},{80,64},{96,112},{112,96},{1... | collective-permute-start | bytes 1032200 | tf_op jit(solution)/shard_map/ppermute | solution.py:304
  131.3 6.2 %copy-start.1 = (f32[2,8,256]{2,1,0:T(8,128)S(1)}, f32[2,8,256]{2,1,0:T(8,128)}, u32[]{:S(2)}) copy-start(f32[2,8,256]{2,1,0:T(8,128)} %refs_2_.1) | copy-start | bytes 49156
  131.3 6.1 %collective-permute-start.12 = (f32[1,16,128]{2,1,0:T(8,128)S(1)}, f32[1,16,128]{2,1,0:T(8,128)S(1)}, u32[]{:S(2)}, u32[]{:S(2)}) collective-permute-start(f32[1,16,128]{2,1,0:T(8,128)S(1)} %total.1.refs_0_), channel_id=1, source_target_pairs={{0,16},{16,0},{32,48},{48,32},{64,80},{80,64},{96,112},{112,96},{1... | collective-permute-start | bytes 24584 | tf_op jit(solution)/shard_map/ppermute | solution.py:360

commit v6 on v5

--- a/solution.py
+++ b/solution.py
@@ -39,7 +39,7 @@
             ref[k * tx : (k + 1) * tx] = state[lo:hi, pl.ds(pl.multiple_of(row, 8), Y)]
 
 
-def prepare_kernel(cur_hbm, bef_hbm, mat_hbm, state_ref, odd_even_ref, even_odd_ref, cur_ref, bef_ref, mat_ref, sems):
+def prepare_kernel(cur_hbm, bef_hbm, mat_hbm, state_ref, y_b, y_a, x_b, x_a, cur_ref, bef_ref, mat_ref, sems):
     tx, ty, _ = cur_ref.shape
     pairs = ((mat_hbm, mat_ref), (cur_hbm, cur_ref), (bef_hbm, bef_ref))
     copies = [pltpu.make_async_copy(src, dst, sems.at[k]) for k, (src, dst) in enumerate(pairs)]
@@ -52,7 +52,8 @@
     state_ref[0:tx] = jnp.where(mat == 1, 0.0, cur_ref[...])
     copies[2].wait()
     state_ref[tx : 2 * tx] = jnp.where(mat == 1, 0.0, bef_ref[...])
-    write_edges(state_ref, odd_even_ref, even_odd_ref, 3, tx, ty)
+    write_edges(state_ref, y_b, y_a, 3, tx, ty)
+    write_messages(state_ref, x_b, x_a, split_tiles(3, tx, ty, 2 * W)[0], 3, tx, ty)
 
 
 def message_tiles(fields, tx, ty, reach):
@@ -71,11 +72,20 @@
     return tiles
 
 
-def write_messages(own, b_ref, a_ref, fields, tx, ty, reach):
+def split_tiles(fields, tx, ty, reach):
+    tiles = message_tiles(fields, tx, ty, reach)
+    return [t for t in tiles if t[2] < ty], [t for t in tiles if t[2] >= ty]
+
+
+def joined_tiles(fields, tx, ty):
+    return split_tiles(fields, tx, ty, 2 * W)[1] if fields == 3 else message_tiles(fields, tx, ty, 2 * W)
+
+
+def write_messages(own, b_ref, a_ref, tiles, fields, tx, ty):
     odd = lax.axis_index("gx") % 2
     wide = own.shape[1] == ty + 16
     low = lax.broadcasted_iota(jnp.int32, (8, own.shape[2]), 0) < 4
-    for k, (field, d, row, packed) in enumerate(message_tiles(fields, tx, ty, reach)):
+    for k, (field, d, row, packed) in enumerate(tiles):
         for ref, below in ((a_ref, odd), (b_ref, 1 - odd)):
             plane = plane_sets(fields, tx)[field][0] + below * (d - 1) + (1 - below) * (tx - d)
             tile = own[plane, row : row + 8]
@@ -84,10 +94,10 @@
             ref[k] = tile
 
 
-def read_messages(targets, b_ref, a_ref, tx, ty, reach):
+def read_messages(targets, b_ref, a_ref, tiles, tx, ty):
     odd = lax.axis_index("gx") % 2
     wide = targets[0].shape[1] == ty + 16
-    for k, (field, d, row, packed) in enumerate(message_tiles(len(targets), tx, ty, reach)):
+    for k, (field, d, row, packed) in enumerate(tiles):
         for ref, below in ((a_ref, odd), (b_ref, 1 - odd)):
             plane = below * (tx - d) + (1 - below) * (2 * tx + d - 1)
             tile = ref[k]
@@ -102,7 +112,7 @@
     for ref, row in ((y_a, ty + 8 * odd), (y_b, ty + 8 - 8 * odd)):
         for k, (lo, hi) in enumerate(plane_sets(fields, tx)):
             own_ref[lo:hi, pl.ds(pl.multiple_of(row, 8), 8)] = ref[k * tx : (k + 1) * tx]
-    write_messages(own_ref, odd_even_ref, even_odd_ref, fields, tx, ty, 2 * W)
+    write_messages(own_ref, odd_even_ref, even_odd_ref, joined_tiles(fields, tx, ty), fields, tx, ty)
 
 
 def around(plane, x):
@@ -155,6 +165,7 @@
     refs = list(refs)
     take = lambda n: [refs.pop(0) for _ in range(n)]
     own, x_b, x_a = take(3)
+    from_y = take(2) if kind == "first" else ()
     (cell_row,) = take(1)
     if kind != "first":
         coefs = take(3)
@@ -176,8 +187,11 @@
     else:
         one[tx : 2 * tx] = own[0:tx]
         two[tx - 1 : 2 * tx + 1] = own[tx:]
-    reach = 2 * W if kind in ("first", "wide") else W
-    read_messages(targets, x_b, x_a, tx, ty, reach)
+    if from_y:
+        for pair, tiles in zip(((x_b, x_a), from_y), split_tiles(len(targets), tx, ty, 2 * W)):
+            read_messages(targets, *pair, tiles, tx, ty)
+    else:
+        read_messages(targets, x_b, x_a, message_tiles(2, tx, ty, 2 * W if kind == "wide" else W), tx, ty)
     if kind == "first":
         for k in (0, 1):
             coefs[k][...] = jnp.zeros(coefs[k].shape, F32)
@@ -222,7 +236,7 @@
     if kind == "inner":
         write_edges(state_ref, *rest, 2, tx, ty)
     else:
-        write_messages(state_ref, *rest, 2, tx, ty, W)
+        write_messages(state_ref, *rest, message_tiles(2, tx, ty, W), 2, tx, ty)
 
 
 def sin_cos_turns(p):
@@ -288,13 +302,21 @@
     turn = (step_of * bin_of).astype(F32)
     turn = turn - period * jnp.floor(turn * (1.0 / period))
     sin_t, cos_t = sin_cos_turns(turn * (1.0 / period))
-    dot = lambda a, b: jnp.dot(a, b, preferred_element_type=F32, precision=lax.Precision.HIGHEST)
+    waves = jnp.concatenate([cos_t, -sin_t])
+    wave_high = waves.astype(BF16)
+    wave_low = (waves - wave_high.astype(F32)).astype(BF16)
+    wave_both = jnp.concatenate([wave_high, wave_low])
+    dot = lambda a, b: jnp.dot(a, b, preferred_element_type=F32)
     core = lax.axis_index("gx") % 2
     for traces, half in ((trace_ref[0], core), (other_ref[0], 1 - core)):
         at = pl.ds(pl.multiple_of(half * 128, 128), 128)
         traces = traces * F32(scale)
-        out_ref[0, :, at] = spec_ref[0, :, at] + dot(cos_t, traces)
-        out_ref[1, :, at] = spec_ref[1, :, at] - dot(sin_t, traces)
+        high = traces.astype(BF16)
+        low = (traces - high.astype(F32)).astype(BF16)
+        both = dot(wave_both, high)
+        added = both[0 : 2 * bins] + (both[2 * bins :] + dot(wave_high, low))
+        out_ref[0, :, at] = spec_ref[0, :, at] + added[0:bins]
+        out_ref[1, :, at] = spec_ref[1, :, at] + added[bins:]
 
 
 def swap(odd_even, even_odd, axis):
@@ -312,37 +334,44 @@
     wide, thin = (3 * tx, ty + 2 * Y, nz), (3 * tx, ty + 2 * W, nz)
     scratch = lambda s: [pltpu.VMEM(s, F32)] * 2
 
-    def exchange_y(fields, state, *edges):
-        size = shape(len(message_tiles(fields, tx, ty, 2 * W)), 8, nz)
-        return call(
+    def count(tiles):
+        return shape(len(tiles), 8, nz)
+
+    def exchange_both(fields, state, y_b, y_a, *own_rows):
+        y_rows = swap(y_b, y_a, "gy")
+        ahead = swap(*own_rows, "gx") if own_rows else ()
+        size = count(joined_tiles(fields, tx, ty))
+        own, x_b, x_a = call(
             lambda *refs: join_kernel(fields, tx, ty, *refs), [shape(*state.shape[:1], *wide[1:]), size, size], name="join"
-        )(state, *swap(*edges, "gy"))
+        )(state, *y_rows)
+        return [own, *ahead, *swap(x_b, x_a, "gx"), cells]
 
     def exchange_x(own, *messages):
         return [own, *swap(*messages, "gx"), cells]
 
     cells = jnp.concatenate([slot_cell, slot_cell])[None, :]
-    tile, edge = (tx, ty, nz), (tx, Y, nz)
+    tile = (tx, ty, nz)
     hbm = pl.BlockSpec(memory_space=pltpu.HBM)
     state = call(
         prepare_kernel,
-        [shape(3 * tx, ty, nz), shape(3 * tx, Y, nz), shape(3 * tx, Y, nz)],
+        [shape(3 * tx, ty, nz)] + [shape(3 * tx, Y, nz)] * 2 + [count(split_tiles(3, tx, ty, 2 * W)[0])] * 2,
         [pltpu.VMEM(tile, F32), pltpu.VMEM(tile, F32), pltpu.VMEM(tile, jnp.int32), pltpu.SemaphoreType.DMA((3,))],
         name="prepare",
         specs=[hbm] * 3,
     )(*(pltpu.with_memory_space_constraint(v, pltpu.HBM) for v in (pressure, previous, material)))
-    own = exchange_y(3, *state)
     part = shape(W, 128)
-    message = shape(len(message_tiles(2, tx, ty, W)), 8, nz)
+    message = count(message_tiles(2, tx, ty, W))
     between = [shape(2 * tx + 2, *thin[1:]), message, message, part]
     *own, first, p, q, r, p4, q4, r4 = call(
         window("first"), between + [shape(*wide)] * 3 + [shape(*thin)] * 3, scratch(wide), name="window_first"
-    )(*exchange_x(*own))
+    )(*exchange_both(3, *state))
     *state, second = call(
-        window("inner"), [shape(2 * tx + 2, ty, nz), shape(2 * tx, Y, nz), shape(2 * tx, Y, nz), part], scratch(thin), name="window_inner"
+        window("inner"),
+        [shape(2 * tx + 2, ty, nz)] + [shape(2 * tx, Y, nz)] * 2 + [part],
+        scratch(thin),
+        name="window_inner",
     )(*exchange_x(*own), p4, q4, r4)
-    own = exchange_y(2, *state)
-    *own, third = call(window("wide"), between, scratch(wide), name="window_wide")(*exchange_x(*own), p, q, r)
+    *own, third = call(window("wide"), between, scratch(wide), name="window_wide")(*exchange_both(2, *state), p, q, r)
     current, before, series = call(
         window("last"), [shape(*tile), shape(*tile), shape(STEPS, 128)], scratch(thin), name="window_last"
     )(*exchange_x(*own), p4, q4, r4, first, second, third)

time: 139 us -> 139 us (level)
  starting transfers between devices: 44.3 us -> 55.2 us
  waiting for transfers between devices: 29.5 us -> 19.7 us
    ppermute x6 -> x7, waiting for transfers between devices: 17.4 us -> 9.73 us  [swap(): got = lax.ppermute(odd_even, axis, pairs)]
    ppermute x6 -> x7, starting transfers between devices: 15.9 us -> 22.5 us  [swap(): got = lax.ppermute(odd_even, axis, pairs)]
    ppermute x6 -> x7, starting transfers between devices: 23.1 us -> 27 us  [swap(): lax.ppermute(even_odd, axis, [(i, i ^ 1) for i in range(count) if i ^ 1 <...]
    ppermute x6 -> x7, waiting for transfers between devices: 11.3 us -> 9.21 us  [swap(): lax.ppermute(even_odd, axis, [(i, i ^ 1) for i in range(count) if i ^ 1 <...]
    all_to_all x1, blocking collectives: 23.1 us -> 21.4 us  [body(): lax.all_to_all(share, ('gx', 'gy'), 0, 0, tiled=True, axis_index_groups=r...]
  transfers between devices with their start and end apart: 13 -> 15, of which waited for: 7 -> 7; matrix products, arithmetic and copies ran while one was open for 0% -> 0% of each run, Pallas kernels for 1% -> 2%
where the time goes in v6:
time: 139 us; the launch traced here: 138 us
  starting transfers between devices  55.2 us (40%)
  blocking collectives  49.1 us (35%)
  waiting for transfers between devices  19.7 us (14%)
  Pallas kernels  13.4 us (10%)
    all_to_all x1, blocking collectives, body(): lax.all_to_all(share, 'gx', 0, 0, tiled=True, axis_index_groups=chips)  27.7 us
    ppermute x7, starting transfers between devices, swap(): lax.ppermute(even_odd, axis, [(i, i ^ 1) for i in range(count) if i ^ 1 <...  27 us
    ppermute x7, starting transfers between devices, swap(): got = lax.ppermute(odd_even, axis, pairs)  22.5 us
    all_to_all x1, blocking collectives, body(): lax.all_to_all(share, ('gx', 'gy'), 0, 0, tiled=True, axis_index_groups=r...  21.4 us
    ppermute x7, waiting for transfers between devices, swap(): got = lax.ppermute(odd_even, axis, pairs)  9.73 us
    ppermute x7, waiting for transfers between devices, swap(): lax.ppermute(even_odd, axis, [(i, i ^ 1) for i in range(count) if i ^ 1 <...  9.21 us
    ppermute x1, starting transfers between devices, body(): other = lax.ppermute(traces, 'gx', [(i, i ^ 1) for i in range(ngx)])  5.66 us
  transfers between devices with their start and end apart: 15, of which 7 were waited for; matrix products, arithmetic and copies ran while one was open for 0% of the time, Pallas kernels for 2%

profile of v6, /device:TPU:1, one launch (start us, length us, event | category | flops | bytes accessed | tf_op | source)
XLA Modules:
  0.0 138.4 jit_solution(13978746240647980516)
XLA Ops:
  1.9 5.4 %collective-permute-start.2 = (f32[44,8,384]{2,1,0:T(8,128)S(1)}, f32[44,8,384]{2,1,0:T(8,128)S(1)}, u32[]{:S(2)}, u32[]{:S(2)}) collective-permute-start(f32[44,8,384]{2,1,0:T(8,128)S(1)} %get-tuple-element.41), channel_id=1, source_target_pairs={{16,32},{32,16},{48,64},{64,48},{80,96},{96,80},{112,128},{128,112... | collective-permute-start | bytes 1622024 | tf_op jit(solution)/shard_map/ppermute | solution.py:325
  7.3 7.7 %collective-permute-start.3 = (f32[44,8,384]{2,1,0:T(8,128)S(1)}, f32[44,8,384]{2,1,0:T(8,128)S(1)}, u32[]{:S(2)}, u32[]{:S(2)}) collective-permute-start(f32[44,8,384]{2,1,0:T(8,128)S(1)} %get-tuple-element.42), channel_id=1, source_target_pairs={{0,16},{16,0},{32,48},{48,32},{64,80},{80,64},{96,112},{112,96},{1... | collective-permute-start | bytes 1622024 | tf_op jit(solution)/shard_map/ppermute | solution.py:326
  15.7 3.2 %collective-permute-start.1 = (f32[12,8,384]{2,1,0:T(8,128)S(1)}, f32[12,8,384]{2,1,0:T(8,128)S(1)}, u32[]{:S(2)}, u32[]{:S(2)}) collective-permute-start(f32[12,8,384]{2,1,0:T(8,128)S(1)} %get-tuple-element.39), channel_id=1, source_target_pairs={{0,1},{1,0},{2,3},{3,2},{4,5},{5,4},{6,7},{7,6},{8,9},{9,8},{10,11... | collective-permute-start | bytes 442376 | tf_op jit(solution)/shard_map/ppermute | solution.py:326
  18.9 7.2 %collective-permute-done.1.refs_2_ = f32[12,8,384]{2,1,0:T(8,128)S(1)} collective-permute-done((f32[12,8,384]{2,1,0:T(8,128)S(1)}, f32[12,8,384]{2,1,0:T(8,128)S(1)}, u32[]{:S(2)}, u32[]{:S(2)}) %collective-permute-start.1) | collective-permute-done | bytes 147488 | tf_op jit(solution)/shard_map/ppermute | solution.py:326
  26.2 4.6 %collective-permute-start.4 = (f32[19,8,384]{2,1,0:T(8,128)S(1)}, f32[19,8,384]{2,1,0:T(8,128)S(1)}, u32[]{:S(2)}, u32[]{:S(2)}) collective-permute-start(f32[19,8,384]{2,1,0:T(8,128)S(1)} %get-tuple-element.43), channel_id=1, source_target_pairs={{16,32},{32,16},{48,64},{64,48},{80,96},{96,80},{112,128},{128,112... | collective-permute-start | bytes 700424 | tf_op jit(solution)/shard_map/ppermute | solution.py:325
  30.8 1.9 %collective-permute-start.5 = (f32[19,8,384]{2,1,0:T(8,128)S(1)}, f32[19,8,384]{2,1,0:T(8,128)S(1)}, u32[]{:S(2)}, u32[]{:S(2)}) collective-permute-start(f32[19,8,384]{2,1,0:T(8,128)S(1)} %get-tuple-element.44), channel_id=1, source_target_pairs={{0,16},{16,0},{32,48},{48,32},{64,80},{80,64},{96,112},{112,96},{1... | collective-permute-start | bytes 700424 | tf_op jit(solution)/shard_map/ppermute | solution.py:326
  34.6 2.7 %window_first.1 = (f32[10,40,384]{2,1,0:T(8,128)S(1)}, f32[28,8,384]{2,1,0:T(8,128)S(1)}, f32[28,8,384]{2,1,0:T(8,128)S(1)}, f32[4,128]{1,0:T(4,128)S(1)}, f32[1...) custom-call(f32[12,48,384]{2,1,0:T(8,128)S(1)} %get-tuple-element.40, ...), custom_call_target="tpu_custom_call" | custom-call | tf_op jit(solution)/shard_map/window_first/pallas_call | solution.py:365
  37.2 3.7 %collective-permute-start.6 = (f32[28,8,384]{2,1,0:T(8,128)S(1)}, f32[28,8,384]{2,1,0:T(8,128)S(1)}, u32[]{:S(2)}, u32[]{:S(2)}) collective-permute-start(f32[28,8,384]{2,1,0:T(8,128)S(1)} %get-tuple-element.46), channel_id=1, source_target_pairs={{16,32},{32,16},{48,64},{64,48},{80,96},{96,80},{112,128},{128,112... | collective-permute-start | bytes 1032200 | tf_op jit(solution)/shard_map/ppermute | solution.py:325
  40.9 1.9 %collective-permute-start.7 = (f32[28,8,384]{2,1,0:T(8,128)S(1)}, f32[28,8,384]{2,1,0:T(8,128)S(1)}, u32[]{:S(2)}, u32[]{:S(2)}) collective-permute-start(f32[28,8,384]{2,1,0:T(8,128)S(1)} %get-tuple-element.47), channel_id=1, source_target_pairs={{0,16},{16,0},{32,48},{48,32},{64,80},{80,64},{96,112},{112,96},{1... | collective-permute-start | bytes 1032200 | tf_op jit(solution)/shard_map/ppermute | solution.py:326
  42.8 3.0 %collective-permute-done.6.refs_1_ = f32[28,8,384]{2,1,0:T(8,128)S(1)} collective-permute-done((f32[28,8,384]{2,1,0:T(8,128)S(1)}, f32[28,8,384]{2,1,0:T(8,128)S(1)}, u32[]{:S(2)}, u32[]{:S(2)}) %collective-permute-start.6) | collective-permute-done | bytes 344096 | tf_op jit(solution)/shard_map/ppermute | solution.py:325
  45.8 1.8 %window_inner.1 = (f32[10,32,384]{2,1,0:T(8,128)S(1)}, f32[8,8,384]{2,1,0:T(8,128)S(1)}, f32[8,8,384]{2,1,0:T(8,128)S(1)}, f32[4,128]{1,0:T(4,128)S(1)}) custom-call(f32[10,40,384]{2,1,0:T(8,128)S(1)} %get-tuple-element.45.refs_0_, f32[28,8,384]{2,1,0:T(8,128)S(1)} %collective-permute-done.6.refs_1_, f32[28,8,384]{2,1,0:T(8,128)S(1)} %collective-permute-done.7.refs_2_, ...), custom_call_target="tpu_custom_call" | custom-call | tf_op jit(solution)/shard_map/window_inner/pallas_call | solution.py:368
  48.3 8.4 %collective-permute-start.9 = (f32[8,8,384]{2,1,0:T(8,128)S(1)}, f32[8,8,384]{2,1,0:T(8,128)S(1)}, u32[]{:S(2)}, u32[]{:S(2)}) collective-permute-start(f32[8,8,384]{2,1,0:T(8,128)S(1)} %get-tuple-element.53), channel_id=1, source_target_pairs={{0,1},{1,0},{2,3},{3,2},{4,5},{5,4},{6,7},{7,6},{8,9},{9,8},{10,11... | collective-permute-start | bytes 294920 | tf_op jit(solution)/shard_map/ppermute | solution.py:326
  56.7 2.0 %collective-permute-done.9.refs_2_ = f32[8,8,384]{2,1,0:T(8,128)S(1)} collective-permute-done((f32[8,8,384]{2,1,0:T(8,128)S(1)}, f32[8,8,384]{2,1,0:T(8,128)S(1)}, u32[]{:S(2)}, u32[]{:S(2)}) %collective-permute-start.9) | collective-permute-done | bytes 98336 | tf_op jit(solution)/shard_map/ppermute | solution.py:326
  58.8 3.7 %collective-permute-start.10 = (f32[36,8,384]{2,1,0:T(8,128)S(1)}, f32[36,8,384]{2,1,0:T(8,128)S(1)}, u32[]{:S(2)}, u32[]{:S(2)}) collective-permute-start(f32[36,8,384]{2,1,0:T(8,128)S(1)} %get-tuple-element.55), channel_id=1, source_target_pairs={{16,32},{32,16},{48,64},{64,48},{80,96},{96,80},{112,128},{128,112... | collective-permute-start | bytes 1327112 | tf_op jit(solution)/shard_map/ppermute | solution.py:325
  62.5 1.9 %collective-permute-start.11 = (f32[36,8,384]{2,1,0:T(8,128)S(1)}, f32[36,8,384]{2,1,0:T(8,128)S(1)}, u32[]{:S(2)}, u32[]{:S(2)}) collective-permute-start(f32[36,8,384]{2,1,0:T(8,128)S(1)} %get-tuple-element.56), channel_id=1, source_target_pairs={{0,16},{16,0},{32,48},{48,32},{64,80},{80,64},{96,112},{112,96},{1... | collective-permute-start | bytes 1327112 | tf_op jit(solution)/shard_map/ppermute | solution.py:326
  64.4 4.0 %collective-permute-done.10.refs_1_ = f32[36,8,384]{2,1,0:T(8,128)S(1)} collective-permute-done((f32[36,8,384]{2,1,0:T(8,128)S(1)}, f32[36,8,384]{2,1,0:T(8,128)S(1)}, u32[]{:S(2)}, u32[]{:S(2)}) %collective-permute-start.10) | collective-permute-done | bytes 442400 | tf_op jit(solution)/shard_map/ppermute | solution.py:325
  68.4 2.0 %window_wide.1 = (f32[10,40,384]{2,1,0:T(8,128)S(1)}, f32[28,8,384]{2,1,0:T(8,128)S(1)}, f32[28,8,384]{2,1,0:T(8,128)S(1)}, f32[4,128]{1,0:T(4,128)S(1)}) custom-call(f32[10,48,384]{2,1,0:T(8,128)S(1)} %get-tuple-element.54.refs_0_, f32[36,8,384]{2,1,0:T(8,128)S(1)} %collective-permute-done.10.refs_1_, f32[36,8,384]{2,1,0:T(8,128)S(1)} %collective-permute-done.11.refs_2_, ...), custom_call_target="tpu_custom_call" | custom-call | tf_op jit(solution)/shard_map/window_wide/pallas_call | solution.py:374
  70.4 3.9 %collective-permute-start.12 = (f32[28,8,384]{2,1,0:T(8,128)S(1)}, f32[28,8,384]{2,1,0:T(8,128)S(1)}, u32[]{:S(2)}, u32[]{:S(2)}) collective-permute-start(f32[28,8,384]{2,1,0:T(8,128)S(1)} %get-tuple-element.61), channel_id=1, source_target_pairs={{16,32},{32,16},{48,64},{64,48},{80,96},{96,80},{112,128},{128,112... | collective-permute-start | bytes 1032200 | tf_op jit(solution)/shard_map/ppermute | solution.py:325
  74.3 1.9 %collective-permute-start.13 = (f32[28,8,384]{2,1,0:T(8,128)S(1)}, f32[28,8,384]{2,1,0:T(8,128)S(1)}, u32[]{:S(2)}, u32[]{:S(2)}) collective-permute-start(f32[28,8,384]{2,1,0:T(8,128)S(1)} %get-tuple-element.62), channel_id=1, source_target_pairs={{0,16},{16,0},{32,48},{48,32},{64,80},{80,64},{96,112},{112,96},{1... | collective-permute-start | bytes 1032200 | tf_op jit(solution)/shard_map/ppermute | solution.py:326
  76.2 2.0 %waves.1 = (bf16[128,4096]{1,0:T(8,128)(2,1)S(1)}, bf16[128,4096]{1,0:T(8,128)(2,1)S(1)}) custom-call(s32[1,128]{1,0:T(1,128)S(1)} %add_bitcast_fusion.refs_5_.refs_3_.refs_0_, f32[2,4096]{1,0:T(2,128)S(1)} %copy-done), custom_call_target="tpu_custom_call" | custom-call | tf_op jit(solution)/shard_map/waves/pallas_call | solution.py:381
  79.2 2.3 %window_last.1 = (f32[4,32,384]{2,1,0:T(8,128)}, f32[4,32,384]{2,1,0:T(8,128)}, f32[16,128]{1,0:T(8,128)S(1)}) custom-call(f32[10,40,384]{2,1,0:T(8,128)S(1)} %get-tuple-element.60.refs_0_, f32[28,8,384]{2,1,0:T(8,128)S(1)} %collective-permute-done.12.refs_1_, f32[28,8,384]{2,1,0:T(8,128)S(1)} %collective-permute-done.13.refs_2_, ...), custom_call_target="tpu_custom_call" | custom-call | tf_op jit(solution)/shard_map/window_last/pallas_call | solution.py:375
  81.9 21.4 %all_to_all.10.part_ref = f32[32,16,128]{2,1,0:T(8,128)S(1)} all-to-all(f32[32,16,128]{2,1,0:T(8,128)S(1)} %project.1), channel_id=1, replica_groups={{0,1,2,3,4,5,6,7,8,9,10,11,12,13,14,15,16,17,18,19,20,21,22,23,24,25,26..., dimensions={0} | all-to-all | bytes 524288 | tf_op jit(solution)/shard_map/all_to_all | solution.py:384
  103.4 27.7 %all_to_all.11.part_ref = f32[24,16,128]{2,1,0:T(8,128)S(1)} all-to-all(f32[24,16,128]{2,1,0:T(8,128)S(1)} %row_total.1), channel_id=1, replica_groups={{0,32,64,96,128,160,192,224,256,288,320,352,384,416,448,480,512,544,576..., dimensions={0} | all-to-all | bytes 393216 | tf_op jit(solution)/shard_map/all_to_all | solution.py:387
  131.1 5.7 %collective-permute-start.14 = (f32[1,16,128]{2,1,0:T(8,128)S(1)}, f32[1,16,128]{2,1,0:T(8,128)S(1)}, u32[]{:S(2)}, u32[]{:S(2)}) collective-permute-start(f32[1,16,128]{2,1,0:T(8,128)S(1)} %total.1.refs_0_), channel_id=1, source_target_pairs={{0,16},{16,0},{32,48},{48,32},{64,80},{80,64},{96,112},{112,96},{1... | collective-permute-start | bytes 24584 | tf_op jit(solution)/shard_map/ppermute | solution.py:389
  (27 shorter events, 7.6 us)
Async XLA Ops:
  1.9 32.7 %collective-permute-start.2 = (f32[44,8,384]{2,1,0:T(8,128)S(1)}, f32[44,8,384]{2,1,0:T(8,128)S(1)}, u32[]{:S(2)}, u32[]{:S(2)}) collective-permute-start(f32[44,8,384]{2,1,0:T(8,128)S(1)} %get-tuple-element.41), channel_id=1, source_target_pairs={{16,32},{32,16},{48,64},{64,48},{80,96},{96,80},{112,128},{128,112... | collective-permute-start | bytes 1622024 | tf_op jit(solution)/shard_map/ppermute | solution.py:325
  7.3 27.3 %collective-permute-start.3 = (f32[44,8,384]{2,1,0:T(8,128)S(1)}, f32[44,8,384]{2,1,0:T(8,128)S(1)}, u32[]{:S(2)}, u32[]{:S(2)}) collective-permute-start(f32[44,8,384]{2,1,0:T(8,128)S(1)} %get-tuple-element.42), channel_id=1, source_target_pairs={{0,16},{16,0},{32,48},{48,32},{64,80},{80,64},{96,112},{112,96},{1... | collective-permute-start | bytes 1622024 | tf_op jit(solution)/shard_map/ppermute | solution.py:326
  15.0 3.9 %collective-permute-start = (f32[12,8,384]{2,1,0:T(8,128)S(1)}, f32[12,8,384]{2,1,0:T(8,128)S(1)}, u32[]{:S(2)}, u32[]{:S(2)}) collective-permute-start(f32[12,8,384]{2,1,0:T(8,128)S(1)} %get-tuple-element.38), channel_id=1, source_target_pairs={{1,2},{2,1},{3,4},{4,3},{5,6},{6,5},{7,8},{8,7},{9,10},{10,9},{11,... | collective-permute-start | bytes 442376 | tf_op jit(solution)/shard_map/ppermute | solution.py:325
  15.7 10.4 %collective-permute-start.1 = (f32[12,8,384]{2,1,0:T(8,128)S(1)}, f32[12,8,384]{2,1,0:T(8,128)S(1)}, u32[]{:S(2)}, u32[]{:S(2)}) collective-permute-start(f32[12,8,384]{2,1,0:T(8,128)S(1)} %get-tuple-element.39), channel_id=1, source_target_pairs={{0,1},{1,0},{2,3},{3,2},{4,5},{5,4},{6,7},{7,6},{8,9},{9,8},{10,11... | collective-permute-start | bytes 442376 | tf_op jit(solution)/shard_map/ppermute | solution.py:326
  26.2 6.6 %copy-start.2 = (s32[64]{0:T(128)S(1)}, s32[64]{0:T(128)}, u32[]{:S(2)}) copy-start(s32[64]{0:T(128)} %param.9) | copy-start | bytes 772
  26.2 8.4 %collective-permute-start.4 = (f32[19,8,384]{2,1,0:T(8,128)S(1)}, f32[19,8,384]{2,1,0:T(8,128)S(1)}, u32[]{:S(2)}, u32[]{:S(2)}) collective-permute-start(f32[19,8,384]{2,1,0:T(8,128)S(1)} %get-tuple-element.43), channel_id=1, source_target_pairs={{16,32},{32,16},{48,64},{64,48},{80,96},{96,80},{112,128},{128,112... | collective-permute-start | bytes 700424 | tf_op jit(solution)/shard_map/ppermute | solution.py:325
  30.8 3.7 %collective-permute-start.5 = (f32[19,8,384]{2,1,0:T(8,128)S(1)}, f32[19,8,384]{2,1,0:T(8,128)S(1)}, u32[]{:S(2)}, u32[]{:S(2)}) collective-permute-start(f32[19,8,384]{2,1,0:T(8,128)S(1)} %get-tuple-element.44), channel_id=1, source_target_pairs={{0,16},{16,0},{32,48},{48,32},{64,80},{80,64},{96,112},{112,96},{1... | collective-permute-start | bytes 700424 | tf_op jit(solution)/shard_map/ppermute | solution.py:326
  37.2 8.6 %collective-permute-start.6 = (f32[28,8,384]{2,1,0:T(8,128)S(1)}, f32[28,8,384]{2,1,0:T(8,128)S(1)}, u32[]{:S(2)}, u32[]{:S(2)}) collective-permute-start(f32[28,8,384]{2,1,0:T(8,128)S(1)} %get-tuple-element.46), channel_id=1, source_target_pairs={{16,32},{32,16},{48,64},{64,48},{80,96},{96,80},{112,128},{128,112... | collective-permute-start | bytes 1032200 | tf_op jit(solution)/shard_map/ppermute | solution.py:325
  40.9 4.9 %collective-permute-start.7 = (f32[28,8,384]{2,1,0:T(8,128)S(1)}, f32[28,8,384]{2,1,0:T(8,128)S(1)}, u32[]{:S(2)}, u32[]{:S(2)}) collective-permute-start(f32[28,8,384]{2,1,0:T(8,128)S(1)} %get-tuple-element.47), channel_id=1, source_target_pairs={{0,16},{16,0},{32,48},{48,32},{64,80},{80,64},{96,112},{112,96},{1... | collective-permute-start | bytes 1032200 | tf_op jit(solution)/shard_map/ppermute | solution.py:326
  47.6 9.1 %collective-permute-start.8 = (f32[8,8,384]{2,1,0:T(8,128)S(1)}, f32[8,8,384]{2,1,0:T(8,128)S(1)}, u32[]{:S(2)}, u32[]{:S(2)}) collective-permute-start(f32[8,8,384]{2,1,0:T(8,128)S(1)} %get-tuple-element.52), channel_id=1, source_target_pairs={{1,2},{2,1},{3,4},{4,3},{5,6},{6,5},{7,8},{8,7},{9,10},{10,9},{11,... | collective-permute-start | bytes 294920 | tf_op jit(solution)/shard_map/ppermute | solution.py:325
  48.3 10.4 %collective-permute-start.9 = (f32[8,8,384]{2,1,0:T(8,128)S(1)}, f32[8,8,384]{2,1,0:T(8,128)S(1)}, u32[]{:S(2)}, u32[]{:S(2)}) collective-permute-start(f32[8,8,384]{2,1,0:T(8,128)S(1)} %get-tuple-element.53), channel_id=1, source_target_pairs={{0,1},{1,0},{2,3},{3,2},{4,5},{5,4},{6,7},{7,6},{8,9},{9,8},{10,11... | collective-permute-start | bytes 294920 | tf_op jit(solution)/shard_map/ppermute | solution.py:326
  58.8 9.6 %collective-permute-start.10 = (f32[36,8,384]{2,1,0:T(8,128)S(1)}, f32[36,8,384]{2,1,0:T(8,128)S(1)}, u32[]{:S(2)}, u32[]{:S(2)}) collective-permute-start(f32[36,8,384]{2,1,0:T(8,128)S(1)} %get-tuple-element.55), channel_id=1, source_target_pairs={{16,32},{32,16},{48,64},{64,48},{80,96},{96,80},{112,128},{128,112... | collective-permute-start | bytes 1327112 | tf_op jit(solution)/shard_map/ppermute | solution.py:325
  62.5 6.0 %collective-permute-start.11 = (f32[36,8,384]{2,1,0:T(8,128)S(1)}, f32[36,8,384]{2,1,0:T(8,128)S(1)}, u32[]{:S(2)}, u32[]{:S(2)}) collective-permute-start(f32[36,8,384]{2,1,0:T(8,128)S(1)} %get-tuple-element.56), channel_id=1, source_target_pairs={{0,16},{16,0},{32,48},{48,32},{64,80},{80,64},{96,112},{112,96},{1... | collective-permute-start | bytes 1327112 | tf_op jit(solution)/shard_map/ppermute | solution.py:326
  68.4 7.8 %copy-start = (f32[2,4096]{1,0:T(2,128)S(1)}, f32[2,4096]{1,0:T(2,128)}, u32[]{:S(2)}) copy-start(f32[2,4096]{1,0:T(2,128)} %refs_1_.1) | copy-start | bytes 98308
  70.4 8.8 %collective-permute-start.12 = (f32[28,8,384]{2,1,0:T(8,128)S(1)}, f32[28,8,384]{2,1,0:T(8,128)S(1)}, u32[]{:S(2)}, u32[]{:S(2)}) collective-permute-start(f32[28,8,384]{2,1,0:T(8,128)S(1)} %get-tuple-element.61), channel_id=1, source_target_pairs={{16,32},{32,16},{48,64},{64,48},{80,96},{96,80},{112,128},{128,112... | collective-permute-start | bytes 1032200 | tf_op jit(solution)/shard_map/ppermute | solution.py:325
  74.3 4.9 %collective-permute-start.13 = (f32[28,8,384]{2,1,0:T(8,128)S(1)}, f32[28,8,384]{2,1,0:T(8,128)S(1)}, u32[]{:S(2)}, u32[]{:S(2)}) collective-permute-start(f32[28,8,384]{2,1,0:T(8,128)S(1)} %get-tuple-element.62), channel_id=1, source_target_pairs={{0,16},{16,0},{32,48},{48,32},{64,80},{80,64},{96,112},{112,96},{1... | collective-permute-start | bytes 1032200 | tf_op jit(solution)/shard_map/ppermute | solution.py:326
  131.1 6.5 %copy-start.1 = (f32[2,8,256]{2,1,0:T(8,128)S(1)}, f32[2,8,256]{2,1,0:T(8,128)}, u32[]{:S(2)}) copy-start(f32[2,8,256]{2,1,0:T(8,128)} %refs_2_.1) | copy-start | bytes 49156
  131.1 6.5 %collective-permute-start.14 = (f32[1,16,128]{2,1,0:T(8,128)S(1)}, f32[1,16,128]{2,1,0:T(8,128)S(1)}, u32[]{:S(2)}, u32[]{:S(2)}) collective-permute-start(f32[1,16,128]{2,1,0:T(8,128)S(1)} %total.1.refs_0_), channel_id=1, source_target_pairs={{0,16},{16,0},{32,48},{48,32},{64,80},{80,64},{96,112},{112,96},{1... | collective-permute-start | bytes 24584 | tf_op jit(solution)/shard_map/ppermute | solution.py:389

commit v7 on v6

--- a/solution.py
+++ b/solution.py
@@ -15,7 +15,7 @@
 TURN = 6.283185307179586
 
 
-def call(kernel, outs, scratch=(), name=None, specs=None):
+def call(kernel, outs, scratch=(), name=None, specs=None, cost=None):
     more = {} if specs is None else {"in_specs": specs}
     return pl.pallas_call(
         kernel,
@@ -23,6 +23,7 @@
         scratch_shapes=list(scratch),
         compiler_params=pltpu.CompilerParams(vmem_limit_bytes=16 * 1024 * 1024),
         name=name,
+        cost_estimate=cost,
         **more,
     )
 
@@ -77,10 +78,6 @@
     return [t for t in tiles if t[2] < ty], [t for t in tiles if t[2] >= ty]
 
 
-def joined_tiles(fields, tx, ty):
-    return split_tiles(fields, tx, ty, 2 * W)[1] if fields == 3 else message_tiles(fields, tx, ty, 2 * W)
-
-
 def write_messages(own, b_ref, a_ref, tiles, fields, tx, ty):
     odd = lax.axis_index("gx") % 2
     wide = own.shape[1] == ty + 16
@@ -112,7 +109,7 @@
     for ref, row in ((y_a, ty + 8 * odd), (y_b, ty + 8 - 8 * odd)):
         for k, (lo, hi) in enumerate(plane_sets(fields, tx)):
             own_ref[lo:hi, pl.ds(pl.multiple_of(row, 8), 8)] = ref[k * tx : (k + 1) * tx]
-    write_messages(own_ref, odd_even_ref, even_odd_ref, joined_tiles(fields, tx, ty), fields, tx, ty)
+    write_messages(own_ref, odd_even_ref, even_odd_ref, split_tiles(fields, tx, ty, 2 * W)[1], fields, tx, ty)
 
 
 def around(plane, x):
@@ -165,7 +162,7 @@
     refs = list(refs)
     take = lambda n: [refs.pop(0) for _ in range(n)]
     own, x_b, x_a = take(3)
-    from_y = take(2) if kind == "first" else ()
+    from_y = take(2) if kind in ("first", "wide") else ()
     (cell_row,) = take(1)
     if kind != "first":
         coefs = take(3)
@@ -173,7 +170,7 @@
     if kind == "last":
         out_cur, out_bef, series_ref = take(3)
     else:
-        state_ref, *rest = take(3)
+        state_ref, *rest = take(5 if kind == "inner" else 3)
         (sample_ref,) = take(1)
     if kind == "first":
         coefs, coefs4 = take(3), take(3)
@@ -191,7 +188,7 @@
         for pair, tiles in zip(((x_b, x_a), from_y), split_tiles(len(targets), tx, ty, 2 * W)):
             read_messages(targets, *pair, tiles, tx, ty)
     else:
-        read_messages(targets, x_b, x_a, message_tiles(2, tx, ty, 2 * W if kind == "wide" else W), tx, ty)
+        read_messages(targets, x_b, x_a, message_tiles(2, tx, ty, W), tx, ty)
     if kind == "first":
         for k in (0, 1):
             coefs[k][...] = jnp.zeros(coefs[k].shape, F32)
@@ -234,7 +231,8 @@
     state_ref[0:tx] = cut(cur[tx : 2 * tx])
     state_ref[tx:] = cut(bef[tx - 1 : 2 * tx + 1])
     if kind == "inner":
-        write_edges(state_ref, *rest, 2, tx, ty)
+        write_edges(state_ref, *rest[:2], 2, tx, ty)
+        write_messages(state_ref, *rest[2:], split_tiles(2, tx, ty, 2 * W)[0], 2, tx, ty)
     else:
         write_messages(state_ref, *rest, message_tiles(2, tx, ty, W), 2, tx, ty)
 
@@ -337,12 +335,14 @@
     def count(tiles):
         return shape(len(tiles), 8, nz)
 
-    def exchange_both(fields, state, y_b, y_a, *own_rows):
+    cover = pl.CostEstimate(flops=3 * 10**10, transcendentals=0, bytes_accessed=1)
+
+    def exchange_both(fields, state, y_b, y_a, x_b, x_a):
         y_rows = swap(y_b, y_a, "gy")
-        ahead = swap(*own_rows, "gx") if own_rows else ()
-        size = count(joined_tiles(fields, tx, ty))
+        ahead = swap(x_b, x_a, "gx")
+        size = count(split_tiles(fields, tx, ty, 2 * W)[1])
         own, x_b, x_a = call(
-            lambda *refs: join_kernel(fields, tx, ty, *refs), [shape(*state.shape[:1], *wide[1:]), size, size], name="join"
+            lambda *refs: join_kernel(fields, tx, ty, *refs), [shape(*state.shape[:1], *wide[1:]), size, size], name="join", cost=cover
         )(state, *y_rows)
         return [own, *ahead, *swap(x_b, x_a, "gx"), cells]
 
@@ -367,7 +367,7 @@
     )(*exchange_both(3, *state))
     *state, second = call(
         window("inner"),
-        [shape(2 * tx + 2, ty, nz)] + [shape(2 * tx, Y, nz)] * 2 + [part],
+        [shape(2 * tx + 2, ty, nz)] + [shape(2 * tx, Y, nz)] * 2 + [count(split_tiles(2, tx, ty, 2 * W)[0])] * 2 + [part],
         scratch(thin),
         name="window_inner",
     )(*exchange_x(*own), p4, q4, r4)

time: 139 us -> 134 us (0.964)
  waiting for transfers between devices: 19.7 us -> 7.85 us
  starting transfers between devices: 55.2 us -> 61.2 us
    ppermute x7 -> x8, waiting for transfers between devices: 9.21 us -> 0.47 us  [swap(): lax.ppermute(even_odd, axis, [(i, i ^ 1) for i in range(count) if i ^ 1 <...]
    ppermute x7 -> x8, starting transfers between devices: 22.5 us -> 28.9 us  [swap(): got = lax.ppermute(odd_even, axis, pairs)]
    ppermute x7 -> x8, waiting for transfers between devices: 9.73 us -> 6.57 us  [swap(): got = lax.ppermute(odd_even, axis, pairs)]
    ppermute x7 -> x8, starting transfers between devices: 27 us -> 26.9 us  [swap(): lax.ppermute(even_odd, axis, [(i, i ^ 1) for i in range(count) if i ^ 1 <...]
  transfers between devices with their start and end apart: 15 -> 17, of which waited for: 7 -> 6; matrix products, arithmetic and copies ran while one was open for 0% -> 0% of each run, Pallas kernels for 2% -> 2%
where the time goes in v7:
time: 134 us; the launch traced here: 133 us
  starting transfers between devices  61.2 us (46%)
  blocking collectives  49.7 us (37%)
  Pallas kernels  13.4 us (10%)
  waiting for transfers between devices  7.85 us (6%)
    ppermute x8, starting transfers between devices, swap(): got = lax.ppermute(odd_even, axis, pairs)  28.9 us
    all_to_all x1, blocking collectives, body(): lax.all_to_all(share, 'gx', 0, 0, tiled=True, axis_index_groups=chips)  28.3 us
    ppermute x8, starting transfers between devices, swap(): lax.ppermute(even_odd, axis, [(i, i ^ 1) for i in range(count) if i ^ 1 <...  26.9 us
    all_to_all x1, blocking collectives, body(): lax.all_to_all(share, ('gx', 'gy'), 0, 0, tiled=True, axis_index_groups=r...  21.4 us
    ppermute x8, waiting for transfers between devices, swap(): got = lax.ppermute(odd_even, axis, pairs)  6.57 us
    ppermute x1, starting transfers between devices, body(): other = lax.ppermute(traces, 'gx', [(i, i ^ 1) for i in range(ngx)])  5.33 us
  transfers between devices with their start and end apart: 17, of which 6 were waited for; matrix products, arithmetic and copies ran while one was open for 0% of the time, Pallas kernels for 2%

profile of v7, /device:TPU:1, one launch (start us, length us, event | category | flops | bytes accessed | tf_op | source)
XLA Modules:
  0.0 133.1 jit_solution(18086988660033415260)
XLA Ops:
  2.6 9.8 %collective-permute-start.1 = (f32[12,8,384]{2,1,0:T(8,128)S(1)}, f32[12,8,384]{2,1,0:T(8,128)S(1)}, u32[]{:S(2)}, u32[]{:S(2)}) collective-permute-start(f32[12,8,384]{2,1,0:T(8,128)S(1)} %get-tuple-element.41), channel_id=1, source_target_pairs={{0,1},{1,0},{2,3},{3,2},{4,5},{5,4},{6,7},{7,6},{8,9},{9,8},{10,11... | collective-permute-start | bytes 442376 | tf_op jit(solution)/shard_map/ppermute | solution.py:324
  12.4 5.1 %collective-permute-start.2 = (f32[44,8,384]{2,1,0:T(8,128)S(1)}, f32[44,8,384]{2,1,0:T(8,128)S(1)}, u32[]{:S(2)}, u32[]{:S(2)}) collective-permute-start(f32[44,8,384]{2,1,0:T(8,128)S(1)} %get-tuple-element.43), channel_id=1, source_target_pairs={{16,32},{32,16},{48,64},{64,48},{80,96},{96,80},{112,128},{128,112... | collective-permute-start | bytes 1622024 | tf_op jit(solution)/shard_map/ppermute | solution.py:323
  17.5 1.9 %collective-permute-start.3 = (f32[44,8,384]{2,1,0:T(8,128)S(1)}, f32[44,8,384]{2,1,0:T(8,128)S(1)}, u32[]{:S(2)}, u32[]{:S(2)}) collective-permute-start(f32[44,8,384]{2,1,0:T(8,128)S(1)} %get-tuple-element.44), channel_id=1, source_target_pairs={{0,16},{16,0},{32,48},{48,32},{64,80},{80,64},{96,112},{112,96},{1... | collective-permute-start | bytes 1622024 | tf_op jit(solution)/shard_map/ppermute | solution.py:324
  19.6 4.7 %collective-permute-start.4 = (f32[19,8,384]{2,1,0:T(8,128)S(1)}, f32[19,8,384]{2,1,0:T(8,128)S(1)}, u32[]{:S(2)}, u32[]{:S(2)}) collective-permute-start(f32[19,8,384]{2,1,0:T(8,128)S(1)} %get-tuple-element.45), channel_id=1, source_target_pairs={{16,32},{32,16},{48,64},{64,48},{80,96},{96,80},{112,128},{128,112... | collective-permute-start | bytes 700424 | tf_op jit(solution)/shard_map/ppermute | solution.py:323
  24.3 1.9 %collective-permute-start.5 = (f32[19,8,384]{2,1,0:T(8,128)S(1)}, f32[19,8,384]{2,1,0:T(8,128)S(1)}, u32[]{:S(2)}, u32[]{:S(2)}) collective-permute-start(f32[19,8,384]{2,1,0:T(8,128)S(1)} %get-tuple-element.46), channel_id=1, source_target_pairs={{0,16},{16,0},{32,48},{48,32},{64,80},{80,64},{96,112},{112,96},{1... | collective-permute-start | bytes 700424 | tf_op jit(solution)/shard_map/ppermute | solution.py:324
  26.3 1.7 %collective-permute-done.4.refs_3_ = f32[19,8,384]{2,1,0:T(8,128)S(1)} collective-permute-done((f32[19,8,384]{2,1,0:T(8,128)S(1)}, f32[19,8,384]{2,1,0:T(8,128)S(1)}, u32[]{:S(2)}, u32[]{:S(2)}) %collective-permute-start.4) | collective-permute-done | bytes 233504 | tf_op jit(solution)/shard_map/ppermute | solution.py:323
  28.1 2.7 %window_first.1 = (f32[10,40,384]{2,1,0:T(8,128)S(1)}, f32[28,8,384]{2,1,0:T(8,128)S(1)}, f32[28,8,384]{2,1,0:T(8,128)S(1)}, f32[4,128]{1,0:T(4,128)S(1)}, f32[1...) custom-call(f32[12,48,384]{2,1,0:T(8,128)S(1)} %get-tuple-element.42, ...), custom_call_target="tpu_custom_call" | custom-call | tf_op jit(solution)/shard_map/window_first/pallas_call | solution.py:365
  30.7 3.7 %collective-permute-start.6 = (f32[28,8,384]{2,1,0:T(8,128)S(1)}, f32[28,8,384]{2,1,0:T(8,128)S(1)}, u32[]{:S(2)}, u32[]{:S(2)}) collective-permute-start(f32[28,8,384]{2,1,0:T(8,128)S(1)} %get-tuple-element.48), channel_id=1, source_target_pairs={{16,32},{32,16},{48,64},{64,48},{80,96},{96,80},{112,128},{128,112... | collective-permute-start | bytes 1032200 | tf_op jit(solution)/shard_map/ppermute | solution.py:323
  34.4 1.9 %collective-permute-start.7 = (f32[28,8,384]{2,1,0:T(8,128)S(1)}, f32[28,8,384]{2,1,0:T(8,128)S(1)}, u32[]{:S(2)}, u32[]{:S(2)}) collective-permute-start(f32[28,8,384]{2,1,0:T(8,128)S(1)} %get-tuple-element.49), channel_id=1, source_target_pairs={{0,16},{16,0},{32,48},{48,32},{64,80},{80,64},{96,112},{112,96},{1... | collective-permute-start | bytes 1032200 | tf_op jit(solution)/shard_map/ppermute | solution.py:324
  36.3 3.0 %collective-permute-done.6.refs_1_ = f32[28,8,384]{2,1,0:T(8,128)S(1)} collective-permute-done((f32[28,8,384]{2,1,0:T(8,128)S(1)}, f32[28,8,384]{2,1,0:T(8,128)S(1)}, u32[]{:S(2)}, u32[]{:S(2)}) %collective-permute-start.6) | collective-permute-done | bytes 344096 | tf_op jit(solution)/shard_map/ppermute | solution.py:323
  39.3 1.8 %window_inner.1 = (f32[10,32,384]{2,1,0:T(8,128)S(1)}, f32[8,8,384]{2,1,0:T(8,128)S(1)}, f32[8,8,384]{2,1,0:T(8,128)S(1)}, f32[24,8,384]{2,1,0:T(8,128)S(1)}, f3...) custom-call(f32[10,40,384]{2,1,0:T(8,128)S(1)} %get-tuple-element.47.refs_0_, ...), custom_call_target="tpu_custom_call" | custom-call | tf_op jit(solution)/shard_map/window_inner/pallas_call | solution.py:368
  41.8 5.6 %collective-permute-start.9 = (f32[8,8,384]{2,1,0:T(8,128)S(1)}, f32[8,8,384]{2,1,0:T(8,128)S(1)}, u32[]{:S(2)}, u32[]{:S(2)}) collective-permute-start(f32[8,8,384]{2,1,0:T(8,128)S(1)} %get-tuple-element.55), channel_id=1, source_target_pairs={{0,1},{1,0},{2,3},{3,2},{4,5},{5,4},{6,7},{7,6},{8,9},{9,8},{10,11... | collective-permute-start | bytes 294920 | tf_op jit(solution)/shard_map/ppermute | solution.py:324
  47.4 4.2 %collective-permute-start.10 = (f32[24,8,384]{2,1,0:T(8,128)S(1)}, f32[24,8,384]{2,1,0:T(8,128)S(1)}, u32[]{:S(2)}, u32[]{:S(2)}) collective-permute-start(f32[24,8,384]{2,1,0:T(8,128)S(1)} %get-tuple-element.57), channel_id=1, source_target_pairs={{16,32},{32,16},{48,64},{64,48},{80,96},{96,80},{112,128},{128,112... | collective-permute-start | bytes 884744 | tf_op jit(solution)/shard_map/ppermute | solution.py:323
  51.6 1.9 %collective-permute-start.11 = (f32[24,8,384]{2,1,0:T(8,128)S(1)}, f32[24,8,384]{2,1,0:T(8,128)S(1)}, u32[]{:S(2)}, u32[]{:S(2)}) collective-permute-start(f32[24,8,384]{2,1,0:T(8,128)S(1)} %get-tuple-element.58), channel_id=1, source_target_pairs={{0,16},{16,0},{32,48},{48,32},{64,80},{80,64},{96,112},{112,96},{1... | collective-permute-start | bytes 884744 | tf_op jit(solution)/shard_map/ppermute | solution.py:324
  53.6 4.6 %collective-permute-start.12 = (f32[12,8,384]{2,1,0:T(8,128)S(1)}, f32[12,8,384]{2,1,0:T(8,128)S(1)}, u32[]{:S(2)}, u32[]{:S(2)}) collective-permute-start(f32[12,8,384]{2,1,0:T(8,128)S(1)} %get-tuple-element.59), channel_id=1, source_target_pairs={{16,32},{32,16},{48,64},{64,48},{80,96},{96,80},{112,128},{128,112... | collective-permute-start | bytes 442376 | tf_op jit(solution)/shard_map/ppermute | solution.py:323
  58.3 1.9 %collective-permute-start.13 = (f32[12,8,384]{2,1,0:T(8,128)S(1)}, f32[12,8,384]{2,1,0:T(8,128)S(1)}, u32[]{:S(2)}, u32[]{:S(2)}) collective-permute-start(f32[12,8,384]{2,1,0:T(8,128)S(1)} %get-tuple-element.60), channel_id=1, source_target_pairs={{0,16},{16,0},{32,48},{48,32},{64,80},{80,64},{96,112},{112,96},{1... | collective-permute-start | bytes 442376 | tf_op jit(solution)/shard_map/ppermute | solution.py:324
  61.5 2.0 %window_wide.1 = (f32[10,40,384]{2,1,0:T(8,128)S(1)}, f32[28,8,384]{2,1,0:T(8,128)S(1)}, f32[28,8,384]{2,1,0:T(8,128)S(1)}, f32[4,128]{1,0:T(4,128)S(1)}) custom-call(f32[10,48,384]{2,1,0:T(8,128)S(1)} %get-tuple-element.56.refs_0_, f32[24,8,384]{2,1,0:T(8,128)S(1)} %collective-permute-done.10.refs_1_, f32[24,8,384]{2,1,0:T(8,128)S(1)} %collective-permute-done.11.refs_2_, ...), custom_call_target="tpu_custom_call" | custom-call | tf_op jit(solution)/shard_map/window_wide/pallas_call | solution.py:374
  63.5 5.2 %collective-permute-start.14 = (f32[28,8,384]{2,1,0:T(8,128)S(1)}, f32[28,8,384]{2,1,0:T(8,128)S(1)}, u32[]{:S(2)}, u32[]{:S(2)}) collective-permute-start(f32[28,8,384]{2,1,0:T(8,128)S(1)} %get-tuple-element.65), channel_id=1, source_target_pairs={{16,32},{32,16},{48,64},{64,48},{80,96},{96,80},{112,128},{128,112... | collective-permute-start | bytes 1032200 | tf_op jit(solution)/shard_map/ppermute | solution.py:323
  68.7 1.9 %collective-permute-start.15 = (f32[28,8,384]{2,1,0:T(8,128)S(1)}, f32[28,8,384]{2,1,0:T(8,128)S(1)}, u32[]{:S(2)}, u32[]{:S(2)}) collective-permute-start(f32[28,8,384]{2,1,0:T(8,128)S(1)} %get-tuple-element.66), channel_id=1, source_target_pairs={{0,16},{16,0},{32,48},{48,32},{64,80},{80,64},{96,112},{112,96},{1... | collective-permute-start | bytes 1032200 | tf_op jit(solution)/shard_map/ppermute | solution.py:324
  70.7 2.0 %waves.1 = (bf16[128,4096]{1,0:T(8,128)(2,1)S(1)}, bf16[128,4096]{1,0:T(8,128)(2,1)S(1)}) custom-call(s32[1,128]{1,0:T(1,128)S(1)} %add_bitcast_fusion.refs_5_.refs_3_.refs_0_, f32[2,4096]{1,0:T(2,128)S(1)} %copy-done), custom_call_target="tpu_custom_call" | custom-call | tf_op jit(solution)/shard_map/waves/pallas_call | solution.py:381
  73.7 2.3 %window_last.1 = (f32[4,32,384]{2,1,0:T(8,128)}, f32[4,32,384]{2,1,0:T(8,128)}, f32[16,128]{1,0:T(8,128)S(1)}) custom-call(f32[10,40,384]{2,1,0:T(8,128)S(1)} %get-tuple-element.64.refs_0_, f32[28,8,384]{2,1,0:T(8,128)S(1)} %collective-permute-done.14.refs_1_, f32[28,8,384]{2,1,0:T(8,128)S(1)} %collective-permute-done.15.refs_2_, ...), custom_call_target="tpu_custom_call" | custom-call | tf_op jit(solution)/shard_map/window_last/pallas_call | solution.py:375
  76.4 21.4 %all_to_all.10.part_ref = f32[32,16,128]{2,1,0:T(8,128)S(1)} all-to-all(f32[32,16,128]{2,1,0:T(8,128)S(1)} %project.1), channel_id=1, replica_groups={{0,1,2,3,4,5,6,7,8,9,10,11,12,13,14,15,16,17,18,19,20,21,22,23,24,25,26..., dimensions={0} | all-to-all | bytes 524288 | tf_op jit(solution)/shard_map/all_to_all | solution.py:384
  97.9 28.3 %all_to_all.11.part_ref = f32[24,16,128]{2,1,0:T(8,128)S(1)} all-to-all(f32[24,16,128]{2,1,0:T(8,128)S(1)} %row_total.1), channel_id=1, replica_groups={{0,32,64,96,128,160,192,224,256,288,320,352,384,416,448,480,512,544,576..., dimensions={0} | all-to-all | bytes 393216 | tf_op jit(solution)/shard_map/all_to_all | solution.py:387
  126.2 5.3 %collective-permute-start.16 = (f32[1,16,128]{2,1,0:T(8,128)S(1)}, f32[1,16,128]{2,1,0:T(8,128)S(1)}, u32[]{:S(2)}, u32[]{:S(2)}) collective-permute-start(f32[1,16,128]{2,1,0:T(8,128)S(1)} %total.1.refs_0_), channel_id=1, source_target_pairs={{0,16},{16,0},{32,48},{48,32},{64,80},{80,64},{96,112},{112,96},{1... | collective-permute-start | bytes 24584 | tf_op jit(solution)/shard_map/ppermute | solution.py:389
  (31 shorter events, 7.2 us)
Async XLA Ops:
  1.9 17.6 %collective-permute-start = (f32[12,8,384]{2,1,0:T(8,128)S(1)}, f32[12,8,384]{2,1,0:T(8,128)S(1)}, u32[]{:S(2)}, u32[]{:S(2)}) collective-permute-start(f32[12,8,384]{2,1,0:T(8,128)S(1)} %get-tuple-element.40), channel_id=1, source_target_pairs={{1,2},{2,1},{3,4},{4,3},{5,6},{6,5},{7,8},{8,7},{9,10},{10,9},{11,... | collective-permute-start | bytes 442376 | tf_op jit(solution)/shard_map/ppermute | solution.py:323
  2.6 16.9 %collective-permute-start.1 = (f32[12,8,384]{2,1,0:T(8,128)S(1)}, f32[12,8,384]{2,1,0:T(8,128)S(1)}, u32[]{:S(2)}, u32[]{:S(2)}) collective-permute-start(f32[12,8,384]{2,1,0:T(8,128)S(1)} %get-tuple-element.41), channel_id=1, source_target_pairs={{0,1},{1,0},{2,3},{3,2},{4,5},{5,4},{6,7},{7,6},{8,9},{9,8},{10,11... | collective-permute-start | bytes 442376 | tf_op jit(solution)/shard_map/ppermute | solution.py:324
  12.4 15.7 %collective-permute-start.2 = (f32[44,8,384]{2,1,0:T(8,128)S(1)}, f32[44,8,384]{2,1,0:T(8,128)S(1)}, u32[]{:S(2)}, u32[]{:S(2)}) collective-permute-start(f32[44,8,384]{2,1,0:T(8,128)S(1)} %get-tuple-element.43), channel_id=1, source_target_pairs={{16,32},{32,16},{48,64},{64,48},{80,96},{96,80},{112,128},{128,112... | collective-permute-start | bytes 1622024 | tf_op jit(solution)/shard_map/ppermute | solution.py:323
  17.5 10.6 %collective-permute-start.3 = (f32[44,8,384]{2,1,0:T(8,128)S(1)}, f32[44,8,384]{2,1,0:T(8,128)S(1)}, u32[]{:S(2)}, u32[]{:S(2)}) collective-permute-start(f32[44,8,384]{2,1,0:T(8,128)S(1)} %get-tuple-element.44), channel_id=1, source_target_pairs={{0,16},{16,0},{32,48},{48,32},{64,80},{80,64},{96,112},{112,96},{1... | collective-permute-start | bytes 1622024 | tf_op jit(solution)/shard_map/ppermute | solution.py:324
  19.6 6.7 %copy-start.2 = (s32[64]{0:T(128)S(1)}, s32[64]{0:T(128)}, u32[]{:S(2)}) copy-start(s32[64]{0:T(128)} %param.9) | copy-start | bytes 772
  19.6 8.5 %collective-permute-start.4 = (f32[19,8,384]{2,1,0:T(8,128)S(1)}, f32[19,8,384]{2,1,0:T(8,128)S(1)}, u32[]{:S(2)}, u32[]{:S(2)}) collective-permute-start(f32[19,8,384]{2,1,0:T(8,128)S(1)} %get-tuple-element.45), channel_id=1, source_target_pairs={{16,32},{32,16},{48,64},{64,48},{80,96},{96,80},{112,128},{128,112... | collective-permute-start | bytes 700424 | tf_op jit(solution)/shard_map/ppermute | solution.py:323
  24.3 3.7 %collective-permute-start.5 = (f32[19,8,384]{2,1,0:T(8,128)S(1)}, f32[19,8,384]{2,1,0:T(8,128)S(1)}, u32[]{:S(2)}, u32[]{:S(2)}) collective-permute-start(f32[19,8,384]{2,1,0:T(8,128)S(1)} %get-tuple-element.46), channel_id=1, source_target_pairs={{0,16},{16,0},{32,48},{48,32},{64,80},{80,64},{96,112},{112,96},{1... | collective-permute-start | bytes 700424 | tf_op jit(solution)/shard_map/ppermute | solution.py:324
  30.7 8.6 %collective-permute-start.6 = (f32[28,8,384]{2,1,0:T(8,128)S(1)}, f32[28,8,384]{2,1,0:T(8,128)S(1)}, u32[]{:S(2)}, u32[]{:S(2)}) collective-permute-start(f32[28,8,384]{2,1,0:T(8,128)S(1)} %get-tuple-element.48), channel_id=1, source_target_pairs={{16,32},{32,16},{48,64},{64,48},{80,96},{96,80},{112,128},{128,112... | collective-permute-start | bytes 1032200 | tf_op jit(solution)/shard_map/ppermute | solution.py:323
  34.4 4.9 %collective-permute-start.7 = (f32[28,8,384]{2,1,0:T(8,128)S(1)}, f32[28,8,384]{2,1,0:T(8,128)S(1)}, u32[]{:S(2)}, u32[]{:S(2)}) collective-permute-start(f32[28,8,384]{2,1,0:T(8,128)S(1)} %get-tuple-element.49), channel_id=1, source_target_pairs={{0,16},{16,0},{32,48},{48,32},{64,80},{80,64},{96,112},{112,96},{1... | collective-permute-start | bytes 1032200 | tf_op jit(solution)/shard_map/ppermute | solution.py:324
  41.1 12.4 %collective-permute-start.8 = (f32[8,8,384]{2,1,0:T(8,128)S(1)}, f32[8,8,384]{2,1,0:T(8,128)S(1)}, u32[]{:S(2)}, u32[]{:S(2)}) collective-permute-start(f32[8,8,384]{2,1,0:T(8,128)S(1)} %get-tuple-element.54), channel_id=1, source_target_pairs={{1,2},{2,1},{3,4},{4,3},{5,6},{6,5},{7,8},{8,7},{9,10},{10,9},{11,... | collective-permute-start | bytes 294920 | tf_op jit(solution)/shard_map/ppermute | solution.py:323
  41.8 11.8 %collective-permute-start.9 = (f32[8,8,384]{2,1,0:T(8,128)S(1)}, f32[8,8,384]{2,1,0:T(8,128)S(1)}, u32[]{:S(2)}, u32[]{:S(2)}) collective-permute-start(f32[8,8,384]{2,1,0:T(8,128)S(1)} %get-tuple-element.55), channel_id=1, source_target_pairs={{0,1},{1,0},{2,3},{3,2},{4,5},{5,4},{6,7},{7,6},{8,9},{9,8},{10,11... | collective-permute-start | bytes 294920 | tf_op jit(solution)/shard_map/ppermute | solution.py:324
  47.4 14.1 %collective-permute-start.10 = (f32[24,8,384]{2,1,0:T(8,128)S(1)}, f32[24,8,384]{2,1,0:T(8,128)S(1)}, u32[]{:S(2)}, u32[]{:S(2)}) collective-permute-start(f32[24,8,384]{2,1,0:T(8,128)S(1)} %get-tuple-element.57), channel_id=1, source_target_pairs={{16,32},{32,16},{48,64},{64,48},{80,96},{96,80},{112,128},{128,112... | collective-permute-start | bytes 884744 | tf_op jit(solution)/shard_map/ppermute | solution.py:323
  51.6 9.9 %collective-permute-start.11 = (f32[24,8,384]{2,1,0:T(8,128)S(1)}, f32[24,8,384]{2,1,0:T(8,128)S(1)}, u32[]{:S(2)}, u32[]{:S(2)}) collective-permute-start(f32[24,8,384]{2,1,0:T(8,128)S(1)} %get-tuple-element.58), channel_id=1, source_target_pairs={{0,16},{16,0},{32,48},{48,32},{64,80},{80,64},{96,112},{112,96},{1... | collective-permute-start | bytes 884744 | tf_op jit(solution)/shard_map/ppermute | solution.py:324
  53.6 7.4 %collective-permute-start.12 = (f32[12,8,384]{2,1,0:T(8,128)S(1)}, f32[12,8,384]{2,1,0:T(8,128)S(1)}, u32[]{:S(2)}, u32[]{:S(2)}) collective-permute-start(f32[12,8,384]{2,1,0:T(8,128)S(1)} %get-tuple-element.59), channel_id=1, source_target_pairs={{16,32},{32,16},{48,64},{64,48},{80,96},{96,80},{112,128},{128,112... | collective-permute-start | bytes 442376 | tf_op jit(solution)/shard_map/ppermute | solution.py:323
  58.3 3.3 %collective-permute-start.13 = (f32[12,8,384]{2,1,0:T(8,128)S(1)}, f32[12,8,384]{2,1,0:T(8,128)S(1)}, u32[]{:S(2)}, u32[]{:S(2)}) collective-permute-start(f32[12,8,384]{2,1,0:T(8,128)S(1)} %get-tuple-element.60), channel_id=1, source_target_pairs={{0,16},{16,0},{32,48},{48,32},{64,80},{80,64},{96,112},{112,96},{1... | collective-permute-start | bytes 442376 | tf_op jit(solution)/shard_map/ppermute | solution.py:324
  61.5 9.2 %copy-start = (f32[2,4096]{1,0:T(2,128)S(1)}, f32[2,4096]{1,0:T(2,128)}, u32[]{:S(2)}) copy-start(f32[2,4096]{1,0:T(2,128)} %refs_1_.1) | copy-start | bytes 98308
  63.5 10.1 %collective-permute-start.14 = (f32[28,8,384]{2,1,0:T(8,128)S(1)}, f32[28,8,384]{2,1,0:T(8,128)S(1)}, u32[]{:S(2)}, u32[]{:S(2)}) collective-permute-start(f32[28,8,384]{2,1,0:T(8,128)S(1)} %get-tuple-element.65), channel_id=1, source_target_pairs={{16,32},{32,16},{48,64},{64,48},{80,96},{96,80},{112,128},{128,112... | collective-permute-start | bytes 1032200 | tf_op jit(solution)/shard_map/ppermute | solution.py:323
  68.7 4.9 %collective-permute-start.15 = (f32[28,8,384]{2,1,0:T(8,128)S(1)}, f32[28,8,384]{2,1,0:T(8,128)S(1)}, u32[]{:S(2)}, u32[]{:S(2)}) collective-permute-start(f32[28,8,384]{2,1,0:T(8,128)S(1)} %get-tuple-element.66), channel_id=1, source_target_pairs={{0,16},{16,0},{32,48},{48,32},{64,80},{80,64},{96,112},{112,96},{1... | collective-permute-start | bytes 1032200 | tf_op jit(solution)/shard_map/ppermute | solution.py:324
  126.2 6.2 %copy-start.1 = (f32[2,8,256]{2,1,0:T(8,128)S(1)}, f32[2,8,256]{2,1,0:T(8,128)}, u32[]{:S(2)}) copy-start(f32[2,8,256]{2,1,0:T(8,128)} %refs_2_.1) | copy-start | bytes 49156
  126.2 6.1 %collective-permute-start.16 = (f32[1,16,128]{2,1,0:T(8,128)S(1)}, f32[1,16,128]{2,1,0:T(8,128)S(1)}, u32[]{:S(2)}, u32[]{:S(2)}) collective-permute-start(f32[1,16,128]{2,1,0:T(8,128)S(1)} %total.1.refs_0_), channel_id=1, source_target_pairs={{0,16},{16,0},{32,48},{48,32},{64,80},{80,64},{96,112},{112,96},{1... | collective-permute-start | bytes 24584 | tf_op jit(solution)/shard_map/ppermute | solution.py:389

commit v8 on v7

--- a/solution.py
+++ b/solution.py
@@ -158,22 +158,52 @@
     return jnp.concatenate([v[..., 0:ty, :], jnp.where(low, above, below)], axis=-2)
 
 
+def sampler(cell, tx, ty, nz):
+    safe = jnp.maximum(cell, 0)
+    lane = lax.broadcasted_iota(jnp.int32, (1, 128), 1)
+    z_of = safe % nz + (lane >= 64).astype(jnp.int32)
+    row_of = jnp.where(cell >= 0, safe // nz, -1)
+    zhot = (lax.broadcasted_iota(jnp.int32, (nz, 128), 0) == z_of).astype(BF16)
+    rhot = lax.broadcasted_iota(jnp.int32, (tx * ty, 128), 0) == row_of
+
+    def pick(field):
+        now = field.reshape(tx * ty, nz)
+        high = now.astype(BF16)
+        low = (now - high.astype(F32)).astype(BF16)
+        dot = lambda a: jnp.dot(a, zhot, preferred_element_type=F32)
+        return jnp.sum(jnp.where(rhot, dot(high) + dot(low), 0.0), axis=0, keepdims=True)
+
+    return pick
+
+
+def sample_kernel(cell_ref, *refs):
+    *rounds, out_ref = refs
+    pick = sampler(cell_ref[...], *rounds[0].shape[1:])
+    for k in range(len(rounds) * W):
+        out_ref[pl.ds(k, 1), :] = pick(rounds[k // W][k % W])
+
+
+def narrow_kernel(ty, *refs):
+    for src, dst in zip(refs[:3], refs[3:]):
+        dst[...] = narrow(src[...], ty)
+
+
 def window_kernel(kind, tx, ty, *refs):
     refs = list(refs)
     take = lambda n: [refs.pop(0) for _ in range(n)]
     own, x_b, x_a = take(3)
     from_y = take(2) if kind in ("first", "wide") else ()
-    (cell_row,) = take(1)
+    (extra,) = take(1) if kind != "inner" else (None,)
     if kind != "first":
         coefs = take(3)
-    done = take(3) if kind == "last" else ()
+    done = take(2) if kind == "last" else ()
     if kind == "last":
         out_cur, out_bef, series_ref = take(3)
     else:
         state_ref, *rest = take(5 if kind == "inner" else 3)
-        (sample_ref,) = take(1)
+        (fields_ref,) = take(1)
     if kind == "first":
-        coefs, coefs4 = take(3), take(3)
+        coefs = take(3)
         gain_ref = coefs[2]
     one, two = take(2)
     nz = own.shape[2]
@@ -199,34 +229,22 @@
             coefs[1][x] = 0.25 * gain
         for x in range(3 * tx):
             gain_ref[x] = 1.0 - 2.0 * gain_ref[x]
-        for k in range(3):
-            coefs4[k][...] = narrow(coefs[k][...], ty)
-    cell = cell_row[...]
-    safe = jnp.maximum(cell, 0)
-    lane = lax.broadcasted_iota(jnp.int32, (1, 128), 1)
-    z_of = safe % nz + (lane >= 64).astype(jnp.int32)
-    row_of = jnp.where(cell >= 0, safe // nz, -1)
-    zhot = (lax.broadcasted_iota(jnp.int32, (nz, 128), 0) == z_of).astype(BF16)
-    rhot = lax.broadcasted_iota(jnp.int32, (tx * ty, 128), 0) == row_of
-
+    if kind == "last":
+        pick = sampler(extra[...], tx, ty, nz)
     picks = []
     for step in range(1, W + 1):
         cur, bef = (one, two) if step % 2 else (two, one)
         advance_step(cur, bef, coefs, step, 3 * tx - step)
-        now = bef[tx : 2 * tx, 0:ty].reshape(tx * ty, nz)
-        high = now.astype(BF16)
-        low = (now - high.astype(F32)).astype(BF16)
-        dot = lambda a: jnp.dot(a, zhot, preferred_element_type=F32)
-        picked = jnp.where(rhot, dot(high) + dot(low), 0.0)
-        picks.append(jnp.sum(picked, axis=0, keepdims=True))
+        if kind == "last":
+            picks.append(pick(bef[tx : 2 * tx, 0:ty]))
+        else:
+            fields_ref[step - 1] = bef[tx : 2 * tx, 0:ty]
     cur, bef = (one, two) if W % 2 == 0 else (two, one)
     if kind == "last":
         out_cur[...] = cur[tx : 2 * tx, 0:ty]
         out_bef[...] = bef[tx : 2 * tx, 0:ty]
         series_ref[...] = jnp.concatenate([*(d[...] for d in done), *picks])
         return
-    for k, pick in enumerate(picks):
-        sample_ref[pl.ds(k, 1), :] = pick
     cut = (lambda v: v[:, 0:ty]) if kind == "inner" else (lambda v: narrow(v, ty))
     state_ref[0:tx] = cut(cur[tx : 2 * tx])
     state_ref[tx:] = cut(bef[tx - 1 : 2 * tx + 1])
@@ -250,7 +268,8 @@
     return 2.0 * s * c, 1.0 - 2.0 * s * s
 
 
-def waves_kernel(tx, ty, nz, cell_ref, angle_ref, high_ref, low_ref):
+def waves_kernel(tx, ty, nz, cell_ref, angle_ref, high_ref, low_ref, token_ref):
+    token_ref[...] = jnp.zeros(token_ref.shape, F32)
     slots = cell_ref.shape[1] // 2
     cells = jnp.broadcast_to(cell_ref[...], (8, 2 * slots)).astype(F32)
     cells = jnp.concatenate([cells] * (2 * slots // 8)).T[0:slots, 0:1]
@@ -344,10 +363,10 @@
         own, x_b, x_a = call(
             lambda *refs: join_kernel(fields, tx, ty, *refs), [shape(*state.shape[:1], *wide[1:]), size, size], name="join", cost=cover
         )(state, *y_rows)
-        return [own, *ahead, *swap(x_b, x_a, "gx"), cells]
+        return [own, *ahead, *swap(x_b, x_a, "gx")]
 
     def exchange_x(own, *messages):
-        return [own, *swap(*messages, "gx"), cells]
+        return [own, *swap(*messages, "gx")]
 
     cells = jnp.concatenate([slot_cell, slot_cell])[None, :]
     tile = (tx, ty, nz)
@@ -359,26 +378,30 @@
         name="prepare",
         specs=[hbm] * 3,
     )(*(pltpu.with_memory_space_constraint(v, pltpu.HBM) for v in (pressure, previous, material)))
-    part = shape(W, 128)
+    observers = angles.shape[1]
+    half = jax.ShapeDtypeStruct((128, observers), BF16)
+    high, low, token = call(lambda *refs: waves_kernel(tx, ty, nz, *refs), [half, half, shape(8, 128)], name="waves")(cells, angles)
+
+    fields = shape(W, *tile)
+    sample = lambda *v: call(sample_kernel, shape(len(v) * W, 128), name="sample")(cells, *v)
     message = count(message_tiles(2, tx, ty, W))
-    between = [shape(2 * tx + 2, *thin[1:]), message, message, part]
-    *own, first, p, q, r, p4, q4, r4 = call(
-        window("first"), between + [shape(*wide)] * 3 + [shape(*thin)] * 3, scratch(wide), name="window_first"
-    )(*exchange_both(3, *state))
+    between = [shape(2 * tx + 2, *thin[1:]), message, message, fields]
+    *own, first, p, q, r = call(window("first"), between + [shape(*wide)] * 3, scratch(wide), name="window_first")(
+        *exchange_both(3, *state), token
+    )
+    coefs = call(lambda *refs: narrow_kernel(ty, *refs), [shape(*thin)] * 3, name="narrow")(p, q, r)
     *state, second = call(
         window("inner"),
-        [shape(2 * tx + 2, ty, nz)] + [shape(2 * tx, Y, nz)] * 2 + [count(split_tiles(2, tx, ty, 2 * W)[0])] * 2 + [part],
+        [shape(2 * tx + 2, ty, nz)] + [shape(2 * tx, Y, nz)] * 2 + [count(split_tiles(2, tx, ty, 2 * W)[0])] * 2 + [fields],
         scratch(thin),
         name="window_inner",
-    )(*exchange_x(*own), p4, q4, r4)
-    *own, third = call(window("wide"), between, scratch(wide), name="window_wide")(*exchange_both(2, *state), p, q, r)
+    )(*exchange_x(*own), *coefs)
+    early = sample(first, second)
+    *own, third = call(window("wide"), between, scratch(wide), name="window_wide")(*exchange_both(2, *state), early, p, q, r)
     current, before, series = call(
         window("last"), [shape(*tile), shape(*tile), shape(STEPS, 128)], scratch(thin), name="window_last"
-    )(*exchange_x(*own), p4, q4, r4, first, second, third)
-
-    observers = angles.shape[1]
-    half = jax.ShapeDtypeStruct((128, observers), BF16)
-    high, low = call(lambda *refs: waves_kernel(tx, ty, nz, *refs), [half, half], name="waves")(cells, angles)
+    )(*exchange_x(*own), cells, *coefs, early, sample(third))
+
     share = call(project_kernel, shape(2 * ngy, STEPS, 128), name="project")(series, high, low)
     rows = [list(range(k, k + 2 * ngy)) for k in range(0, ngx * ngy, 2 * ngy)]
     share = lax.all_to_all(share, ("gx", "gy"), 0, 0, tiled=True, axis_index_groups=rows)

time: 134 us -> 132 us (0.985)
    pallas_call x2 -> x5, Pallas kernels: 4.67 us -> 5.47 us  [the longest x1 2.3 us: body(): call(window('first'), between + [shape(*wide)] * 3, scratch(wide), name='...]
  transfers between devices with their start and end apart: 17 -> 17, of which waited for: 6 -> 5; matrix products, arithmetic and copies ran while one was open for 0% -> 0% of each run, Pallas kernels for 2% -> 3%
where the time goes in v8:
time: 132 us
  starting transfers between devices  61.7 us (47%)
  blocking collectives  48.5 us (37%)
  Pallas kernels  13.5 us (10%)
  waiting for transfers between devices  6.98 us (5%)
    ppermute x8, starting transfers between devices, swap(): got = lax.ppermute(odd_even, axis, pairs)  29.4 us
    all_to_all x1, blocking collectives, body(): lax.all_to_all(share, 'gx', 0, 0, tiled=True, axis_index_groups=chips)  27.9 us
    ppermute x8, starting transfers between devices, swap(): lax.ppermute(even_odd, axis, [(i, i ^ 1) for i in range(count) if i ^ 1 <...  26.9 us
    all_to_all x1, blocking collectives, body(): lax.all_to_all(share, ('gx', 'gy'), 0, 0, tiled=True, axis_index_groups=r...  20.6 us
    ppermute x8, waiting for transfers between devices, swap(): got = lax.ppermute(odd_even, axis, pairs)  5.7 us
    ppermute x1, starting transfers between devices, body(): other = lax.ppermute(traces, 'gx', [(i, i ^ 1) for i in range(ngx)])  5.33 us
  transfers between devices with their start and end apart: 17, of which 5 were waited for; matrix products, arithmetic and copies ran while one was open for 0% of the time, Pallas kernels for 3%

profile of v8, /device:TPU:1, one launch (start us, length us, event | category | flops | bytes accessed | tf_op | source)
XLA Modules:
  0.0 131.6 jit_solution(8313516548259903593)
XLA Ops:
  2.6 9.8 %collective-permute-start.1 = (f32[12,8,384]{2,1,0:T(8,128)S(1)}, f32[12,8,384]{2,1,0:T(8,128)S(1)}, u32[]{:S(2)}, u32[]{:S(2)}) collective-permute-start(f32[12,8,384]{2,1,0:T(8,128)S(1)} %get-tuple-element.42), channel_id=1, source_target_pairs={{0,1},{1,0},{2,3},{3,2},{4,5},{5,4},{6,7},{7,6},{8,9},{9,8},{10,11... | collective-permute-start | bytes 442376 | tf_op jit(solution)/shard_map/ppermute | solution.py:343
  12.4 5.1 %collective-permute-start.2 = (f32[44,8,384]{2,1,0:T(8,128)S(1)}, f32[44,8,384]{2,1,0:T(8,128)S(1)}, u32[]{:S(2)}, u32[]{:S(2)}) collective-permute-start(f32[44,8,384]{2,1,0:T(8,128)S(1)} %get-tuple-element.44), channel_id=1, source_target_pairs={{16,32},{32,16},{48,64},{64,48},{80,96},{96,80},{112,128},{128,112... | collective-permute-start | bytes 1622024 | tf_op jit(solution)/shard_map/ppermute | solution.py:342
  17.5 1.9 %collective-permute-start.3 = (f32[44,8,384]{2,1,0:T(8,128)S(1)}, f32[44,8,384]{2,1,0:T(8,128)S(1)}, u32[]{:S(2)}, u32[]{:S(2)}) collective-permute-start(f32[44,8,384]{2,1,0:T(8,128)S(1)} %get-tuple-element.45), channel_id=1, source_target_pairs={{0,16},{16,0},{32,48},{48,32},{64,80},{80,64},{96,112},{112,96},{1... | collective-permute-start | bytes 1622024 | tf_op jit(solution)/shard_map/ppermute | solution.py:343
  19.6 4.7 %collective-permute-start.4 = (f32[19,8,384]{2,1,0:T(8,128)S(1)}, f32[19,8,384]{2,1,0:T(8,128)S(1)}, u32[]{:S(2)}, u32[]{:S(2)}) collective-permute-start(f32[19,8,384]{2,1,0:T(8,128)S(1)} %get-tuple-element.46), channel_id=1, source_target_pairs={{16,32},{32,16},{48,64},{64,48},{80,96},{96,80},{112,128},{128,112... | collective-permute-start | bytes 700424 | tf_op jit(solution)/shard_map/ppermute | solution.py:342
  24.3 1.9 %collective-permute-start.5 = (f32[19,8,384]{2,1,0:T(8,128)S(1)}, f32[19,8,384]{2,1,0:T(8,128)S(1)}, u32[]{:S(2)}, u32[]{:S(2)}) collective-permute-start(f32[19,8,384]{2,1,0:T(8,128)S(1)} %get-tuple-element.47), channel_id=1, source_target_pairs={{0,16},{16,0},{32,48},{48,32},{64,80},{80,64},{96,112},{112,96},{1... | collective-permute-start | bytes 700424 | tf_op jit(solution)/shard_map/ppermute | solution.py:343
  26.3 2.0 %waves.1 = (bf16[128,4096]{1,0:T(8,128)(2,1)S(1)}, bf16[128,4096]{1,0:T(8,128)(2,1)S(1)}, f32[8,128]{1,0:T(8,128)S(1)}) custom-call(s32[1,128]{1,0:T(1,128)S(1)} %add_bitcast_fusion.refs_0_.cell_ref.refs_3_, f32[2,4096]{1,0:T(2,128)S(1)} %copy-done), custom_call_target="tpu_custom_call" | custom-call | tf_op jit(solution)/shard_map/waves/pallas_call | solution.py:383
  28.4 2.3 %window_first.1 = (f32[10,40,384]{2,1,0:T(8,128)S(1)}, f32[28,8,384]{2,1,0:T(8,128)S(1)}, f32[28,8,384]{2,1,0:T(8,128)S(1)}, f32[4,4,32,384]{3,2,1,0:T(8,128)S(1...) custom-call(f32[12,48,384]{2,1,0:T(8,128)S(1)} %get-tuple-element.43.refs_0_, ...), custom_call_target="tpu_custom_call" | custom-call | tf_op jit(solution)/shard_map/window_first/pallas_call | solution.py:389
  30.7 4.4 %collective-permute-start.6 = (f32[28,8,384]{2,1,0:T(8,128)S(1)}, f32[28,8,384]{2,1,0:T(8,128)S(1)}, u32[]{:S(2)}, u32[]{:S(2)}) collective-permute-start(f32[28,8,384]{2,1,0:T(8,128)S(1)} %get-tuple-element.50), channel_id=1, source_target_pairs={{16,32},{32,16},{48,64},{64,48},{80,96},{96,80},{112,128},{128,112... | collective-permute-start | bytes 1032200 | tf_op jit(solution)/shard_map/ppermute | solution.py:342
  35.1 1.9 %collective-permute-start.7 = (f32[28,8,384]{2,1,0:T(8,128)S(1)}, f32[28,8,384]{2,1,0:T(8,128)S(1)}, u32[]{:S(2)}, u32[]{:S(2)}) collective-permute-start(f32[28,8,384]{2,1,0:T(8,128)S(1)} %get-tuple-element.51), channel_id=1, source_target_pairs={{0,16},{16,0},{32,48},{48,32},{64,80},{80,64},{96,112},{112,96},{1... | collective-permute-start | bytes 1032200 | tf_op jit(solution)/shard_map/ppermute | solution.py:343
  37.2 2.8 %collective-permute-done.6.refs_1_ = f32[28,8,384]{2,1,0:T(8,128)S(1)} collective-permute-done((f32[28,8,384]{2,1,0:T(8,128)S(1)}, f32[28,8,384]{2,1,0:T(8,128)S(1)}, u32[]{:S(2)}, u32[]{:S(2)}) %collective-permute-start.6) | collective-permute-done | bytes 344096 | tf_op jit(solution)/shard_map/ppermute | solution.py:342
  40.0 1.4 %window_inner.1 = (f32[10,32,384]{2,1,0:T(8,128)S(1)}, f32[8,8,384]{2,1,0:T(8,128)S(1)}, f32[8,8,384]{2,1,0:T(8,128)S(1)}, f32[24,8,384]{2,1,0:T(8,128)S(1)}, f3...) custom-call(f32[10,40,384]{2,1,0:T(8,128)S(1)} %get-tuple-element.49.refs_0_, ...), custom_call_target="tpu_custom_call" | custom-call | tf_op jit(solution)/shard_map/window_inner/pallas_call | solution.py:393
  42.1 5.6 %collective-permute-start.9 = (f32[8,8,384]{2,1,0:T(8,128)S(1)}, f32[8,8,384]{2,1,0:T(8,128)S(1)}, u32[]{:S(2)}, u32[]{:S(2)}) collective-permute-start(f32[8,8,384]{2,1,0:T(8,128)S(1)} %get-tuple-element.60), channel_id=1, source_target_pairs={{0,1},{1,0},{2,3},{3,2},{4,5},{5,4},{6,7},{7,6},{8,9},{9,8},{10,11... | collective-permute-start | bytes 294920 | tf_op jit(solution)/shard_map/ppermute | solution.py:343
  47.7 4.2 %collective-permute-start.10 = (f32[24,8,384]{2,1,0:T(8,128)S(1)}, f32[24,8,384]{2,1,0:T(8,128)S(1)}, u32[]{:S(2)}, u32[]{:S(2)}) collective-permute-start(f32[24,8,384]{2,1,0:T(8,128)S(1)} %get-tuple-element.62), channel_id=1, source_target_pairs={{16,32},{32,16},{48,64},{64,48},{80,96},{96,80},{112,128},{128,112... | collective-permute-start | bytes 884744 | tf_op jit(solution)/shard_map/ppermute | solution.py:342
  51.9 1.9 %collective-permute-start.11 = (f32[24,8,384]{2,1,0:T(8,128)S(1)}, f32[24,8,384]{2,1,0:T(8,128)S(1)}, u32[]{:S(2)}, u32[]{:S(2)}) collective-permute-start(f32[24,8,384]{2,1,0:T(8,128)S(1)} %get-tuple-element.63), channel_id=1, source_target_pairs={{0,16},{16,0},{32,48},{48,32},{64,80},{80,64},{96,112},{112,96},{1... | collective-permute-start | bytes 884744 | tf_op jit(solution)/shard_map/ppermute | solution.py:343
  54.0 4.6 %collective-permute-start.12 = (f32[12,8,384]{2,1,0:T(8,128)S(1)}, f32[12,8,384]{2,1,0:T(8,128)S(1)}, u32[]{:S(2)}, u32[]{:S(2)}) collective-permute-start(f32[12,8,384]{2,1,0:T(8,128)S(1)} %get-tuple-element.64), channel_id=1, source_target_pairs={{16,32},{32,16},{48,64},{64,48},{80,96},{96,80},{112,128},{128,112... | collective-permute-start | bytes 442376 | tf_op jit(solution)/shard_map/ppermute | solution.py:342
  58.6 1.9 %collective-permute-start.13 = (f32[12,8,384]{2,1,0:T(8,128)S(1)}, f32[12,8,384]{2,1,0:T(8,128)S(1)}, u32[]{:S(2)}, u32[]{:S(2)}) collective-permute-start(f32[12,8,384]{2,1,0:T(8,128)S(1)} %get-tuple-element.65), channel_id=1, source_target_pairs={{0,16},{16,0},{32,48},{48,32},{64,80},{80,64},{96,112},{112,96},{1... | collective-permute-start | bytes 442376 | tf_op jit(solution)/shard_map/ppermute | solution.py:343
  61.8 1.6 %window_wide.1 = (f32[10,40,384]{2,1,0:T(8,128)S(1)}, f32[28,8,384]{2,1,0:T(8,128)S(1)}, f32[28,8,384]{2,1,0:T(8,128)S(1)}, f32[4,4,32,384]{3,2,1,0:T(8,128)S(1)}) custom-call(f32[10,48,384]{2,1,0:T(8,128)S(1)} %get-tuple-element.61.refs_0_, f32[24,8,384]{2,1,0:T(8,128)S(1)} %collective-permute-done.10.refs_1_, ...), custom_call_target="tpu_custom_call" | custom-call | tf_op jit(solution)/shard_map/window_wide/pallas_call | solution.py:400
  63.5 5.0 %collective-permute-start.14 = (f32[28,8,384]{2,1,0:T(8,128)S(1)}, f32[28,8,384]{2,1,0:T(8,128)S(1)}, u32[]{:S(2)}, u32[]{:S(2)}) collective-permute-start(f32[28,8,384]{2,1,0:T(8,128)S(1)} %get-tuple-element.69), channel_id=1, source_target_pairs={{16,32},{32,16},{48,64},{64,48},{80,96},{96,80},{112,128},{128,112... | collective-permute-start | bytes 1032200 | tf_op jit(solution)/shard_map/ppermute | solution.py:342
  68.5 1.9 %collective-permute-start.15 = (f32[28,8,384]{2,1,0:T(8,128)S(1)}, f32[28,8,384]{2,1,0:T(8,128)S(1)}, u32[]{:S(2)}, u32[]{:S(2)}) collective-permute-start(f32[28,8,384]{2,1,0:T(8,128)S(1)} %get-tuple-element.70), channel_id=1, source_target_pairs={{0,16},{16,0},{32,48},{48,32},{64,80},{80,64},{96,112},{112,96},{1... | collective-permute-start | bytes 1032200 | tf_op jit(solution)/shard_map/ppermute | solution.py:343
  70.8 2.6 %collective-permute-done.14.refs_1_ = f32[28,8,384]{2,1,0:T(8,128)S(1)} collective-permute-done((f32[28,8,384]{2,1,0:T(8,128)S(1)}, f32[28,8,384]{2,1,0:T(8,128)S(1)}, u32[]{:S(2)}, u32[]{:S(2)}) %collective-permute-start.14) | collective-permute-done | bytes 344096 | tf_op jit(solution)/shard_map/ppermute | solution.py:342
  73.5 2.3 %window_last.1 = (f32[4,32,384]{2,1,0:T(8,128)}, f32[4,32,384]{2,1,0:T(8,128)}, f32[16,128]{1,0:T(8,128)S(1)}) custom-call(f32[10,40,384]{2,1,0:T(8,128)S(1)} %get-tuple-element.68.refs_0_, f32[28,8,384]{2,1,0:T(8,128)S(1)} %collective-permute-done.14.refs_1_, f32[28,8,384]{2,1,0:T(8,128)S(1)} %collective-permute-done.15.refs_2_, ...), custom_call_target="tpu_custom_call" | custom-call | tf_op jit(solution)/shard_map/window_last/pallas_call | solution.py:401
  76.2 20.6 %all_to_all.10.part_ref = f32[32,16,128]{2,1,0:T(8,128)S(1)} all-to-all(f32[32,16,128]{2,1,0:T(8,128)S(1)} %project.1), channel_id=1, replica_groups={{0,1,2,3,4,5,6,7,8,9,10,11,12,13,14,15,16,17,18,19,20,21,22,23,24,25,26..., dimensions={0} | all-to-all | bytes 524288 | tf_op jit(solution)/shard_map/all_to_all | solution.py:407
  96.8 27.9 %all_to_all.11.part_ref = f32[24,16,128]{2,1,0:T(8,128)S(1)} all-to-all(f32[24,16,128]{2,1,0:T(8,128)S(1)} %row_total.1), channel_id=1, replica_groups={{0,32,64,96,128,160,192,224,256,288,320,352,384,416,448,480,512,544,576..., dimensions={0} | all-to-all | bytes 393216 | tf_op jit(solution)/shard_map/all_to_all | solution.py:410
  124.7 5.3 %collective-permute-start.16 = (f32[1,16,128]{2,1,0:T(8,128)S(1)}, f32[1,16,128]{2,1,0:T(8,128)S(1)}, u32[]{:S(2)}, u32[]{:S(2)}) collective-permute-start(f32[1,16,128]{2,1,0:T(8,128)S(1)} %total.1.refs_0_), channel_id=1, source_target_pairs={{0,16},{16,0},{32,48},{48,32},{64,80},{80,64},{96,112},{112,96},{1... | collective-permute-start | bytes 24584 | tf_op jit(solution)/shard_map/ppermute | solution.py:412
  (34 shorter events, 6.8 us)
Async XLA Ops:
  1.9 17.6 %collective-permute-start = (f32[12,8,384]{2,1,0:T(8,128)S(1)}, f32[12,8,384]{2,1,0:T(8,128)S(1)}, u32[]{:S(2)}, u32[]{:S(2)}) collective-permute-start(f32[12,8,384]{2,1,0:T(8,128)S(1)} %get-tuple-element.41), channel_id=1, source_target_pairs={{1,2},{2,1},{3,4},{4,3},{5,6},{6,5},{7,8},{8,7},{9,10},{10,9},{11,... | collective-permute-start | bytes 442376 | tf_op jit(solution)/shard_map/ppermute | solution.py:342
  2.6 16.9 %collective-permute-start.1 = (f32[12,8,384]{2,1,0:T(8,128)S(1)}, f32[12,8,384]{2,1,0:T(8,128)S(1)}, u32[]{:S(2)}, u32[]{:S(2)}) collective-permute-start(f32[12,8,384]{2,1,0:T(8,128)S(1)} %get-tuple-element.42), channel_id=1, source_target_pairs={{0,1},{1,0},{2,3},{3,2},{4,5},{5,4},{6,7},{7,6},{8,9},{9,8},{10,11... | collective-permute-start | bytes 442376 | tf_op jit(solution)/shard_map/ppermute | solution.py:343
  12.4 16.0 %collective-permute-start.2 = (f32[44,8,384]{2,1,0:T(8,128)S(1)}, f32[44,8,384]{2,1,0:T(8,128)S(1)}, u32[]{:S(2)}, u32[]{:S(2)}) collective-permute-start(f32[44,8,384]{2,1,0:T(8,128)S(1)} %get-tuple-element.44), channel_id=1, source_target_pairs={{16,32},{32,16},{48,64},{64,48},{80,96},{96,80},{112,128},{128,112... | collective-permute-start | bytes 1622024 | tf_op jit(solution)/shard_map/ppermute | solution.py:342
  17.5 10.9 %collective-permute-start.3 = (f32[44,8,384]{2,1,0:T(8,128)S(1)}, f32[44,8,384]{2,1,0:T(8,128)S(1)}, u32[]{:S(2)}, u32[]{:S(2)}) collective-permute-start(f32[44,8,384]{2,1,0:T(8,128)S(1)} %get-tuple-element.45), channel_id=1, source_target_pairs={{0,16},{16,0},{32,48},{48,32},{64,80},{80,64},{96,112},{112,96},{1... | collective-permute-start | bytes 1622024 | tf_op jit(solution)/shard_map/ppermute | solution.py:343
  19.5 6.9 %copy-start = (f32[2,4096]{1,0:T(2,128)S(1)}, f32[2,4096]{1,0:T(2,128)}, u32[]{:S(2)}) copy-start(f32[2,4096]{1,0:T(2,128)} %refs_1_.1) | copy-start | bytes 98308
  19.6 6.7 %copy-start.2 = (s32[64]{0:T(128)S(1)}, s32[64]{0:T(128)}, u32[]{:S(2)}) copy-start(s32[64]{0:T(128)} %param.9) | copy-start | bytes 772
  19.6 8.8 %collective-permute-start.4 = (f32[19,8,384]{2,1,0:T(8,128)S(1)}, f32[19,8,384]{2,1,0:T(8,128)S(1)}, u32[]{:S(2)}, u32[]{:S(2)}) collective-permute-start(f32[19,8,384]{2,1,0:T(8,128)S(1)} %get-tuple-element.46), channel_id=1, source_target_pairs={{16,32},{32,16},{48,64},{64,48},{80,96},{96,80},{112,128},{128,112... | collective-permute-start | bytes 700424 | tf_op jit(solution)/shard_map/ppermute | solution.py:342
  24.3 4.0 %collective-permute-start.5 = (f32[19,8,384]{2,1,0:T(8,128)S(1)}, f32[19,8,384]{2,1,0:T(8,128)S(1)}, u32[]{:S(2)}, u32[]{:S(2)}) collective-permute-start(f32[19,8,384]{2,1,0:T(8,128)S(1)} %get-tuple-element.47), channel_id=1, source_target_pairs={{0,16},{16,0},{32,48},{48,32},{64,80},{80,64},{96,112},{112,96},{1... | collective-permute-start | bytes 700424 | tf_op jit(solution)/shard_map/ppermute | solution.py:343
  30.7 9.3 %collective-permute-start.6 = (f32[28,8,384]{2,1,0:T(8,128)S(1)}, f32[28,8,384]{2,1,0:T(8,128)S(1)}, u32[]{:S(2)}, u32[]{:S(2)}) collective-permute-start(f32[28,8,384]{2,1,0:T(8,128)S(1)} %get-tuple-element.50), channel_id=1, source_target_pairs={{16,32},{32,16},{48,64},{64,48},{80,96},{96,80},{112,128},{128,112... | collective-permute-start | bytes 1032200 | tf_op jit(solution)/shard_map/ppermute | solution.py:342
  35.1 4.9 %collective-permute-start.7 = (f32[28,8,384]{2,1,0:T(8,128)S(1)}, f32[28,8,384]{2,1,0:T(8,128)S(1)}, u32[]{:S(2)}, u32[]{:S(2)}) collective-permute-start(f32[28,8,384]{2,1,0:T(8,128)S(1)} %get-tuple-element.51), channel_id=1, source_target_pairs={{0,16},{16,0},{32,48},{48,32},{64,80},{80,64},{96,112},{112,96},{1... | collective-permute-start | bytes 1032200 | tf_op jit(solution)/shard_map/ppermute | solution.py:343
  41.4 12.4 %collective-permute-start.8 = (f32[8,8,384]{2,1,0:T(8,128)S(1)}, f32[8,8,384]{2,1,0:T(8,128)S(1)}, u32[]{:S(2)}, u32[]{:S(2)}) collective-permute-start(f32[8,8,384]{2,1,0:T(8,128)S(1)} %get-tuple-element.59), channel_id=1, source_target_pairs={{1,2},{2,1},{3,4},{4,3},{5,6},{6,5},{7,8},{8,7},{9,10},{10,9},{11,... | collective-permute-start | bytes 294920 | tf_op jit(solution)/shard_map/ppermute | solution.py:342
  42.1 11.8 %collective-permute-start.9 = (f32[8,8,384]{2,1,0:T(8,128)S(1)}, f32[8,8,384]{2,1,0:T(8,128)S(1)}, u32[]{:S(2)}, u32[]{:S(2)}) collective-permute-start(f32[8,8,384]{2,1,0:T(8,128)S(1)} %get-tuple-element.60), channel_id=1, source_target_pairs={{0,1},{1,0},{2,3},{3,2},{4,5},{5,4},{6,7},{7,6},{8,9},{9,8},{10,11... | collective-permute-start | bytes 294920 | tf_op jit(solution)/shard_map/ppermute | solution.py:343
  47.7 14.1 %collective-permute-start.10 = (f32[24,8,384]{2,1,0:T(8,128)S(1)}, f32[24,8,384]{2,1,0:T(8,128)S(1)}, u32[]{:S(2)}, u32[]{:S(2)}) collective-permute-start(f32[24,8,384]{2,1,0:T(8,128)S(1)} %get-tuple-element.62), channel_id=1, source_target_pairs={{16,32},{32,16},{48,64},{64,48},{80,96},{96,80},{112,128},{128,112... | collective-permute-start | bytes 884744 | tf_op jit(solution)/shard_map/ppermute | solution.py:342
  51.9 9.9 %collective-permute-start.11 = (f32[24,8,384]{2,1,0:T(8,128)S(1)}, f32[24,8,384]{2,1,0:T(8,128)S(1)}, u32[]{:S(2)}, u32[]{:S(2)}) collective-permute-start(f32[24,8,384]{2,1,0:T(8,128)S(1)} %get-tuple-element.63), channel_id=1, source_target_pairs={{0,16},{16,0},{32,48},{48,32},{64,80},{80,64},{96,112},{112,96},{1... | collective-permute-start | bytes 884744 | tf_op jit(solution)/shard_map/ppermute | solution.py:343
  54.0 7.4 %collective-permute-start.12 = (f32[12,8,384]{2,1,0:T(8,128)S(1)}, f32[12,8,384]{2,1,0:T(8,128)S(1)}, u32[]{:S(2)}, u32[]{:S(2)}) collective-permute-start(f32[12,8,384]{2,1,0:T(8,128)S(1)} %get-tuple-element.64), channel_id=1, source_target_pairs={{16,32},{32,16},{48,64},{64,48},{80,96},{96,80},{112,128},{128,112... | collective-permute-start | bytes 442376 | tf_op jit(solution)/shard_map/ppermute | solution.py:342
  58.6 3.3 %collective-permute-start.13 = (f32[12,8,384]{2,1,0:T(8,128)S(1)}, f32[12,8,384]{2,1,0:T(8,128)S(1)}, u32[]{:S(2)}, u32[]{:S(2)}) collective-permute-start(f32[12,8,384]{2,1,0:T(8,128)S(1)} %get-tuple-element.65), channel_id=1, source_target_pairs={{0,16},{16,0},{32,48},{48,32},{64,80},{80,64},{96,112},{112,96},{1... | collective-permute-start | bytes 442376 | tf_op jit(solution)/shard_map/ppermute | solution.py:343
  63.5 10.0 %collective-permute-start.14 = (f32[28,8,384]{2,1,0:T(8,128)S(1)}, f32[28,8,384]{2,1,0:T(8,128)S(1)}, u32[]{:S(2)}, u32[]{:S(2)}) collective-permute-start(f32[28,8,384]{2,1,0:T(8,128)S(1)} %get-tuple-element.69), channel_id=1, source_target_pairs={{16,32},{32,16},{48,64},{64,48},{80,96},{96,80},{112,128},{128,112... | collective-permute-start | bytes 1032200 | tf_op jit(solution)/shard_map/ppermute | solution.py:342
  68.5 4.9 %collective-permute-start.15 = (f32[28,8,384]{2,1,0:T(8,128)S(1)}, f32[28,8,384]{2,1,0:T(8,128)S(1)}, u32[]{:S(2)}, u32[]{:S(2)}) collective-permute-start(f32[28,8,384]{2,1,0:T(8,128)S(1)} %get-tuple-element.70), channel_id=1, source_target_pairs={{0,16},{16,0},{32,48},{48,32},{64,80},{80,64},{96,112},{112,96},{1... | collective-permute-start | bytes 1032200 | tf_op jit(solution)/shard_map/ppermute | solution.py:343
  124.7 6.2 %copy-start.1 = (f32[2,8,256]{2,1,0:T(8,128)S(1)}, f32[2,8,256]{2,1,0:T(8,128)}, u32[]{:S(2)}) copy-start(f32[2,8,256]{2,1,0:T(8,128)} %refs_2_.1) | copy-start | bytes 49156
  124.7 6.1 %collective-permute-start.16 = (f32[1,16,128]{2,1,0:T(8,128)S(1)}, f32[1,16,128]{2,1,0:T(8,128)S(1)}, u32[]{:S(2)}, u32[]{:S(2)}) collective-permute-start(f32[1,16,128]{2,1,0:T(8,128)S(1)} %total.1.refs_0_), channel_id=1, source_target_pairs={{0,16},{16,0},{32,48},{48,32},{64,80},{80,64},{96,112},{112,96},{1... | collective-permute-start | bytes 24584 | tf_op jit(solution)/shard_map/ppermute | solution.py:412

commit v9 on v8

--- a/solution.py
+++ b/solution.py
@@ -15,8 +15,10 @@
 TURN = 6.283185307179586
 
 
-def call(kernel, outs, scratch=(), name=None, specs=None, cost=None):
+def call(kernel, outs, scratch=(), name=None, specs=None, cost=None, out_specs=None):
     more = {} if specs is None else {"in_specs": specs}
+    if out_specs is not None:
+        more["out_specs"] = out_specs
     return pl.pallas_call(
         kernel,
         out_shape=outs,
@@ -40,7 +42,31 @@
             ref[k * tx : (k + 1) * tx] = state[lo:hi, pl.ds(pl.multiple_of(row, 8), Y)]
 
 
-def prepare_kernel(cur_hbm, bef_hbm, mat_hbm, state_ref, y_b, y_a, x_b, x_a, cur_ref, bef_ref, mat_ref, sems):
+def openness(mat):
+    return jnp.where(mat == 1, 0.0, jnp.where(mat == 2, F32(1.0) / F32(1.5), F32(1.0)))
+
+
+def edges_kernel(cur_hbm, bef_hbm, mat_hbm, y_b, y_a, cur_ref, bef_ref, mat_ref, sems):
+    tx, ty, _ = cur_hbm.shape
+    even = lax.axis_index("gy") % 2 == 0
+    top, bottom = ty - Y, 0
+    copies = []
+    for k, (src, dst) in enumerate(((mat_hbm, mat_ref), (cur_hbm, cur_ref), (bef_hbm, bef_ref))):
+        for side, row in enumerate((jnp.where(even, bottom, top), jnp.where(even, top, bottom))):
+            rows = pl.ds(pl.multiple_of(row, 8), Y)
+            copies.append(pltpu.make_async_copy(src.at[:, rows], dst.at[side], sems.at[2 * k + side]))
+    for copy in copies:
+        copy.start()
+    for copy in copies:
+        copy.wait()
+    for side, ref in enumerate((y_b, y_a)):
+        mat = mat_ref[side]
+        ref[0:tx] = jnp.where(mat == 1, 0.0, cur_ref[side])
+        ref[tx : 2 * tx] = jnp.where(mat == 1, 0.0, bef_ref[side])
+        ref[2 * tx :] = openness(mat)
+
+
+def prepare_kernel(cur_hbm, bef_hbm, mat_hbm, state_ref, x_b, x_a, cur_ref, bef_ref, mat_ref, sems):
     tx, ty, _ = cur_ref.shape
     pairs = ((mat_hbm, mat_ref), (cur_hbm, cur_ref), (bef_hbm, bef_ref))
     copies = [pltpu.make_async_copy(src, dst, sems.at[k]) for k, (src, dst) in enumerate(pairs)]
@@ -48,12 +74,11 @@
         copy.start()
     copies[0].wait()
     mat = mat_ref[...]
-    state_ref[2 * tx :] = jnp.where(mat == 1, 0.0, jnp.where(mat == 2, F32(1.0) / F32(1.5), F32(1.0)))
+    state_ref[2 * tx :] = openness(mat)
     copies[1].wait()
     state_ref[0:tx] = jnp.where(mat == 1, 0.0, cur_ref[...])
     copies[2].wait()
     state_ref[tx : 2 * tx] = jnp.where(mat == 1, 0.0, bef_ref[...])
-    write_edges(state_ref, y_b, y_a, 3, tx, ty)
     write_messages(state_ref, x_b, x_a, split_tiles(3, tx, ty, 2 * W)[0], 3, tx, ty)
 
 
@@ -371,13 +396,23 @@
     cells = jnp.concatenate([slot_cell, slot_cell])[None, :]
     tile = (tx, ty, nz)
     hbm = pl.BlockSpec(memory_space=pltpu.HBM)
-    state = call(
+    args = [pltpu.with_memory_space_constraint(v, pltpu.HBM) for v in (pressure, previous, material)]
+    edge = (2, tx, Y, nz)
+    y_messages = call(
+        edges_kernel,
+        [shape(3 * tx, Y, nz)] * 2,
+        [pltpu.VMEM(edge, F32), pltpu.VMEM(edge, F32), pltpu.VMEM(edge, jnp.int32), pltpu.SemaphoreType.DMA((6,))],
+        name="edges",
+        specs=[hbm] * 3,
+    )(*args)
+    state, *x_messages = call(
         prepare_kernel,
-        [shape(3 * tx, ty, nz)] + [shape(3 * tx, Y, nz)] * 2 + [count(split_tiles(3, tx, ty, 2 * W)[0])] * 2,
+        [shape(3 * tx, ty, nz)] + [count(split_tiles(3, tx, ty, 2 * W)[0])] * 2,
         [pltpu.VMEM(tile, F32), pltpu.VMEM(tile, F32), pltpu.VMEM(tile, jnp.int32), pltpu.SemaphoreType.DMA((3,))],
         name="prepare",
         specs=[hbm] * 3,
-    )(*(pltpu.with_memory_space_constraint(v, pltpu.HBM) for v in (pressure, previous, material)))
+    )(*args)
+    state = [state, *y_messages, *x_messages]
     observers = angles.shape[1]
     half = jax.ShapeDtypeStruct((128, observers), BF16)
     high, low, token = call(lambda *refs: waves_kernel(tx, ty, nz, *refs), [half, half, shape(8, 128)], name="waves")(cells, angles)

time: 132 us -> 132 us (level)
  no operation moved by 1% of the time
where the time goes in v9:
time: 132 us; the launch traced here: 131 us
  starting transfers between devices  60.5 us (46%)
  blocking collectives  48.3 us (37%)
  Pallas kernels  14.5 us (11%)
  waiting for transfers between devices  6.98 us (5%)
    ppermute x8, starting transfers between devices, swap(): got = lax.ppermute(odd_even, axis, pairs)  29.1 us
    all_to_all x1, blocking collectives, body(): lax.all_to_all(share, 'gx', 0, 0, tiled=True, axis_index_groups=chips)  28.3 us
    ppermute x8, starting transfers between devices, swap(): lax.ppermute(even_odd, axis, [(i, i ^ 1) for i in range(count) if i ^ 1 <...  26 us
    all_to_all x1, blocking collectives, body(): lax.all_to_all(share, ('gx', 'gy'), 0, 0, tiled=True, axis_index_groups=r...  20 us
    ppermute x8, waiting for transfers between devices, swap(): got = lax.ppermute(odd_even, axis, pairs)  5.71 us
    ppermute x1, starting transfers between devices, body(): other = lax.ppermute(traces, 'gx', [(i, i ^ 1) for i in range(ngx)])  5.36 us
  transfers between devices with their start and end apart: 17, of which 5 were waited for; matrix products, arithmetic and copies ran while one was open for 0% of the time, Pallas kernels for 3%

profile of v9, /device:TPU:1, one launch (start us, length us, event | category | flops | bytes accessed | tf_op | source)
XLA Modules:
  0.0 131.3 jit_solution(820106227837229890)
XLA Ops:
  2.3 9.8 %collective-permute-start.1 = (f32[12,8,384]{2,1,0:T(8,128)S(1)}, f32[12,8,384]{2,1,0:T(8,128)S(1)}, u32[]{:S(2)}, u32[]{:S(2)}) collective-permute-start(f32[12,8,384]{2,1,0:T(8,128)S(1)} %get-tuple-element.42), channel_id=1, source_target_pairs={{0,1},{1,0},{2,3},{3,2},{4,5},{5,4},{6,7},{7,6},{8,9},{9,8},{10,11... | collective-permute-start | bytes 442376 | tf_op jit(solution)/shard_map/ppermute | solution.py:368
  13.4 5.1 %collective-permute-start.2 = (f32[44,8,384]{2,1,0:T(8,128)S(1)}, f32[44,8,384]{2,1,0:T(8,128)S(1)}, u32[]{:S(2)}, u32[]{:S(2)}) collective-permute-start(f32[44,8,384]{2,1,0:T(8,128)S(1)} %get-tuple-element.44), channel_id=1, source_target_pairs={{16,32},{32,16},{48,64},{64,48},{80,96},{96,80},{112,128},{128,112... | collective-permute-start | bytes 1622024 | tf_op jit(solution)/shard_map/ppermute | solution.py:367
  18.5 1.9 %collective-permute-start.3 = (f32[44,8,384]{2,1,0:T(8,128)S(1)}, f32[44,8,384]{2,1,0:T(8,128)S(1)}, u32[]{:S(2)}, u32[]{:S(2)}) collective-permute-start(f32[44,8,384]{2,1,0:T(8,128)S(1)} %get-tuple-element.45), channel_id=1, source_target_pairs={{0,16},{16,0},{32,48},{48,32},{64,80},{80,64},{96,112},{112,96},{1... | collective-permute-start | bytes 1622024 | tf_op jit(solution)/shard_map/ppermute | solution.py:368
  20.6 4.4 %collective-permute-start.4 = (f32[19,8,384]{2,1,0:T(8,128)S(1)}, f32[19,8,384]{2,1,0:T(8,128)S(1)}, u32[]{:S(2)}, u32[]{:S(2)}) collective-permute-start(f32[19,8,384]{2,1,0:T(8,128)S(1)} %get-tuple-element.46), channel_id=1, source_target_pairs={{16,32},{32,16},{48,64},{64,48},{80,96},{96,80},{112,128},{128,112... | collective-permute-start | bytes 700424 | tf_op jit(solution)/shard_map/ppermute | solution.py:367
  25.0 1.9 %collective-permute-start.5 = (f32[19,8,384]{2,1,0:T(8,128)S(1)}, f32[19,8,384]{2,1,0:T(8,128)S(1)}, u32[]{:S(2)}, u32[]{:S(2)}) collective-permute-start(f32[19,8,384]{2,1,0:T(8,128)S(1)} %get-tuple-element.47), channel_id=1, source_target_pairs={{0,16},{16,0},{32,48},{48,32},{64,80},{80,64},{96,112},{112,96},{1... | collective-permute-start | bytes 700424 | tf_op jit(solution)/shard_map/ppermute | solution.py:368
  27.0 2.0 %waves.1 = (bf16[128,4096]{1,0:T(8,128)(2,1)S(1)}, bf16[128,4096]{1,0:T(8,128)(2,1)S(1)}, f32[8,128]{1,0:T(8,128)S(1)}) custom-call(s32[1,128]{1,0:T(1,128)S(1)} %add_bitcast_fusion.refs_0_.cell_ref.refs_3_, f32[2,4096]{1,0:T(2,128)S(1)} %copy-done), custom_call_target="tpu_custom_call" | custom-call | tf_op jit(solution)/shard_map/waves/pallas_call | solution.py:418
  29.1 2.3 %window_first.1 = (f32[10,40,384]{2,1,0:T(8,128)S(1)}, f32[28,8,384]{2,1,0:T(8,128)S(1)}, f32[28,8,384]{2,1,0:T(8,128)S(1)}, f32[4,4,32,384]{3,2,1,0:T(8,128)S(1...) custom-call(f32[12,48,384]{2,1,0:T(8,128)S(1)} %get-tuple-element.43.refs_0_, ...), custom_call_target="tpu_custom_call" | custom-call | tf_op jit(solution)/shard_map/window_first/pallas_call | solution.py:424
  31.4 4.4 %collective-permute-start.6 = (f32[28,8,384]{2,1,0:T(8,128)S(1)}, f32[28,8,384]{2,1,0:T(8,128)S(1)}, u32[]{:S(2)}, u32[]{:S(2)}) collective-permute-start(f32[28,8,384]{2,1,0:T(8,128)S(1)} %get-tuple-element.50), channel_id=1, source_target_pairs={{16,32},{32,16},{48,64},{64,48},{80,96},{96,80},{112,128},{128,112... | collective-permute-start | bytes 1032200 | tf_op jit(solution)/shard_map/ppermute | solution.py:367
  35.8 1.9 %collective-permute-start.7 = (f32[28,8,384]{2,1,0:T(8,128)S(1)}, f32[28,8,384]{2,1,0:T(8,128)S(1)}, u32[]{:S(2)}, u32[]{:S(2)}) collective-permute-start(f32[28,8,384]{2,1,0:T(8,128)S(1)} %get-tuple-element.51), channel_id=1, source_target_pairs={{0,16},{16,0},{32,48},{48,32},{64,80},{80,64},{96,112},{112,96},{1... | collective-permute-start | bytes 1032200 | tf_op jit(solution)/shard_map/ppermute | solution.py:368
  37.9 2.8 %collective-permute-done.6.refs_1_ = f32[28,8,384]{2,1,0:T(8,128)S(1)} collective-permute-done((f32[28,8,384]{2,1,0:T(8,128)S(1)}, f32[28,8,384]{2,1,0:T(8,128)S(1)}, u32[]{:S(2)}, u32[]{:S(2)}) %collective-permute-start.6) | collective-permute-done | bytes 344096 | tf_op jit(solution)/shard_map/ppermute | solution.py:367
  40.7 1.4 %window_inner.1 = (f32[10,32,384]{2,1,0:T(8,128)S(1)}, f32[8,8,384]{2,1,0:T(8,128)S(1)}, f32[8,8,384]{2,1,0:T(8,128)S(1)}, f32[24,8,384]{2,1,0:T(8,128)S(1)}, f3...) custom-call(f32[10,40,384]{2,1,0:T(8,128)S(1)} %get-tuple-element.49.refs_0_, ...), custom_call_target="tpu_custom_call" | custom-call | tf_op jit(solution)/shard_map/window_inner/pallas_call | solution.py:428
  42.8 4.7 %collective-permute-start.9 = (f32[8,8,384]{2,1,0:T(8,128)S(1)}, f32[8,8,384]{2,1,0:T(8,128)S(1)}, u32[]{:S(2)}, u32[]{:S(2)}) collective-permute-start(f32[8,8,384]{2,1,0:T(8,128)S(1)} %get-tuple-element.60), channel_id=1, source_target_pairs={{0,1},{1,0},{2,3},{3,2},{4,5},{5,4},{6,7},{7,6},{8,9},{9,8},{10,11... | collective-permute-start | bytes 294920 | tf_op jit(solution)/shard_map/ppermute | solution.py:368
  47.5 4.2 %collective-permute-start.10 = (f32[24,8,384]{2,1,0:T(8,128)S(1)}, f32[24,8,384]{2,1,0:T(8,128)S(1)}, u32[]{:S(2)}, u32[]{:S(2)}) collective-permute-start(f32[24,8,384]{2,1,0:T(8,128)S(1)} %get-tuple-element.62), channel_id=1, source_target_pairs={{16,32},{32,16},{48,64},{64,48},{80,96},{96,80},{112,128},{128,112... | collective-permute-start | bytes 884744 | tf_op jit(solution)/shard_map/ppermute | solution.py:367
  51.7 1.9 %collective-permute-start.11 = (f32[24,8,384]{2,1,0:T(8,128)S(1)}, f32[24,8,384]{2,1,0:T(8,128)S(1)}, u32[]{:S(2)}, u32[]{:S(2)}) collective-permute-start(f32[24,8,384]{2,1,0:T(8,128)S(1)} %get-tuple-element.63), channel_id=1, source_target_pairs={{0,16},{16,0},{32,48},{48,32},{64,80},{80,64},{96,112},{112,96},{1... | collective-permute-start | bytes 884744 | tf_op jit(solution)/shard_map/ppermute | solution.py:368
  53.7 5.1 %collective-permute-start.12 = (f32[12,8,384]{2,1,0:T(8,128)S(1)}, f32[12,8,384]{2,1,0:T(8,128)S(1)}, u32[]{:S(2)}, u32[]{:S(2)}) collective-permute-start(f32[12,8,384]{2,1,0:T(8,128)S(1)} %get-tuple-element.64), channel_id=1, source_target_pairs={{16,32},{32,16},{48,64},{64,48},{80,96},{96,80},{112,128},{128,112... | collective-permute-start | bytes 442376 | tf_op jit(solution)/shard_map/ppermute | solution.py:367
  58.8 1.9 %collective-permute-start.13 = (f32[12,8,384]{2,1,0:T(8,128)S(1)}, f32[12,8,384]{2,1,0:T(8,128)S(1)}, u32[]{:S(2)}, u32[]{:S(2)}) collective-permute-start(f32[12,8,384]{2,1,0:T(8,128)S(1)} %get-tuple-element.65), channel_id=1, source_target_pairs={{0,16},{16,0},{32,48},{48,32},{64,80},{80,64},{96,112},{112,96},{1... | collective-permute-start | bytes 442376 | tf_op jit(solution)/shard_map/ppermute | solution.py:368
  62.1 1.6 %window_wide.1 = (f32[10,40,384]{2,1,0:T(8,128)S(1)}, f32[28,8,384]{2,1,0:T(8,128)S(1)}, f32[28,8,384]{2,1,0:T(8,128)S(1)}, f32[4,4,32,384]{3,2,1,0:T(8,128)S(1)}) custom-call(f32[10,48,384]{2,1,0:T(8,128)S(1)} %get-tuple-element.61.refs_0_, f32[24,8,384]{2,1,0:T(8,128)S(1)} %collective-permute-done.10.refs_1_, ...), custom_call_target="tpu_custom_call" | custom-call | tf_op jit(solution)/shard_map/window_wide/pallas_call | solution.py:435
  63.7 4.6 %collective-permute-start.14 = (f32[28,8,384]{2,1,0:T(8,128)S(1)}, f32[28,8,384]{2,1,0:T(8,128)S(1)}, u32[]{:S(2)}, u32[]{:S(2)}) collective-permute-start(f32[28,8,384]{2,1,0:T(8,128)S(1)} %get-tuple-element.69), channel_id=1, source_target_pairs={{16,32},{32,16},{48,64},{64,48},{80,96},{96,80},{112,128},{128,112... | collective-permute-start | bytes 1032200 | tf_op jit(solution)/shard_map/ppermute | solution.py:367
  68.3 1.9 %collective-permute-start.15 = (f32[28,8,384]{2,1,0:T(8,128)S(1)}, f32[28,8,384]{2,1,0:T(8,128)S(1)}, u32[]{:S(2)}, u32[]{:S(2)}) collective-permute-start(f32[28,8,384]{2,1,0:T(8,128)S(1)} %get-tuple-element.70), channel_id=1, source_target_pairs={{0,16},{16,0},{32,48},{48,32},{64,80},{80,64},{96,112},{112,96},{1... | collective-permute-start | bytes 1032200 | tf_op jit(solution)/shard_map/ppermute | solution.py:368
  70.6 2.6 %collective-permute-done.14.refs_1_ = f32[28,8,384]{2,1,0:T(8,128)S(1)} collective-permute-done((f32[28,8,384]{2,1,0:T(8,128)S(1)}, f32[28,8,384]{2,1,0:T(8,128)S(1)}, u32[]{:S(2)}, u32[]{:S(2)}) %collective-permute-start.14) | collective-permute-done | bytes 344096 | tf_op jit(solution)/shard_map/ppermute | solution.py:367
  73.2 2.3 %window_last.1 = (f32[4,32,384]{2,1,0:T(8,128)}, f32[4,32,384]{2,1,0:T(8,128)}, f32[16,128]{1,0:T(8,128)S(1)}) custom-call(f32[10,40,384]{2,1,0:T(8,128)S(1)} %get-tuple-element.68.refs_0_, f32[28,8,384]{2,1,0:T(8,128)S(1)} %collective-permute-done.14.refs_1_, f32[28,8,384]{2,1,0:T(8,128)S(1)} %collective-permute-done.15.refs_2_, ...), custom_call_target="tpu_custom_call" | custom-call | tf_op jit(solution)/shard_map/window_last/pallas_call | solution.py:436
  75.9 20.0 %all_to_all.10.part_ref = f32[32,16,128]{2,1,0:T(8,128)S(1)} all-to-all(f32[32,16,128]{2,1,0:T(8,128)S(1)} %project.1), channel_id=1, replica_groups={{0,1,2,3,4,5,6,7,8,9,10,11,12,13,14,15,16,17,18,19,20,21,22,23,24,25,26..., dimensions={0} | all-to-all | bytes 524288 | tf_op jit(solution)/shard_map/all_to_all | solution.py:442
  96.0 28.3 %all_to_all.11.part_ref = f32[24,16,128]{2,1,0:T(8,128)S(1)} all-to-all(f32[24,16,128]{2,1,0:T(8,128)S(1)} %row_total.1), channel_id=1, replica_groups={{0,32,64,96,128,160,192,224,256,288,320,352,384,416,448,480,512,544,576..., dimensions={0} | all-to-all | bytes 393216 | tf_op jit(solution)/shard_map/all_to_all | solution.py:445
  124.3 5.4 %collective-permute-start.16 = (f32[1,16,128]{2,1,0:T(8,128)S(1)}, f32[1,16,128]{2,1,0:T(8,128)S(1)}, u32[]{:S(2)}, u32[]{:S(2)}) collective-permute-start(f32[1,16,128]{2,1,0:T(8,128)S(1)} %total.1.refs_0_), channel_id=1, source_target_pairs={{0,16},{16,0},{32,48},{48,32},{64,80},{80,64},{96,112},{112,96},{1... | collective-permute-start | bytes 24584 | tf_op jit(solution)/shard_map/ppermute | solution.py:447
  (35 shorter events, 7.8 us)
Async XLA Ops:
  1.7 18.8 %collective-permute-start = (f32[12,8,384]{2,1,0:T(8,128)S(1)}, f32[12,8,384]{2,1,0:T(8,128)S(1)}, u32[]{:S(2)}, u32[]{:S(2)}) collective-permute-start(f32[12,8,384]{2,1,0:T(8,128)S(1)} %get-tuple-element.41), channel_id=1, source_target_pairs={{1,2},{2,1},{3,4},{4,3},{5,6},{6,5},{7,8},{8,7},{9,10},{10,9},{11,... | collective-permute-start | bytes 442376 | tf_op jit(solution)/shard_map/ppermute | solution.py:367
  2.3 18.1 %collective-permute-start.1 = (f32[12,8,384]{2,1,0:T(8,128)S(1)}, f32[12,8,384]{2,1,0:T(8,128)S(1)}, u32[]{:S(2)}, u32[]{:S(2)}) collective-permute-start(f32[12,8,384]{2,1,0:T(8,128)S(1)} %get-tuple-element.42), channel_id=1, source_target_pairs={{0,1},{1,0},{2,3},{3,2},{4,5},{5,4},{6,7},{7,6},{8,9},{9,8},{10,11... | collective-permute-start | bytes 442376 | tf_op jit(solution)/shard_map/ppermute | solution.py:368
  13.4 15.7 %collective-permute-start.2 = (f32[44,8,384]{2,1,0:T(8,128)S(1)}, f32[44,8,384]{2,1,0:T(8,128)S(1)}, u32[]{:S(2)}, u32[]{:S(2)}) collective-permute-start(f32[44,8,384]{2,1,0:T(8,128)S(1)} %get-tuple-element.44), channel_id=1, source_target_pairs={{16,32},{32,16},{48,64},{64,48},{80,96},{96,80},{112,128},{128,112... | collective-permute-start | bytes 1622024 | tf_op jit(solution)/shard_map/ppermute | solution.py:367
  18.5 10.5 %collective-permute-start.3 = (f32[44,8,384]{2,1,0:T(8,128)S(1)}, f32[44,8,384]{2,1,0:T(8,128)S(1)}, u32[]{:S(2)}, u32[]{:S(2)}) collective-permute-start(f32[44,8,384]{2,1,0:T(8,128)S(1)} %get-tuple-element.45), channel_id=1, source_target_pairs={{0,16},{16,0},{32,48},{48,32},{64,80},{80,64},{96,112},{112,96},{1... | collective-permute-start | bytes 1622024 | tf_op jit(solution)/shard_map/ppermute | solution.py:368
  20.5 6.5 %copy-start = (f32[2,4096]{1,0:T(2,128)S(1)}, f32[2,4096]{1,0:T(2,128)}, u32[]{:S(2)}) copy-start(f32[2,4096]{1,0:T(2,128)} %refs_1_.1) | copy-start | bytes 98308
  20.6 6.3 %copy-start.2 = (s32[64]{0:T(128)S(1)}, s32[64]{0:T(128)}, u32[]{:S(2)}) copy-start(s32[64]{0:T(128)} %param.9) | copy-start | bytes 772
  20.6 8.4 %collective-permute-start.4 = (f32[19,8,384]{2,1,0:T(8,128)S(1)}, f32[19,8,384]{2,1,0:T(8,128)S(1)}, u32[]{:S(2)}, u32[]{:S(2)}) collective-permute-start(f32[19,8,384]{2,1,0:T(8,128)S(1)} %get-tuple-element.46), channel_id=1, source_target_pairs={{16,32},{32,16},{48,64},{64,48},{80,96},{96,80},{112,128},{128,112... | collective-permute-start | bytes 700424 | tf_op jit(solution)/shard_map/ppermute | solution.py:367
  25.0 4.0 %collective-permute-start.5 = (f32[19,8,384]{2,1,0:T(8,128)S(1)}, f32[19,8,384]{2,1,0:T(8,128)S(1)}, u32[]{:S(2)}, u32[]{:S(2)}) collective-permute-start(f32[19,8,384]{2,1,0:T(8,128)S(1)} %get-tuple-element.47), channel_id=1, source_target_pairs={{0,16},{16,0},{32,48},{48,32},{64,80},{80,64},{96,112},{112,96},{1... | collective-permute-start | bytes 700424 | tf_op jit(solution)/shard_map/ppermute | solution.py:368
  31.4 9.3 %collective-permute-start.6 = (f32[28,8,384]{2,1,0:T(8,128)S(1)}, f32[28,8,384]{2,1,0:T(8,128)S(1)}, u32[]{:S(2)}, u32[]{:S(2)}) collective-permute-start(f32[28,8,384]{2,1,0:T(8,128)S(1)} %get-tuple-element.50), channel_id=1, source_target_pairs={{16,32},{32,16},{48,64},{64,48},{80,96},{96,80},{112,128},{128,112... | collective-permute-start | bytes 1032200 | tf_op jit(solution)/shard_map/ppermute | solution.py:367
  35.8 4.9 %collective-permute-start.7 = (f32[28,8,384]{2,1,0:T(8,128)S(1)}, f32[28,8,384]{2,1,0:T(8,128)S(1)}, u32[]{:S(2)}, u32[]{:S(2)}) collective-permute-start(f32[28,8,384]{2,1,0:T(8,128)S(1)} %get-tuple-element.51), channel_id=1, source_target_pairs={{0,16},{16,0},{32,48},{48,32},{64,80},{80,64},{96,112},{112,96},{1... | collective-permute-start | bytes 1032200 | tf_op jit(solution)/shard_map/ppermute | solution.py:368
  42.1 11.5 %collective-permute-start.8 = (f32[8,8,384]{2,1,0:T(8,128)S(1)}, f32[8,8,384]{2,1,0:T(8,128)S(1)}, u32[]{:S(2)}, u32[]{:S(2)}) collective-permute-start(f32[8,8,384]{2,1,0:T(8,128)S(1)} %get-tuple-element.59), channel_id=1, source_target_pairs={{1,2},{2,1},{3,4},{4,3},{5,6},{6,5},{7,8},{8,7},{9,10},{10,9},{11,... | collective-permute-start | bytes 294920 | tf_op jit(solution)/shard_map/ppermute | solution.py:367
  42.8 10.9 %collective-permute-start.9 = (f32[8,8,384]{2,1,0:T(8,128)S(1)}, f32[8,8,384]{2,1,0:T(8,128)S(1)}, u32[]{:S(2)}, u32[]{:S(2)}) collective-permute-start(f32[8,8,384]{2,1,0:T(8,128)S(1)} %get-tuple-element.60), channel_id=1, source_target_pairs={{0,1},{1,0},{2,3},{3,2},{4,5},{5,4},{6,7},{7,6},{8,9},{9,8},{10,11... | collective-permute-start | bytes 294920 | tf_op jit(solution)/shard_map/ppermute | solution.py:368
  47.5 14.6 %collective-permute-start.10 = (f32[24,8,384]{2,1,0:T(8,128)S(1)}, f32[24,8,384]{2,1,0:T(8,128)S(1)}, u32[]{:S(2)}, u32[]{:S(2)}) collective-permute-start(f32[24,8,384]{2,1,0:T(8,128)S(1)} %get-tuple-element.62), channel_id=1, source_target_pairs={{16,32},{32,16},{48,64},{64,48},{80,96},{96,80},{112,128},{128,112... | collective-permute-start | bytes 884744 | tf_op jit(solution)/shard_map/ppermute | solution.py:367
  51.7 10.4 %collective-permute-start.11 = (f32[24,8,384]{2,1,0:T(8,128)S(1)}, f32[24,8,384]{2,1,0:T(8,128)S(1)}, u32[]{:S(2)}, u32[]{:S(2)}) collective-permute-start(f32[24,8,384]{2,1,0:T(8,128)S(1)} %get-tuple-element.63), channel_id=1, source_target_pairs={{0,16},{16,0},{32,48},{48,32},{64,80},{80,64},{96,112},{112,96},{1... | collective-permute-start | bytes 884744 | tf_op jit(solution)/shard_map/ppermute | solution.py:368
  53.7 7.9 %collective-permute-start.12 = (f32[12,8,384]{2,1,0:T(8,128)S(1)}, f32[12,8,384]{2,1,0:T(8,128)S(1)}, u32[]{:S(2)}, u32[]{:S(2)}) collective-permute-start(f32[12,8,384]{2,1,0:T(8,128)S(1)} %get-tuple-element.64), channel_id=1, source_target_pairs={{16,32},{32,16},{48,64},{64,48},{80,96},{96,80},{112,128},{128,112... | collective-permute-start | bytes 442376 | tf_op jit(solution)/shard_map/ppermute | solution.py:367
  58.8 3.3 %collective-permute-start.13 = (f32[12,8,384]{2,1,0:T(8,128)S(1)}, f32[12,8,384]{2,1,0:T(8,128)S(1)}, u32[]{:S(2)}, u32[]{:S(2)}) collective-permute-start(f32[12,8,384]{2,1,0:T(8,128)S(1)} %get-tuple-element.65), channel_id=1, source_target_pairs={{0,16},{16,0},{32,48},{48,32},{64,80},{80,64},{96,112},{112,96},{1... | collective-permute-start | bytes 442376 | tf_op jit(solution)/shard_map/ppermute | solution.py:368
  63.7 9.5 %collective-permute-start.14 = (f32[28,8,384]{2,1,0:T(8,128)S(1)}, f32[28,8,384]{2,1,0:T(8,128)S(1)}, u32[]{:S(2)}, u32[]{:S(2)}) collective-permute-start(f32[28,8,384]{2,1,0:T(8,128)S(1)} %get-tuple-element.69), channel_id=1, source_target_pairs={{16,32},{32,16},{48,64},{64,48},{80,96},{96,80},{112,128},{128,112... | collective-permute-start | bytes 1032200 | tf_op jit(solution)/shard_map/ppermute | solution.py:367
  68.3 4.9 %collective-permute-start.15 = (f32[28,8,384]{2,1,0:T(8,128)S(1)}, f32[28,8,384]{2,1,0:T(8,128)S(1)}, u32[]{:S(2)}, u32[]{:S(2)}) collective-permute-start(f32[28,8,384]{2,1,0:T(8,128)S(1)} %get-tuple-element.70), channel_id=1, source_target_pairs={{0,16},{16,0},{32,48},{48,32},{64,80},{80,64},{96,112},{112,96},{1... | collective-permute-start | bytes 1032200 | tf_op jit(solution)/shard_map/ppermute | solution.py:368
  124.3 6.2 %copy-start.1 = (f32[2,8,256]{2,1,0:T(8,128)S(1)}, f32[2,8,256]{2,1,0:T(8,128)}, u32[]{:S(2)}) copy-start(f32[2,8,256]{2,1,0:T(8,128)} %refs_2_.1) | copy-start | bytes 49156
  124.3 6.2 %collective-permute-start.16 = (f32[1,16,128]{2,1,0:T(8,128)S(1)}, f32[1,16,128]{2,1,0:T(8,128)S(1)}, u32[]{:S(2)}, u32[]{:S(2)}) collective-permute-start(f32[1,16,128]{2,1,0:T(8,128)S(1)} %total.1.refs_0_), channel_id=1, source_target_pairs={{0,16},{16,0},{32,48},{48,32},{64,80},{80,64},{96,112},{112,96},{1... | collective-permute-start | bytes 24584 | tf_op jit(solution)/shard_map/ppermute | solution.py:447
